TPU v7x, 32 devices: a whole 2x2x4 slice. The times are simulated.
32 devices in a mesh: wide: 8 (over z, y), lev: 4 (over x, core).
Axes of the slice: x: 2, y: 2, z: 4, core: 2. Of those that a mesh axis runs over, the one named last changes fastest.
Arguments:
- state_field: float32 [12, 1472, 1472], P('lev', 'wide'), may hold values from -8 to 8
- to_modes: float32 [12, 12], replicated, may hold values from -4 to 4
- from_modes: float32 [12, 12], replicated, may hold values from -4 to 4, as said below
- mode_depth: float32 [12], replicated, may hold values from 0.1 to 2000
Outputs:
- updated_field: float32 [12, 1472, 1472], P('lev', 'wide')
Inputs may be any that keep to these rules, and one draw needn't show every extreme that they name: `from_modes`: the inverse of to_modes.
All inputs are finite; a program needn't handle non-finite values.
Results may differ from a plain program's by a relative error of at most 0.000094.
Values sent between devices are 32-bit elements; how exact they have to be, the bound alone decides.
No kernel may reach another device: no remote copies, remote signals or barrier semaphores. Data moves between devices by JAX's collectives and lax.ppermute only.
A program may use at most 64 MiB of HBM per device.

v0:
```python
import math

import jax
import jax.numpy as jnp
from jax import lax
from jax.sharding import PartitionSpec as P

I = 1472
E = 64
KT = 512


highest = lax.Precision.HIGHEST


def spread(block, axis, owner):
    block = jnp.where(lax.axis_index(axis) == owner, block, jnp.zeros_like(block))
    return lax.psum(block, axis)


def blend_weights(fraction):
    square = fraction * fraction
    cubed = square * fraction
    return (
        2.0 * cubed - 3.0 * square + 1.0,
        cubed - 2.0 * square + fraction,
        -2.0 * cubed + 3.0 * square,
        cubed - square,
    )


def hermite_mix(start_val, start_slope, end_val, end_slope, weights):
    return (
        weights[0] * end_val
        + weights[1] * end_slope
        + weights[2] * start_val
        + weights[3] * start_slope
    )


def extend_cols(sub_block, extra):
    fraction = (jnp.arange(extra, dtype=jnp.float32) + 1.0) / (extra + 1.0)
    weights = blend_weights(fraction)
    end_val = sub_block[..., -1:]
    end_slope = sub_block[..., -1:] - sub_block[..., -2:-1]
    start_val = sub_block[..., :1]
    start_slope = sub_block[..., 1:2] - sub_block[..., :1]
    added = hermite_mix(start_val, start_slope, end_val, end_slope, weights)
    return jnp.concatenate([sub_block, added], axis=-1)


def laplace(waves, length):
    sines = jnp.sin(math.pi / length * waves.astype(jnp.float32))
    return 4.0 * sines * sines


def cas_table(positions, waves, length):
    product = positions[:, None] * waves[None, :] % length
    phase_angle = 2.0 * math.pi / length * product.astype(jnp.float32)
    return jnp.cos(phase_angle) + jnp.sin(phase_angle)


def wave_numbers(amount, length, bound):
    indices = jnp.arange(amount, dtype=jnp.int32)
    waves = jnp.where(indices < bound, indices, length - 2 * bound + 1 + indices)
    live_mask = indices < 2 * bound - 1
    waves = jnp.where(live_mask, waves, 0)
    magnitude = jnp.minimum(waves, length - waves)
    return (waves, live_mask.astype(jnp.float32), magnitude)


def shards(state_field, to_modes, from_modes, mode_depth):
    wide_count = lax.axis_size("wide")
    wide_index = lax.axis_index("wide")
    lev_index = lax.axis_index("lev")
    levels, row_count, col_count = state_field.shape
    length = I + E
    ext_count = E // wide_count
    row_total = row_count + ext_count
    head_strip = spread(state_field[:, :2], "wide", 0)
    tail_strip = spread(state_field[:, row_count - 2 :], "wide", wide_count - 1)
    ext_slot = (wide_count - wide_index) % wide_count
    row_ids = ext_slot * ext_count + jnp.arange(ext_count, dtype=jnp.int32)
    fraction = (row_ids.astype(jnp.float32) + 1.0) / (E + 1.0)
    weights = tuple((weight[:, None] for weight in blend_weights(fraction)))
    end_val = tail_strip[:, 1:2]
    end_slope = tail_strip[:, 1:2] - tail_strip[:, 0:1]
    start_val = head_strip[:, 0:1]
    start_slope = head_strip[:, 1:2] - head_strip[:, 0:1]
    ext_block = hermite_mix(start_val, start_slope, end_val, end_slope, weights)
    stacked = jnp.concatenate([state_field, ext_block], axis=1)
    widened = extend_cols(stacked, E)
    spec_count = 2 * KT
    waves, live_mask, magnitude = wave_numbers(spec_count, length, KT)
    lap_all = laplace(waves, length)
    positions = jnp.arange(length, dtype=jnp.int32)
    forward_x = cas_table(positions, waves, length) * live_mask[None, :]
    row_owner = positions // row_total
    local_row = positions % row_total
    ext_owner = (wide_count - row_owner) % wide_count
    row_pos = jnp.where(
        local_row < row_count,
        row_owner * row_count + local_row,
        I + ext_owner * ext_count + local_row - row_count,
    )
    forward_y = cas_table(row_pos, waves, length) * live_mask[None, :]
    inverse_y = forward_y.T / length
    inverse_x = forward_x[:I].T / length
    col_span = spec_count // wide_count
    col_start = wide_index * col_span
    spec_x = jnp.einsum("irn,nc->irc", widened, forward_x, precision=highest)
    spectrum = jnp.einsum(
        "irc,rk->ick",
        lax.all_to_all(spec_x, "wide", split_axis=2, concat_axis=1, tiled=True),
        forward_y,
        precision=highest,
    )
    lev_start = lev_index * levels
    sub_block = lax.dynamic_slice(to_modes, (0, lev_start), (lax.axis_size("lev") * levels, levels))
    mode_values = lax.psum_scatter(
        jnp.einsum("ml,lck->mck", sub_block, spectrum, precision=highest),
        "lev",
        scatter_dimension=0,
        tiled=True,
    )
    lap_cols = lax.dynamic_slice_in_dim(lap_all, col_start, col_span)
    mag_cols = lax.dynamic_slice_in_dim(magnitude, col_start, col_span)
    live_cols = lax.dynamic_slice_in_dim(live_mask, col_start, col_span)
    inside = (
        mag_cols[:, None] * mag_cols[:, None] + magnitude[None, :] * magnitude[None, :] < KT * KT
    )
    keep_mask = live_cols[:, None] * live_mask[None, :] * inside.astype(jnp.float32)
    keep_mask, lap_sum = (keep_mask, lap_cols[:, None] + lap_all[None, :])
    mode_rates = lax.dynamic_slice_in_dim(mode_depth, lev_start, levels)
    solved = mode_values * keep_mask / (1.0 + mode_rates[:, None, None] * lap_sum)
    shard_piece = lax.all_gather(solved, "lev", axis=0, tiled=True)
    sub_block = lax.dynamic_slice(from_modes, (lev_start, 0), (levels, shard_piece.shape[0]))
    mixed_levels = jnp.einsum("lm,mck->lck", sub_block, shard_piece, precision=highest)
    rows_back = jnp.einsum("ick,kr->icr", mixed_levels, inverse_y, precision=highest)
    return jnp.einsum(
        "icr,cn->irn",
        lax.all_to_all(rows_back, "wide", split_axis=2, concat_axis=1, tiled=True)[
            :, :, :row_count
        ],
        inverse_x,
        precision=highest,
    )


def solution(mesh):
    placed = (P("lev", "wide", None), P(), P(), P())
    return jax.shard_map(
        shards, mesh=mesh, in_specs=placed, out_specs=P("lev", "wide", None), check_vma=False
    )
```

profile of v0, /device:TPU:0, one launch (start us, length us, event | category | flops | bytes accessed | tf_op | source)
XLA Modules:
  0.0 513.1 jit_solution(13678874333688489325)
XLA Ops:
  6.5 0.0 copy-start
  6.5 0.0 all-reduce.3.cloned.1.call-start
  6.5 1.8 slice_select_fusion.1
  8.3 0.0 all-reduce.3.cloned.1.call-update
  8.5 74.6 %all-reduce.3.cloned.1.call-done = (f32[3,2,1472]{2,1,0:T(2,128)}, f32[3,2,1472]{2,1,0:T(2,128)}) async-done(((f32[3,2,1472]{2,1,0:T(2,128)}, f32[3,2,1472]{2,1,0:T(2,128)}), (f32[3,2,1472]{2,1,0:T(2,128)}, f32[3,2,1472]{2,1,0:T(2,128)})) %all-reduce.3.cloned.1.call-update) | async-done | bytes 70672 | tf_op jit(solution)/shard_map/psum | solution.py:18
  83.1 0.9 fusion.107
  84.1 0.1 multiply_add_fusion.1
  84.2 2.0 fusion.66
  86.2 0.4 multiply_add_fusion
  86.6 0.0 copy-done.4
  86.6 0.4 fusion.124
  87.0 38.5 %fusion.12 = f32[3,192,1024]{2,1,0:T(8,128)S(1)} fusion(f32[1024]{0:T(1024)S(1)} %fusion.85, s32[1024]{0:T(1024)S(1)} %fusion.86, f32[3,192,1536]{2,1,0:T(8,128)S(1)} %fusion.124), kind=kOutput, calls=%fused_computation.15 | convolution fusion | flops 10888937472 | bytes 5906432 | tf_op jit(solution)/shard_map/irn,nc->irc/dot_general | solution.py:111
  125.5 3.2 copy.32
  128.7 4.8 all-to-all-start
  133.5 0.0 reduce-scatter.2.cloned.1.call-start
  133.5 91.4 %all-to-all-done = f32[3,192,1024]{1,0,2:T(4,128)} async-done(((f32[3,192,1024]{1,0,2:T(4,128)}), f32[3,192,1024]{1,0,2:T(4,128)}, u32[]{:S(2)}, u32[]{:S(2)}) %all-to-all-start) | async-done | bytes 2359328 | tf_op jit(solution)/shard_map/all_to_all | solution.py:114
  224.9 3.4 copy.45
  228.3 41.6 %fusion.10 = f32[3,128,1024]{2,1,0:T(8,128)S(1)} fusion(f32[3,1536,128]{2,1,0:T(8,128)S(1)} %bitcast.57, s32[1536]{0:T(1024)S(1)} %fusion.78, f32[1024]{0:T(1024)S(1)} %fusion.85, s32[1024]{0:T(1024)S(1)} %fusion.86), kind=kOutput, calls=%fused_computation.13 | convolution fusion | flops 7265058816 | bytes 3946496 | tf_op jit(solution)/shard_map/irc,rk->ick/dot_general | solution.py:112
  270.0 0.0 copy-done
  270.0 7.3 %fusion.59 = f32[12,128,1024]{2,0,1:T(8,128)S(1)} fusion(f32[3,128,1024]{2,1,0:T(8,128)S(1)} %fusion.10, f32[12,12]{1,0:T(8,128)S(1)} %copy-done, s32[]{:T(128)S(6)} %select_n.144), kind=kOutput, calls=%fused_computation.63 | convolution fusion | flops 56623104 | bytes 7864900 | tf_op jit(solution)/shard_map/ml,lck->mck/dot_general | solution.py:121
  277.3 6.3 %copy.37 = f32[12,128,1024]{2,1,0:T(8,128)} copy(f32[12,128,1024]{2,0,1:T(8,128)S(1)} %fusion.59) | data formatting | bytes 12582912 | tf_op jit(solution)/shard_map/ml,lck->mck/dot_general | solution.py:121
  283.6 0.0 reduce-scatter.2.cloned.1.call-update
  283.6 0.0 all-gather.2.cloned.1.call-start
  283.7 0.1 dynamic_slice.21
  283.8 0.1 dynamic_slice.23
  283.9 0.4 copy-done.5
  284.3 0.1 dynamic_slice.22
  284.3 0.1 dynamic-slice_multiply_fusion
  284.4 0.1 broadcast_add_fusion
  284.5 0.2 multiply_select_fusion
  284.7 56.9 %reduce-scatter.2.cloned.1.call-done = f32[3,128,1024]{2,1,0:T(8,128)} async-done(((f32[12,128,1024]{2,1,0:T(8,128)}), f32[3,128,1024]{2,1,0:T(8,128)}) %reduce-scatter.2.cloned.1.call-update) | async-done | bytes 1572880 | tf_op jit(solution)/shard_map/reduce_scatter | solution.py:120
  341.7 2.9 add_divide_fusion
  344.6 0.0 all-gather.2.cloned.1.call-update
  344.7 27.9 %fusion.122 = f32[1024,1536,1]{1,0,2:T(8,128)} fusion(f32[1024]{0:T(1024)S(1)} %fusion.85, s32[1024]{0:T(1024)S(1)} %fusion.86, s32[1536]{0:T(1024)S(1)} %fusion.78), kind=kLoop, calls=%fused_computation.12.clone.1 | loop fusion | flops 18874368 | bytes 6305792 | tf_op jit(solution)/shard_map/ick,kr->icr/dot_general | solution.py:139
  372.5 18.7 %all-gather.2.cloned.1.call-done = f32[12,128,1024]{2,1,0:T(8,128)} async-done(((f32[3,128,1024]{2,1,0:T(8,128)}), f32[12,128,1024]{2,1,0:T(8,128)}) %all-gather.2.cloned.1.call-update) | async-done | bytes 6291472 | tf_op jit(solution)/shard_map/all_gather | solution.py:136
  391.2 11.3 %fusion = f32[3,128,1024]{2,0,1:T(4,128)S(1)} fusion(f32[12,128,1024]{2,1,0:T(8,128)} %all-gather.2.cloned.1.call-done, f32[12,12]{1,0:T(8,128)} %param.6, s32[]{:T(128)S(6)} %select_n.144), kind=kOutput, calls=%fused_computation.3 | convolution fusion | flops 56623104 | bytes 7866372 | tf_op jit(solution)/shard_map/lm,mck->lck/dot_general | solution.py:138
  402.5 0.0 copy-done.2
  402.5 8.6 %fusion.8 = f32[3,128,1536]{2,1,0:T(8,128)S(1)} fusion(f32[3,128,1024]{2,0,1:T(4,128)S(1)} %fusion, f32[1024,1536,1]{1,0,2:T(8,128)S(1)} %copy-done.2), kind=kOutput, calls=%fused_computation.11 | convolution fusion | flops 7247757312 | bytes 10223616 | tf_op jit(solution)/shard_map/ick,kr->icr/dot_general | solution.py:139
  411.1 2.7 copy.40
  413.9 5.8 %all-to-all-start.1 = ((f32[3,128,1536]{1,0,2:T(4,128)}), f32[3,128,1536]{1,0,2:T(4,128)S(1)}, u32[]{:S(2)}, u32[]{:S(2)}) async-start(f32[3,128,1536]{1,0,2:T(4,128)} %copy.40), calls=%async_computation.2 | async-start | bytes 6291456 | tf_op jit(solution)/shard_map/all_to_all | solution.py:142
  419.6 27.2 %add_multiply_fusion = f32[1536,1024]{1,0:T(8,128)} fusion(f32[1024]{0:T(1024)S(1)} %fusion.85, s32[1024]{0:T(1024)S(1)} %fusion.86), kind=kLoop, calls=%fused_computation.32 | loop fusion | flops 17301504 | bytes 6299648 | tf_op jit(solution)/shard_map/mul | solution.py:97
  446.8 43.9 %all-to-all-done.1 = f32[3,128,1536]{1,0,2:T(4,128)S(1)} async-done(((f32[3,128,1536]{1,0,2:T(4,128)}), f32[3,128,1536]{1,0,2:T(4,128)S(1)}, u32[]{:S(2)}, u32[]{:S(2)}) %all-to-all-start.1) | async-done | bytes 2359328 | tf_op jit(solution)/shard_map/all_to_all | solution.py:142
  490.7 0.2 copy.41
  490.9 0.0 copy-start.1
  490.9 0.3 copy.64
  491.2 2.3 copy-done.3
  493.5 12.7 %fusion.37 = f32[3,184,1472]{2,1,0:T(8,128)} fusion(f32[1536,1024]{1,0:T(8,128)S(1)} %copy-done.3, f32[3,1024,192]{1,2,0:T(8,128)S(1)} %bitcast.56), kind=kOutput, calls=%fused_computation.41 | convolution fusion | flops 9986048000 | bytes 11540480 | tf_op jit(solution)/shard_map/icr,cn->irn/dot_general | solution.py:140
  506.2 0.0 copy-done.1
  (18 shorter events, 0.2 us)
Async XLA Ops:
  6.5 263.4 %copy-start = (f32[12,12]{1,0:T(8,128)S(1)}, f32[12,12]{1,0:T(8,128)}, u32[]{:S(2)}) copy-start(f32[12,12]{1,0:T(8,128)} %param.5) | copy-start | bytes 1732
  6.5 80.1 %copy-start.4 = (f32[3,184,1472]{2,1,0:T(8,128)S(1)}, f32[3,184,1472]{2,1,0:T(8,128)}, u32[]{:S(2)}) copy-start(f32[3,184,1472]{2,1,0:T(8,128)} %param.4) | copy-start | bytes 9750532
  6.5 76.5 %all-reduce.3.cloned.1.call-start = ((), (), s32[]{:S(2)}) async-start(), calls=%async_computation.5 | async-start | bytes 147456 | tf_op jit(solution)/shard_map/psum | solution.py:18
  128.7 96.2 %all-to-all-start = ((f32[3,192,1024]{1,0,2:T(4,128)}), f32[3,192,1024]{1,0,2:T(4,128)}, u32[]{:S(2)}, u32[]{:S(2)}) async-start(f32[3,192,1024]{1,0,2:T(4,128)} %copy.32), calls=%async_computation | async-start | bytes 8388608 | tf_op jit(solution)/shard_map/all_to_all | solution.py:114
  133.5 208.2 %reduce-scatter.2.cloned.1.call-start = ((), (), s32[]{:S(2)}) async-start(), calls=%async_computation.3 | async-start | bytes 7864320 | tf_op jit(solution)/shard_map/reduce_scatter | solution.py:120
  283.6 0.7 copy-start.5
  283.6 107.5 %all-gather.2.cloned.1.call-start = ((), (), s32[]{:S(2)}) async-start(), calls=%async_computation.4 | async-start | bytes 7864320 | tf_op jit(solution)/shard_map/all_gather | solution.py:136
  391.2 11.4 %copy-start.2 = (f32[1024,1536,1]{1,0,2:T(8,128)S(1)}, f32[1024,1536,1]{1,0,2:T(8,128)}, u32[]{:S(2)}) copy-start(f32[1024,1536,1]{1,0,2:T(8,128)} %fusion.122) | copy-start | bytes 18874372
  413.9 76.8 %all-to-all-start.1 = ((f32[3,128,1536]{1,0,2:T(4,128)}), f32[3,128,1536]{1,0,2:T(4,128)S(1)}, u32[]{:S(2)}, u32[]{:S(2)}) async-start(f32[3,128,1536]{1,0,2:T(4,128)} %copy.40), calls=%async_computation.2 | async-start | bytes 6291456 | tf_op jit(solution)/shard_map/all_to_all | solution.py:142
  490.7 2.8 copy-start.3
  490.9 15.3 %copy-start.1 = (f32[12,12]{1,0:T(8,128)S(1)}, f32[12,12]{1,0:T(8,128)}, u32[]{:S(2)}) copy-start(f32[12,12]{1,0:T(8,128)} %param.5) | copy-start | bytes 1732
Sparse Core Ops, SparseCore 0:
  10.8 72.1 all-reduce.2
  283.8 57.8 reduce-scatter.1
  344.8 46.3 all-gather.1
where the time goes:
time: 522 us; the launch traced here: 513 us
  waiting for transfers between devices  286 us (55%)
  matrix products  120 us (23%)
  other arithmetic  64.1 us (12%)
  local copies, waits for them, and re-layouts  19 us (4%)
  between operations  13.7 us (3%)
  starting transfers between devices  10.6 us (2%)
    all_to_all x1, waiting for transfers between devices, shards(): lax.all_to_all(spec_x, 'wide', split_axis=2, concat_axis=1, tiled=True)  91.4 us
    psum x1, waiting for transfers between devices, spread(): return lax.psum(block, axis)  74.6 us
    reduce_scatter x1, waiting for transfers between devices, shards(): lax.psum_scatter(jnp.einsum('ml,lck->mck', sub_block, spectrum, precision...  56.9 us
    all_to_all x1, waiting for transfers between devices, shards(): lax.all_to_all(rows_back, 'wide', split_axis=2, concat_axis=1, tiled=True)  43.9 us
    dot_general x1, matrix products, shards(): jnp.einsum('irc,rk->ick', lax.all_to_all(spec_x, 'wide', split_axis=2, co...  41.6 us
    dot_general x1, matrix products, shards(): spec_x = jnp.einsum('irn,nc->irc', widened, forward_x, precision=highest)  38.5 us
    dot_general x1, other arithmetic, shards(): jnp.einsum('ick,kr->icr', mixed_levels, inverse_y, precision=highest)  27.9 us
    mul x1, other arithmetic, shards(): forward_x = cas_table(positions, waves, length) * live_mask[None, :]  27.2 us
  transfers between devices with their start and end apart: 5, of which 5 were waited for; matrix products, arithmetic and copies ran while one was open for 11% of the time, Pallas kernels for 0%

commit v1 on v0

v1 whole, which is shorter than its diff:
```python
import math

import jax
import jax.numpy as jnp
import numpy as np
from jax import lax
from jax.sharding import PartitionSpec as P

I = 1472
E = 64
KT = 512
STEP = 16

HIGH = lax.Precision.HIGH
HIGHEST = lax.Precision.HIGHEST
AXES = ("wide", "lev")


def blend_weights(extra):
    f = (np.arange(extra, dtype=np.float64) + 1.0) / (extra + 1.0)
    f2, f3 = f * f, f * f * f
    return 2 * f3 - 3 * f2 + 1, f3 - 2 * f2 + f, -2 * f3 + 3 * f2, f3 - f2


def edge_weights(extra):
    h00, h10, h01, h11 = blend_weights(extra)
    return np.stack([h01 - h11, h11, -h10, h00 + h10]).astype(np.float32)


def extend(block, extra):
    w = jnp.asarray(edge_weights(extra))
    added = (
        block[..., :1] * w[0] + block[..., 1:2] * w[1] + block[..., -2:-1] * w[2] + block[..., -1:] * w[3]
    )
    return jnp.concatenate([block, added], axis=-1)


def cas_seeds(waves, positions, length):
    turn = 2.0 * np.pi / length
    base = waves[::STEP].astype(np.int64)
    coarse = turn * ((base[:, None] * positions[None, :]) % length)
    fine = turn * ((np.arange(STEP)[:, None] * positions[None, :]) % length)
    parts = np.cos(coarse) + np.sin(coarse), np.cos(coarse) - np.sin(coarse), np.cos(fine), np.sin(fine)
    return [np.asarray(a, np.float32) for a in parts]


def cas_table(waves, positions, length):
    plus, minus, cosine, sine = (jnp.asarray(a) for a in cas_seeds(waves, positions, length))
    table = plus[:, None, :] * cosine[None] + minus[:, None, :] * sine[None]
    return table.reshape(len(waves), len(positions))


def plain(state, to_modes, from_modes, mode_depth):
    wide, lev = lax.axis_size("wide"), lax.axis_size("lev")
    devices = wide * lev
    levels, rows, cols = state.shape
    length = I + E
    waves = np.arange(-KT, KT)
    share = len(waves) // devices
    table = cas_table(waves, np.arange(length), length)
    spec = jnp.einsum("qn,lrn->qlr", table, extend(state, E), precision=HIGH)
    spec = spec.reshape(devices, share, levels * rows)
    spec = lax.all_to_all(spec, AXES, 0, 0, tiled=True)
    spec = spec.reshape(wide, lev, share, levels, rows).transpose(1, 3, 2, 0, 4)
    spec = extend(spec.reshape(lev * levels, share, wide * rows), E)
    spec = jnp.einsum("lqr,pr->lqp", spec, table, precision=HIGH)
    first = (lax.axis_index("wide") * lev + lax.axis_index("lev")) * share
    lap = (4.0 * np.sin(np.pi * waves / length) ** 2).astype(np.float32)
    square = (waves * waves).astype(np.int32)
    lap_q = lax.dynamic_slice_in_dim(jnp.asarray(lap), first, share)
    square_q = lax.dynamic_slice_in_dim(jnp.asarray(square), first, share)
    keep = (square_q[:, None] + square[None, :] < KT * KT).astype(jnp.float32)
    modes = jnp.einsum("ml,lqp->mqp", to_modes, spec, precision=HIGHEST)
    solved = modes * keep / (1.0 + mode_depth[:, None, None] * (lap_q[:, None] + lap[None, :]))
    mixed = jnp.einsum("lm,mqp->lqp", from_modes, solved, precision=HIGHEST)
    back = jnp.einsum("lqp,pr->lqr", mixed, table[:, :I], precision=HIGH)
    back = back.reshape(lev, levels, share, wide, rows).transpose(3, 0, 2, 1, 4)
    back = lax.all_to_all(back.reshape(devices, share, levels * rows), AXES, 0, 0, tiled=True)
    back = back.reshape(len(waves), levels, rows)
    return jnp.einsum("qlr,qn->lrn", back, table[:, :I], precision=HIGH) / (length * length)


def solution(mesh):
    placed = (P("lev", "wide", None), P(), P(), P())
    return jax.shard_map(
        plain, mesh=mesh, in_specs=placed, out_specs=P("lev", "wide", None), check_vma=False
    )
```

time: 522 us -> 216 us (0.41); the launches traced: 513 us -> 215 us
  waiting for transfers between devices: 286 us -> 59.7 us
  matrix products: 120 us -> 40.6 us
  blocking collectives: 0 us -> 64.4 us
  other arithmetic: 64.1 us -> 4.95 us
  local copies, waits for them, and re-layouts: 19 us -> 37.5 us
  between operations: 13.7 us -> 0.32 us
    dot_general x6, matrix products: 120 us -> 40.6 us  [the longest x1 12.1 us: plain(): jnp.einsum('qlr,qn->lrn', back, table[:, :I], precision=HIGH)]
    all_to_all x2 -> x1, waiting for transfers between devices: 135 us -> 59.7 us  [plain(): spec = lax.all_to_all(spec, AXES, 0, 0, tiled=True)]
    psum x1 -> x0, waiting for transfers between devices: 74.6 us -> none  [spread(): return lax.psum(block, axis)]
    all_to_all x0 -> x1, blocking collectives: none -> 64.4 us  [plain(): lax.all_to_all(back.reshape(devices, share, levels * rows), AXES, 0, 0, t...]
    reduce_scatter x1 -> x0, waiting for transfers between devices: 56.9 us -> none  [shards(): lax.psum_scatter(jnp.einsum('ml,lck->mck', sub_block, spectrum, precision...]
    dot_general x2 -> x0, other arithmetic: 28.2 us -> none  [the longest x1 27.9 us: shards(): jnp.einsum('ick,kr->icr', mixed_levels, inverse_y, precision=highest)]
    mul x5 -> x0, other arithmetic: 27.5 us -> none  [the longest x1 27.2 us: shards(): forward_x = cas_table(positions, waves, length) * live_mask[None, :]]
    reshape x0 -> x6, local copies, waits for them, and re-layouts: none -> 26.5 us  [the longest x2 8.05 us: plain(): back = back.reshape(lev, levels, share, wide, rows).transpose(3, 0, 2, 1, 4)]
  transfers between devices with their start and end apart: 5 -> 1, of which waited for: 5 -> 1; matrix products, arithmetic and copies ran while one was open for 11% -> 0% of each run, Pallas kernels for 0% -> 0%
where the time goes in v1:
time: 216 us; the launch traced here: 215 us
  blocking collectives  64.4 us (30%)
  waiting for transfers between devices  59.7 us (28%)
  matrix products  40.6 us (19%)
  local copies, waits for them, and re-layouts  37.5 us (17%)
  starting transfers between devices  7.5 us (3%)
  other arithmetic  4.95 us (2%)
    all_to_all x1, blocking collectives, plain(): lax.all_to_all(back.reshape(devices, share, levels * rows), AXES, 0, 0, t...  64.4 us
    all_to_all x1, waiting for transfers between devices, plain(): spec = lax.all_to_all(spec, AXES, 0, 0, tiled=True)  59.7 us
    dot_general x1, matrix products, plain(): jnp.einsum('qlr,qn->lrn', back, table[:, :I], precision=HIGH)  12.1 us
    dot_general x1, matrix products, plain(): spec = jnp.einsum('qn,lrn->qlr', table, extend(state, E), precision=HIGH)  9.25 us
    reshape x2, local copies, waits for them, and re-layouts, plain(): back = back.reshape(lev, levels, share, wide, rows).transpose(3, 0, 2, 1, 4)  8.05 us
    all_to_all x1, starting transfers between devices, plain(): spec = lax.all_to_all(spec, AXES, 0, 0, tiled=True)  7.5 us
    dot_general x1, matrix products, plain(): back = jnp.einsum('lqp,pr->lqr', mixed, table[:, :I], precision=HIGH)  6.55 us
    dot_general x1, matrix products, plain(): spec = jnp.einsum('lqr,pr->lqp', spec, table, precision=HIGH)  6.53 us
  transfers between devices with their start and end apart: 1, of which 1 were waited for; matrix products, arithmetic and copies ran while one was open for 0% of the time, Pallas kernels for 0%

profile of v1, /device:TPU:0, one launch (start us, length us, event | category | flops | bytes accessed | tf_op | source)
XLA Modules:
  0.0 214.9 jit_solution(8308265685047915788)
XLA Ops:
  0.0 0.0 copy-start
  0.0 2.0 slice_reduce_fusion.3
  2.0 1.1 multiply_add_fusion.1
  3.0 0.0 copy-start.2
  3.0 0.0 copy-start.3
  3.1 0.0 copy-start.4
  3.1 0.0 copy-start.5
  3.1 2.4 %pad_maximum_fusion = f32[3,184,1536]{2,1,0:T(8,128)S(1)} fusion(f32[3,184,64]{2,1,0:T(8,128)S(1)} %multiply_add_fusion.1, f32[3,184,1472]{2,1,0:T(8,128)} %param.14), kind=kLoop, calls=%fused_computation.6 | loop fusion | flops 847872 | bytes 6782976 | tf_op jit(solution)/shard_map/concatenate | solution.py:35
  5.5 0.0 copy-done.2
  5.5 0.0 copy-done.3
  5.5 0.0 copy-done.4
  5.5 0.0 copy-done.5
  5.5 1.1 multiply_add_fusion
  6.6 0.0 copy-start.1
  6.6 2.7 %copy-done.1 = f32[64,16,1536]{2,1,0:T(8,128)} copy-done((f32[64,16,1536]{2,1,0:T(8,128)}, f32[64,16,1536]{2,1,0:T(8,128)S(1)}, u32[]{:S(2)}) %copy-start.1) | copy-done | bytes 6291480
  9.3 9.2 %fusion.25 = f32[32,32,552]{2,1,0:T(8,128)} fusion(f32[32,32,1536]{2,1,0:T(8,128)S(1)} %bitcast.37, f32[552,1536,1]{1,0,2:T(8,128)S(1)} %bitcast.45), kind=kOutput, calls=%fused_computation.42 | convolution fusion | flops 5209325568 | bytes 11943936 | tf_op jit(solution)/shard_map/qn,lrn->qlr/dot_general | solution.py:61
  18.5 7.5 %all-to-all-start = ((f32[32,32,552]{2,1,0:T(8,128)}), f32[32,32,552]{2,1,0:T(8,128)S(1)}, u32[]{:S(2)}, u32[]{:S(2)}) async-start(f32[32,32,552]{2,1,0:T(8,128)} %fusion.25), calls=%async_computation | async-start | bytes 5242880 | tf_op jit(solution)/shard_map/all_to_all | solution.py:63
  26.0 0.0 copy-done.7
  26.0 0.1 dynamic_slice.7
  26.1 0.0 copy-done.6
  26.1 0.1 dynamic_slice.6
  26.2 0.1 broadcast_add_fusion
  26.3 0.1 fusion.20
  26.4 59.7 %all-to-all-done = f32[32,32,552]{2,1,0:T(8,128)S(1)} async-done(((f32[32,32,552]{2,1,0:T(8,128)}), f32[32,32,552]{2,1,0:T(8,128)S(1)}, u32[]{:S(2)}, u32[]{:S(2)}) %all-to-all-start) | async-done | bytes 2261024 | tf_op jit(solution)/shard_map/all_to_all | solution.py:63
  86.0 3.9 %reshape.117 = f32[8,4,32,3,184]{4,3,2,1,0:T(4,128)} reshape(f32[32,32,552]{2,1,0:T(8,128)S(1)} %all-to-all-done) | data formatting | bytes 4521984 | tf_op jit(solution)/shard_map/reshape | solution.py:64
  89.9 5.7 %copy.20 = f32[4,3,32,8,184]{4,3,2,1,0:T(8,128)} copy(f32[4,3,32,8,184]{4,1,2,0,3:T(4,128)} %bitcast.43) | data formatting | bytes 4521984 | tf_op jit(solution)/shard_map/transpose | solution.py:64
  95.6 3.3 %reshape.118 = f32[12,32,1472]{2,1,0:T(8,128)S(1)} reshape(f32[4,3,32,8,184]{4,3,2,1,0:T(8,128)} %copy.20) | data formatting | bytes 4521984 | tf_op jit(solution)/shard_map/reshape | solution.py:65
  98.9 0.4 slice_reduce_fusion.7
  99.4 0.0 copy-done.8
  99.4 0.0 copy-done.9
  99.4 0.0 copy-done.10
  99.4 0.3 multiply_add_fusion.2
  99.7 0.0 copy-start.13
  99.7 6.5 %fusion.4 = f32[12,32,1024]{2,1,0:T(8,128)S(1)} fusion(f32[1024,1536,1]{1,0,2:T(8,128)} %bitcast.38, f32[12,32,64]{2,1,0:T(8,128)S(1)} %multiply_add_fusion.2, f32[12,32,1472]{2,1,0:T(8,128)S(1)} %reshape.118), kind=kOutput, calls=%fused_computation.8 | convolution fusion | flops 3624468480 | bytes 10223616 | tf_op jit(solution)/shard_map/lqr,pr->lqp/dot_general | solution.py:66
  106.3 0.0 copy-start.12
  106.3 0.0 slice-start
  106.3 3.4 %fusion.9 = f32[32,1024,12]{1,2,0:T(8,128)S(1)} fusion(f32[12,32,1024]{2,1,0:T(8,128)S(1)} %fusion.4, f32[12,12]{1,0:T(8,128)S(1)} %copy-done), kind=kOutput, calls=%fused_computation.14 | convolution fusion | flops 56623104 | bytes 3146304 | tf_op jit(solution)/shard_map/ml,lqp->mqp/dot_general | solution.py:73
  109.7 0.0 slice-start.1
  109.7 2.7 %fusion.14 = f32[12,32,1024]{2,0,1:T(8,128)S(1)} fusion(f32[32,1024,12]{1,2,0:T(8,128)S(1)} %fusion.9, f32[32,1024]{1,0:T(8,128)S(1)} %broadcast_add_fusion, f32[12]{0:T(128)S(1)} %copy-done.13, f32[32,1024]{1,0:T(8,128)S(1)} %fusion.20, f32[12,12]{1,0:T(8,128)S(1)} %copy-done.12), kind=kOutput, calls=%fused_computation.19 | convolution fusion | flops 58195968 | bytes 3408496 | tf_op jit(solution)/shard_map/lm,mqp->lqp/dot_general | solution.py:75
  112.5 0.0 slice-done
  112.5 0.0 slice-done.1
  112.5 6.5 %fusion.1 = f32[12,32,1472]{2,1,0:T(8,128)} fusion(f32[1024,1536]{1,0:T(8,128)S(1)} %bitcast.42, f32[12,32,1024]{2,0,1:T(8,128)S(1)} %fusion.14), kind=kOutput, calls=%fused_computation.3 | convolution fusion | flops 3472883712 | bytes 10125312 | tf_op jit(solution)/shard_map/lqp,pr->lqr/dot_general | solution.py:76
  119.0 3.9 %reshape.119 = f32[4,3,32,8,184]{4,3,2,1,0:T(8,128)S(1)} reshape(f32[12,32,1472]{2,1,0:T(8,128)} %fusion.1) | data formatting | bytes 4521984 | tf_op jit(solution)/shard_map/reshape | solution.py:77
  122.9 4.2 %copy.34 = f32[4,3,32,8,184]{4,1,2,0,3:T(4,128)} copy(f32[4,3,32,8,184]{4,3,2,1,0:T(8,128)S(1)} %reshape.119) | data formatting | bytes 4521984 | tf_op jit(solution)/shard_map/reshape | solution.py:77
  127.1 4.8 %reshape.120 = f32[32,32,552]{2,1,0:T(8,128)S(1)} reshape(f32[8,4,32,3,184]{4,3,2,1,0:T(4,128)} %bitcast.44) | data formatting | bytes 4521984 | tf_op jit(solution)/shard_map/reshape | solution.py:78
  131.9 64.4 %all_to_all.10 = f32[32,32,552]{2,1,0:T(8,128)} all-to-all(f32[32,32,552]{2,1,0:T(8,128)S(1)} %reshape.120), channel_id=1, replica_groups=mesh['wide'=8,'lev'=4] {'wide','lev'}, dimensions={0} | all-to-all | bytes 4521984 | tf_op jit(solution)/shard_map/all_to_all | solution.py:78
  196.4 6.4 %reshape.121 = f32[1024,3,184]{2,1,0:T(4,128)} reshape(f32[32,32,552]{2,1,0:T(8,128)} %all_to_all.10) | data formatting | bytes 4521984 | tf_op jit(solution)/shard_map/reshape | solution.py:79
  202.8 12.1 %fusion.2 = f32[3,184,1472]{2,1,0:T(8,128)} fusion(f32[1024,1536]{1,0:T(8,128)} %bitcast.39, f32[1024,3,184]{2,1,0:T(4,128)} %reshape.121), kind=kOutput, calls=%fused_computation.5 | convolution fusion | flops 4993082880 | bytes 11802624 | tf_op jit(solution)/shard_map/qlr,qn->lrn/dot_general | solution.py:80
  (11 shorter events, 0.0 us)
Async XLA Ops:
  0.0 106.2 %copy-start = (f32[12,12]{1,0:T(8,128)S(1)}, f32[12,12]{1,0:T(8,128)}, u32[]{:S(2)}) copy-start(f32[12,12]{1,0:T(8,128)} %param.15) | copy-start | bytes 1732
  3.0 2.4 %copy-start.2 = (f32[64,1536]{1,0:T(8,128)S(1)}, f32[64,1536]{1,0:T(8,128)}, u32[]{:S(2)}) copy-start(f32[64,1536]{1,0:T(8,128)} %constant.42.clone) | copy-start | bytes 1179652
  3.0 2.4 %copy-start.3 = (f32[64,1536]{1,0:T(8,128)S(1)}, f32[64,1536]{1,0:T(8,128)}, u32[]{:S(2)}) copy-start(f32[64,1536]{1,0:T(8,128)} %constant.43.clone) | copy-start | bytes 1179652
  3.1 2.4 %copy-start.4 = (f32[16,1536]{1,0:T(8,128)S(1)}, f32[16,1536]{1,0:T(8,128)}, u32[]{:S(2)}) copy-start(f32[16,1536]{1,0:T(8,128)} %constant.44.clone) | copy-start | bytes 294916
  3.1 2.4 %copy-start.5 = (f32[16,1536]{1,0:T(8,128)S(1)}, f32[16,1536]{1,0:T(8,128)}, u32[]{:S(2)}) copy-start(f32[16,1536]{1,0:T(8,128)} %constant.45.clone) | copy-start | bytes 294916
  6.6 2.7 %copy-start.1 = (f32[64,16,1536]{2,1,0:T(8,128)}, f32[64,16,1536]{2,1,0:T(8,128)S(1)}, u32[]{:S(2)}) copy-start(f32[64,16,1536]{2,1,0:T(8,128)S(1)} %multiply_add_fusion) | copy-start | bytes 18874372
  18.5 7.5 %copy-start.7 = (f32[1024]{0:T(1024)S(1)}, f32[1024]{0:T(1024)}, u32[]{:S(2)}) copy-start(f32[1024]{0:T(1024)} %constant.47.clone) | copy-start | bytes 12292
  18.5 7.6 %copy-start.6 = (s32[1024]{0:T(1024)S(1)}, s32[1024]{0:T(1024)}, u32[]{:S(2)}) copy-start(s32[1024]{0:T(1024)} %constant.48.clone) | copy-start | bytes 12292
  18.5 67.5 %all-to-all-start = ((f32[32,32,552]{2,1,0:T(8,128)}), f32[32,32,552]{2,1,0:T(8,128)S(1)}, u32[]{:S(2)}, u32[]{:S(2)}) async-start(f32[32,32,552]{2,1,0:T(8,128)} %fusion.25), calls=%async_computation | async-start | bytes 5242880 | tf_op jit(solution)/shard_map/all_to_all | solution.py:63
  95.6 3.8 %copy-start.8 = (f32[64]{0:T(128)S(1)}, f32[64]{0:T(128)}, u32[]{:S(2)}) copy-start(f32[64]{0:T(128)} %constant.53) | copy-start | bytes 772
  95.6 3.8 %copy-start.9 = (f32[64]{0:T(128)S(1)}, f32[64]{0:T(128)}, u32[]{:S(2)}) copy-start(f32[64]{0:T(128)} %constant.55) | copy-start | bytes 772
  95.6 3.8 %copy-start.10 = (f32[64]{0:T(128)S(1)}, f32[64]{0:T(128)}, u32[]{:S(2)}) copy-start(f32[64]{0:T(128)} %constant.57) | copy-start | bytes 772
  95.6 3.8 %copy-start.11 = (f32[64]{0:T(128)S(1)}, f32[64]{0:T(128)}, u32[]{:S(2)}) copy-start(f32[64]{0:T(128)} %constant.59) | copy-start | bytes 772
  99.7 10.0 %copy-start.13 = (f32[12]{0:T(128)S(1)}, f32[12]{0:T(128)}, u32[]{:S(2)}) copy-start(f32[12]{0:T(128)} %param.17) | copy-start | bytes 148
  106.3 3.5 %copy-start.12 = (f32[12,12]{1,0:T(8,128)S(1)}, f32[12,12]{1,0:T(8,128)}, u32[]{:S(2)}) copy-start(f32[12,12]{1,0:T(8,128)} %param.16) | copy-start | bytes 1732
  106.3 6.2 %slice-start = ((s8[6291456]{0:T(1024)(128)(4,1)}), s8[4194304]{0:T(1024)(128)(4,1)S(1)}, s32[]{:S(2)}) async-start(s8[6291456]{0:T(1024)(128)(4,1)} %bitcast.40), calls=%async_computation.2 | async-start | bytes 8388608
  109.7 2.7 %slice-start.1 = ((s8[6291456]{0:T(1024)(128)(4,1)}), s8[2097152]{0:T(1024)(128)(4,1)S(1)}, s32[]{:S(2)}) async-start(s8[6291456]{0:T(1024)(128)(4,1)} %bitcast.40), calls=%async_computation.3 | async-start | bytes 4194304

commit v2 on v1

--- a/solution.py
+++ b/solution.py
@@ -1,15 +1,20 @@
-import math
+import functools
 
 import jax
 import jax.numpy as jnp
 import numpy as np
 from jax import lax
+from jax.experimental import pallas as pl
+from jax.experimental.pallas import tpu as pltpu
 from jax.sharding import PartitionSpec as P
 
 I = 1472
 E = 64
 KT = 512
 STEP = 16
+LANES = 128
+HALF = 64
+TILE = 256
 
 HIGH = lax.Precision.HIGH
 HIGHEST = lax.Precision.HIGHEST
@@ -80,8 +85,382 @@
     return jnp.einsum("qlr,qn->lrn", back, table[:, :I], precision=HIGH) / (length * length)
 
 
+def split(value):
+    high = value.astype(jnp.bfloat16)
+    return high, (value - high.astype(jnp.float32)).astype(jnp.bfloat16)
+
+
+def dot(a, b, contract):
+    return lax.dot_general(a, b, (contract, ((), ())), preferred_element_type=jnp.float32)
+
+
+def left_half():
+    return lax.broadcasted_iota(jnp.int32, (1, LANES), 1) < HALF
+
+
+def swap(value):
+    return pltpu.roll(value, HALF, 1)
+
+
+def at(start, size, unit):
+    return pl.ds(start if isinstance(start, int) else pl.multiple_of(start, unit), size)
+
+
+def fill_table(seeds, first, high, low):
+    plus, minus, cosine, sine = seeds
+    cosines, sines = cosine[...], sine[...]
+    for group in range(high.shape[0] // STEP):
+        rows = slice(group * STEP, (group + 1) * STEP)
+        pick = pl.ds(first + group, 1)
+        high[rows], low[rows] = split(plus[pick] * cosines + minus[pick] * sines)
+
+
+def forward_x(chunk, odd, x, edge, *refs, with_y):
+    levels, rows, cols = x.shape
+    seeds, refs = refs[:4], refs[4:]
+    if with_y:
+        seeds_y, refs = refs[:4], refs[4:]
+        out, high, low, y_high, y_low, xs_high, xs_low = refs
+    else:
+        out, high, low, xs_high, xs_low = refs
+    step = pl.program_id(0)
+
+    @pl.when(step == 0)
+    def _():
+        whole = cols // LANES * LANES
+
+        def place(start, value):
+            extra = sum(value[:, c : c + 1] * edge[i : i + 1] for i, c in enumerate((0, 1, cols - 2, cols - 1)))
+            rest = value[:, whole:]
+            last = jnp.concatenate([rest, jnp.zeros_like(rest)], axis=1) + extra
+            where = at(start, value.shape[0], HALF)
+            xs_high[where, :whole], xs_low[where, :whole] = split(value[:, :whole])
+            xs_high[where, whole:], xs_low[where, whole:] = split(last)
+
+        blank = jnp.zeros((LANES + HALF - rows, cols), jnp.float32)
+        flag = odd[0]
+        for level in range(levels):
+            place(level * LANES, x[level, :LANES])
+            rest = jnp.concatenate([x[level, LANES:], blank], axis=0)
+            if level < 2:
+                place(levels * LANES + HALF * (flag if level == 0 else 1 - flag), rest)
+            else:
+                place((levels + 1) * LANES, rest)
+                place((levels + 1) * LANES + HALF, rest)
+
+    fill_table(seeds, chunk + step * (high.shape[0] // STEP), high, low)
+    if with_y:
+        fill_table(seeds_y, step * (y_high.shape[0] // STEP), y_high, y_low)
+    t_high = high[...]
+    across = ((1,), (1,))
+    spec = dot(t_high, xs_high[...], across) + (dot(low[...], xs_high[...], across) + dot(t_high, xs_low[...], across))
+    left = left_half()
+    for d in range(out.shape[0]):
+        part = spec[d * STEP : (d + 1) * STEP]
+        for piece in range(levels + 1):
+            out[d, piece * STEP : (piece + 1) * STEP] = part[:, piece * LANES : (piece + 1) * LANES]
+        last = part[:, (levels + 1) * LANES :]
+        out[d, (levels + 1) * STEP :] = jnp.where(left, last[: STEP // 2], last[STEP // 2 :])
+
+
+def middle(
+    chunk, devices, me, to_modes, from_modes, depth, got, high, low, edge, own, line, out, xs, ms, ends, *, wide, tail
+):
+    count = got.shape[0]
+    lev = count // wide
+    total = to_modes.shape[0]
+    levels = total // lev
+    span = total * STEP
+    left = left_half()
+    rem = slice(levels * STEP, (levels + 1) * STEP)
+    rem2 = slice((levels + 1) * STEP, (levels + 1) * STEP + STEP // 2)
+
+    def rows_of(lv, level):
+        start = (lv * levels + level) * STEP
+        return start, slice(start, start + STEP)
+
+    for lv in range(lev):
+        first_src, last_src = lv, (wide - 1) * lev + lv
+        for level in range(levels):
+            start, rows = rows_of(lv, level)
+            ends[rows, 0:2] = got[first_src, level * STEP : (level + 1) * STEP, 0:2]
+            if level < 2:
+                lane = (HALF if level == 0 else 0) + tail - 2
+                ends[rows, 2:4] = got[last_src, rem, lane : lane + 2]
+            else:
+                ends[start : start + STEP // 2, 2:4] = got[last_src, rem2, tail - 2 : tail]
+                ends[start + STEP // 2 : start + STEP, 2:4] = got[last_src, rem2, HALF + tail - 2 : HALF + tail]
+
+    def gather(pair, carry):
+        weights = edge[:, at(pair * LANES, LANES, LANES)]
+
+        def put(start, size, lanes, value):
+            for base, part in zip((0, span), split(value)):
+                xs[base + start : base + start + size, lanes] = part
+
+        for lv in range(lev):
+            even, uneven = 2 * pair * lev + lv, (2 * pair + 1) * lev + lv
+            for level in range(levels):
+                start, rows = rows_of(lv, level)
+                full = slice(level * STEP, (level + 1) * STEP)
+                put(start, STEP, at(2 * pair * LANES, LANES, LANES), got[even, full])
+                put(start, STEP, at((2 * pair + 1) * LANES, LANES, LANES), got[uneven, full])
+                if level < 2:
+                    a, b = got[even, rem], got[uneven, rem]
+                    value = jnp.where(left, a, b) if level == 0 else swap(jnp.where(left, b, a))
+                else:
+                    a, b = got[even, rem2], got[uneven, rem2]
+                    value = jnp.concatenate([jnp.where(left, a, swap(b)), jnp.where(left, swap(a), b)], axis=0)
+                for i in range(4):
+                    value = value + ends[rows, i : i + 1] * weights[i : i + 1]
+                put(start, STEP, at(wide * LANES + pair * LANES, LANES, LANES), value)
+        return carry
+
+    lax.fori_loop(0, wide // 2, gather, 0)
+
+    group = chunk * devices + me[0]
+    mine = lax.broadcasted_iota(jnp.int32, (1, LANES), 1) == group
+    lap_q = jnp.sum(jnp.where(mine, own[0], 0.0), axis=1, keepdims=True)
+    square_q = jnp.sum(jnp.where(mine, own[1], 0.0), axis=1, keepdims=True)
+    length = high.shape[1]
+
+    def solve(tile, carry):
+        where = at(tile * TILE, TILE, TILE)
+        across = ((1,), (1,))
+        both = dot(xs[...], high[where], across)
+        spec = both[:span] + (both[span:] + dot(xs[:span], low[where], across))
+        for half in range(TILE // LANES):
+            lanes = slice(half * LANES, (half + 1) * LANES)
+            here = at(tile * TILE + half * LANES, LANES, LANES)
+            lap = lap_q + line[0:1, here]
+            scale = jnp.where(square_q + line[1:2, here] < float(KT * KT), 1.0 / (length * length), 0.0)
+            parts = [spec[l * STEP : (l + 1) * STEP, lanes] for l in range(total)]
+            solved = []
+            for m in range(total):
+                mode = sum(to_modes[m, l] * parts[l] for l in range(total))
+                solved.append(mode * scale / (1.0 + depth[m] * lap))
+            for l in range(total):
+                mixed = sum(from_modes[l, m] * solved[m] for m in range(total))
+                for base, part in zip((0, span), split(mixed)):
+                    ms[base + l * STEP : base + (l + 1) * STEP, here] = part
+        return carry
+
+    lax.fori_loop(0, high.shape[0] // TILE, solve, 0)
+
+    def back(start):
+        where = at(start, TILE, TILE)
+        down = ((1,), (0,))
+        both = dot(ms[...], high[:, where], down)
+        return both[:span] + (both[span:] + dot(ms[:span], low[:, where], down))
+
+    def scatter(pair, carry):
+        value = back(pair * TILE)
+        for half in range(2):
+            for lv in range(lev):
+                for level in range(levels):
+                    _, rows = rows_of(lv, level)
+                    out[(2 * pair + half) * lev + lv, level * STEP : (level + 1) * STEP] = value[
+                        rows, half * LANES : (half + 1) * LANES
+                    ]
+        return carry
+
+    lax.fori_loop(0, wide // 2, scatter, 0)
+
+    def scatter_rest(quad, carry):
+        value = back(wide * LANES + quad * TILE)
+        for half in range(2):
+            pair = 2 * quad + half
+            lanes = slice(half * LANES, (half + 1) * LANES)
+            for lv in range(lev):
+                even, uneven = 2 * pair * lev + lv, (2 * pair + 1) * lev + lv
+                a, b = value[rows_of(lv, 0)[1], lanes], swap(value[rows_of(lv, 1)[1], lanes])
+                out[even, rem] = jnp.where(left, a, b)
+                out[uneven, rem] = jnp.where(left, b, a)
+                start = rows_of(lv, 2)[0]
+                a, b = value[start : start + STEP // 2, lanes], value[start + STEP // 2 : start + STEP, lanes]
+                out[even, rem2] = jnp.where(left, a, swap(b))
+                out[uneven, rem2] = jnp.where(left, swap(a), b)
+        return carry
+
+    lax.fori_loop(0, wide // 4, scatter_rest, 0)
+
+
+def inverse_x(odd, got, high, low, *refs, more):
+    prior, refs = (refs[0], refs[1:]) if more else (None, refs)
+    out, zs = refs
+    levels, rows, _ = out.shape
+    span = zs.shape[0] // 2
+    waves = zs.shape[1]
+
+    @pl.when(pl.program_id(0) == 0)
+    def _():
+        def place(start, value):
+            size = min(LANES, span - start)
+            turned = value.reshape(waves, LANES).T[:size]
+            for base, part in zip((0, span), split(turned)):
+                zs[base + start : base + start + size] = part
+
+        for piece in range(levels + 1):
+            place(piece * LANES, got[:, piece * STEP : (piece + 1) * STEP])
+        last = got[:, (levels + 1) * STEP :]
+        turned = swap(last.reshape(waves // 2, LANES)).reshape(last.shape)
+        place((levels + 1) * LANES, jnp.concatenate([last, turned], axis=1))
+
+    down = ((1,), (0,))
+    both = dot(zs[...], high[...], down)
+    value = both[:span] + (both[span:] + dot(zs[:span], low[...], down))
+    flag = odd[0]
+    rest = rows - LANES
+    places = [(level, slice(0, LANES), level * LANES) for level in range(levels)]
+    for level, start in ((flag, levels * LANES), (1 - flag, levels * LANES + HALF), (2, (levels + 1) * LANES)):
+        places.append((level, slice(LANES, rows), start))
+    for level, where, start in places:
+        part = value[start : start + where.stop - where.start]
+        out[level, where] = part + prior[level, where] if more else part
+
+
+def packs(wide, lev, levels, rows, cols):
+    share = 2 * KT // (wide * lev)
+    return (
+        levels == 3
+        and wide % 4 == 0
+        and LANES < rows <= LANES + HALF
+        and (LANES + HALF - rows) * wide == E
+        and cols % LANES == HALF == E
+        and (cols + E) % TILE == 0
+        and (wide * lev * STEP) % TILE == 0
+        and share % STEP == 0
+        and 2 * KT // STEP <= LANES
+    )
+
+
+def packed(state, to_modes, from_modes, mode_depth):
+    wide, lev = lax.axis_size("wide"), lax.axis_size("lev")
+    levels, rows, cols = state.shape
+    devices = wide * lev
+    length = cols + E
+    chunks = 2 * KT // (devices * STEP)
+    width = devices * STEP
+    tail = rows - LANES
+    extra = E // wide
+    block = (levels + 1) * STEP + STEP // 2
+    total = lev * levels
+    f32, bf16 = jnp.float32, jnp.bfloat16
+
+    waves = np.arange(-KT, KT)
+    columns = np.arange(length)
+    starts = np.arange(wide)[:, None]
+    order = np.concatenate(
+        [
+            (starts * rows + np.arange(LANES)).reshape(-1),
+            np.concatenate(
+                [starts * rows + LANES + np.arange(tail), cols + starts * extra + np.arange(extra)], axis=1
+            ).reshape(-1),
+        ]
+    )
+    seeds_x = [jnp.asarray(a) for a in cas_seeds(waves, columns, length)]
+    seeds_y = [jnp.asarray(a) for a in cas_seeds(waves, order, length)]
+    weights = edge_weights(E)
+    edge_x = np.concatenate([np.zeros((4, HALF), np.float32), weights], axis=1)
+    edge_y = np.zeros((4, length), np.float32)
+    edge_y[:, order >= cols] = weights[:, order[order >= cols] - cols]
+    edge_y = edge_y[:, wide * LANES :]
+    lap = (4.0 * np.sin(np.pi * waves / length) ** 2).astype(np.float32)
+    line = np.stack([lap, (waves * waves).astype(np.float32)])
+    own = np.zeros((2, STEP, LANES), np.float32)
+    own[:, :, : len(waves) // STEP] = line.reshape(2, -1, STEP).transpose(0, 2, 1)
+
+    odd = lax.rem(lax.axis_index("wide"), 2).reshape(1)
+    me = (lax.axis_index("wide") * lev + lax.axis_index("lev")).reshape(1)
+    smem = pl.BlockSpec(memory_space=pltpu.SMEM)
+    vmem = pl.BlockSpec(memory_space=pltpu.VMEM)
+    params = pltpu.CompilerParams(vmem_limit_bytes=56 << 20)
+
+    def whole(a):
+        return pl.BlockSpec(a.shape, lambda i: (0,) * a.ndim)
+
+    def cost(flops, size):
+        return pl.CostEstimate(flops=flops, bytes_accessed=size, transcendentals=0)
+
+    def to_columns(chunk):
+        with_y = chunk == chunks - 1
+        steps = width // TILE
+        operands = [state, jnp.asarray(edge_x), *seeds_x] + (seeds_y if with_y else [])
+        shapes = [((devices, block, LANES), f32), ((width, length), bf16), ((width, length), bf16)]
+        if with_y:
+            shapes += [((2 * KT, length), bf16)] * 2
+        span = (levels + 2) * LANES
+        return pl.pallas_call(
+            functools.partial(forward_x, chunk * devices, with_y=with_y),
+            grid=(steps,),
+            in_specs=[smem] + [whole(a) for a in operands],
+            out_specs=[
+                pl.BlockSpec((s[0] // steps, *s[1:]), lambda i, n=len(s): (i,) + (0,) * (n - 1)) for s, _ in shapes
+            ],
+            out_shape=[jax.ShapeDtypeStruct(s, d) for s, d in shapes],
+            scratch_shapes=[pltpu.VMEM((span, length), bf16)] * 2,
+            compiler_params=params,
+            cost_estimate=cost(6 * width * span * length, 8 << 20),
+            name=f"forward_x_{chunk}",
+        )(odd, *operands)
+
+    def through(chunk, got, high, low):
+        operands = [got, high, low, jnp.asarray(edge_y), jnp.asarray(own), jnp.asarray(line)]
+        span = total * STEP
+        return pl.pallas_call(
+            functools.partial(middle, chunk, devices, wide=wide, tail=tail),
+            in_specs=[smem] * 4 + [vmem] * len(operands),
+            out_specs=vmem,
+            out_shape=jax.ShapeDtypeStruct(got.shape, f32),
+            scratch_shapes=[
+                pltpu.VMEM((2 * span, length), bf16),
+                pltpu.VMEM((2 * span, 2 * KT), bf16),
+                pltpu.VMEM((span, LANES), f32),
+            ],
+            compiler_params=params,
+            cost_estimate=cost(12 * span * 2 * KT * length, 9 << 20),
+            name=f"middle_{chunk}",
+        )(me, to_modes, from_modes, mode_depth, *operands)
+
+    def to_rows(got, high, low, prior):
+        span = (levels + 1) * LANES + HALF
+        tables = pl.BlockSpec((width, TILE), lambda i: (0, i))
+        sums = pl.BlockSpec((levels, rows, TILE), lambda i: (0, 0, i))
+        more = prior is not None
+        return pl.pallas_call(
+            functools.partial(inverse_x, more=more),
+            grid=(length // TILE,),
+            in_specs=[smem, whole(got), tables, tables] + [sums] * more,
+            out_specs=sums,
+            out_shape=jax.ShapeDtypeStruct(state.shape, f32),
+            scratch_shapes=[pltpu.VMEM((2 * span, width), bf16)],
+            compiler_params=params,
+            cost_estimate=cost(6 * width * span * length, 8 << 20),
+            name="inverse_x",
+        )(odd, got, high, low, *([prior] if more else []))
+
+    def exchange(sent):
+        return lax.all_to_all(sent, AXES, 0, 0, tiled=True)
+
+    tables, arrived = [], []
+    for chunk in range(chunks):
+        sent, high, low, *table_y = to_columns(chunk)
+        tables.append((high, low))
+        arrived.append(exchange(sent))
+    returned = [exchange(through(chunk, got, *table_y)) for chunk, got in enumerate(arrived)]
+    value = None
+    for got, table in zip(returned, tables):
+        value = to_rows(got, *table, value)
+    return value
+
+
 def solution(mesh):
     placed = (P("lev", "wide", None), P(), P(), P())
+
+    def shards(state, *rest):
+        fits = packs(lax.axis_size("wide"), lax.axis_size("lev"), *state.shape)
+        return (packed if fits else plain)(state, *rest)
+
     return jax.shard_map(
-        plain, mesh=mesh, in_specs=placed, out_specs=P("lev", "wide", None), check_vma=False
+        shards, mesh=mesh, in_specs=placed, out_specs=P("lev", "wide", None), check_vma=False
     )

time: 216 us -> 153 us (0.71)
  blocking collectives: 64.4 us -> 0 us
  Pallas kernels: 0 us -> 62.7 us
  matrix products: 40.6 us -> 0 us
  local copies, waits for them, and re-layouts: 37.5 us -> 1.01 us
  starting transfers between devices: 7.5 us -> 18.2 us
  waiting for transfers between devices: 59.7 us -> 70.1 us
  other arithmetic: 4.95 us -> 0 us
    all_to_all x1 -> x0, blocking collectives: 64.4 us -> none  [plain(): lax.all_to_all(back.reshape(devices, share, levels * rows), AXES, 0, 0, t...]
    pallas_call x0 -> x6, Pallas kernels: none -> 62.7 us  [the longest x2 26.4 us: through(): pl.pallas_call(functools.partial(middle, chunk, devices, wide=wide, tail=...]
    dot_general x6 -> x0, matrix products: 40.6 us -> none  [the longest x1 12.1 us: plain(): jnp.einsum('qlr,qn->lrn', back, table[:, :I], precision=HIGH)]
    reshape x6 -> x0, local copies, waits for them, and re-layouts: 26.5 us -> none  [the longest x2 8.05 us: plain(): back = back.reshape(lev, levels, share, wide, rows).transpose(3, 0, 2, 1, 4)]
    all_to_all x1 -> x4, starting transfers between devices: 7.5 us -> 18.2 us  [exchange(): return lax.all_to_all(sent, AXES, 0, 0, tiled=True)]
    all_to_all x1 -> x4, waiting for transfers between devices: 59.7 us -> 70.1 us  [exchange(): return lax.all_to_all(sent, AXES, 0, 0, tiled=True)]
    transpose x1 -> x0, local copies, waits for them, and re-layouts: 5.67 us -> none  [plain(): spec = spec.reshape(wide, lev, share, levels, rows).transpose(1, 3, 2, 0, 4)]
    add x4 -> x0, other arithmetic: 2.49 us -> none  [the longest x2 1.33 us: extend(): block[..., :1] * w[0] + block[..., 1:2] * w[1] + block[..., -2:-1] * w[2]]
  transfers between devices with their start and end apart: 1 -> 4, of which waited for: 1 -> 4; matrix products, arithmetic and copies ran while one was open for 0% -> 0% of each run, Pallas kernels for 0% -> 30%
where the time goes in v2:
time: 153 us; the launch traced here: 152 us
  waiting for transfers between devices  70.1 us (46%)
  Pallas kernels  62.7 us (41%)
  starting transfers between devices  18.2 us (12%)
    all_to_all x4, waiting for transfers between devices, exchange(): return lax.all_to_all(sent, AXES, 0, 0, tiled=True)  70.1 us
    pallas_call x2, Pallas kernels, through(): pl.pallas_call(functools.partial(middle, chunk, devices, wide=wide, tail=...  26.4 us
    pallas_call x2, Pallas kernels, to_columns(): pl.pallas_call(functools.partial(forward_x, chunk * devices, with_y=with_...  19.7 us
    all_to_all x4, starting transfers between devices, exchange(): return lax.all_to_all(sent, AXES, 0, 0, tiled=True)  18.2 us
    pallas_call x2, Pallas kernels, to_rows(): pl.pallas_call(functools.partial(inverse_x, more=more), grid=(length // T...  16.6 us
  transfers between devices with their start and end apart: 4, of which 4 were waited for; matrix products, arithmetic and copies ran while one was open for 0% of the time, Pallas kernels for 30%

profile of v2, /device:TPU:0, one launch (start us, length us, event | category | flops | bytes accessed | tf_op | source)
XLA Modules:
  0.0 152.1 jit_solution(3713189663603335256)
XLA Ops:
  0.0 8.2 %forward_x_0.1 = (f32[32,72,128]{2,1,0:T(8,128)}, bf16[512,1536]{1,0:T(8,128)(2,1)}, bf16[512,1536]{1,0:T(8,128)(2,1)}) custom-call(s32[1]{0:T(128)} %bitcast.odd, f32[3,184,1472]{2,1,0:T(8,128)} %x.3, f32[4,128]{1,0:T(4,128)} %constant.48.clone.edge, f32[64,1536]{1,0:T(8,128)} %constant.40.clone.refs_0_, f32[64,1536]{1,0:T(8,128)} %constant.41.clone.refs_1_, ...), custom_call_target="tpu_custom_call" | custom-call | flops 3019898880 | bytes 8388608 | tf_op jit(solution)/shard_map/forward_x_0/pallas_call | solution.py:393
  8.2 7.3 %all-to-all-start.2 = ((f32[32,72,128]{2,1,0:T(8,128)}), f32[32,72,128]{2,1,0:T(8,128)S(1)}, u32[]{:S(2)}, u32[]{:S(2)}) async-start(f32[32,72,128]{2,1,0:T(8,128)} %get-tuple-element.18), calls=%async_computation.2 | async-start | bytes 2359296 | tf_op jit(solution)/shard_map/all_to_all | solution.py:443
  15.6 11.5 %forward_x_1.1 = (f32[32,72,128]{2,1,0:T(8,128)}, bf16[512,1536]{1,0:T(8,128)(2,1)}, bf16[512,1536]{1,0:T(8,128)(2,1)}, bf16[1024,1536]{1,0:T(8,128)(2,1)}, bf16[1024,1536]{1,0:T(8,128)(2,1)}) custom-call(s32[1]{0:T(128)} %bitcast.odd, f32[3,184,1472]{2,1,0:T(8,128)} %x.3, f32[4,128]{1,0:T(4,128)} %constant.48.clone.edge, ...), custom_call_target="tpu_custom_call" | custom-call | flops 3019898880 | bytes 8388608 | tf_op jit(solution)/shard_map/forward_x_1/pallas_call | solution.py:393
  27.0 17.6 %all-to-all-done.2.got = f32[32,72,128]{2,1,0:T(8,128)S(1)} async-done(((f32[32,72,128]{2,1,0:T(8,128)}), f32[32,72,128]{2,1,0:T(8,128)S(1)}, u32[]{:S(2)}, u32[]{:S(2)}) %all-to-all-start.2) | async-done | bytes 1179680 | tf_op jit(solution)/shard_map/all_to_all | solution.py:443
  44.6 0.0 copy-start.1
  44.6 3.6 %all-to-all-start = ((f32[32,72,128]{2,1,0:T(8,128)}), f32[32,72,128]{2,1,0:T(8,128)S(1)}, u32[]{:S(2)}, u32[]{:S(2)}) async-start(f32[32,72,128]{2,1,0:T(8,128)} %get-tuple-element.13), calls=%async_computation | async-start | bytes 2359296 | tf_op jit(solution)/shard_map/all_to_all | solution.py:443
  48.2 0.0 copy-done.1
  48.2 13.2 %middle_0.1 = f32[32,72,128]{2,1,0:T(8,128)} custom-call(s32[1]{0:T(128)} %bitcast.1.me, f32[12,12]{1,0:T(8,128)} %to_modes.3, f32[12,12]{1,0:T(8,128)} %from_modes.3, f32[12]{0:T(128)} %depth.3, f32[32,72,128]{2,1,0:T(8,128)} %copy-done.1, bf16[1024,1536]{1,0:T(8,128)(2,1)} %get-tuple-element.14.high, bf16[1024,1536]{1,0:T(8,128)(2,1)} %get-tuple-element.15.low, ...), custom_call_target="tpu_custom_call" | custom-call | flops 3623878656 | bytes 9437184 | tf_op jit(solution)/shard_map/middle_0/pallas_call | solution.py:410
  61.4 15.8 %all-to-all-done.got = f32[32,72,128]{2,1,0:T(8,128)S(1)} async-done(((f32[32,72,128]{2,1,0:T(8,128)}), f32[32,72,128]{2,1,0:T(8,128)S(1)}, u32[]{:S(2)}, u32[]{:S(2)}) %all-to-all-start) | async-done | bytes 1179680 | tf_op jit(solution)/shard_map/all_to_all | solution.py:443
  77.2 0.0 copy-start.2
  77.2 3.6 %all-to-all-start.3 = ((f32[32,72,128]{2,1,0:T(8,128)}), f32[32,72,128]{2,1,0:T(8,128)S(1)}, u32[]{:S(2)}, u32[]{:S(2)}) async-start(f32[32,72,128]{2,1,0:T(8,128)} %middle_0.1), calls=%async_computation.3 | async-start | bytes 2359296 | tf_op jit(solution)/shard_map/all_to_all | solution.py:443
  80.9 0.0 copy-done.2
  80.9 13.2 %middle_1.1 = f32[32,72,128]{2,1,0:T(8,128)} custom-call(s32[1]{0:T(128)} %bitcast.1.me, f32[12,12]{1,0:T(8,128)} %to_modes.3, f32[12,12]{1,0:T(8,128)} %from_modes.3, f32[12]{0:T(128)} %depth.3, f32[32,72,128]{2,1,0:T(8,128)} %copy-done.2, bf16[1024,1536]{1,0:T(8,128)(2,1)} %get-tuple-element.14.high, bf16[1024,1536]{1,0:T(8,128)(2,1)} %get-tuple-element.15.low, ...), custom_call_target="tpu_custom_call" | custom-call | flops 3623878656 | bytes 9437184 | tf_op jit(solution)/shard_map/middle_1/pallas_call | solution.py:410
  94.1 15.8 %all-to-all-done.3.got = f32[32,72,128]{2,1,0:T(8,128)S(1)} async-done(((f32[32,72,128]{2,1,0:T(8,128)}), f32[32,72,128]{2,1,0:T(8,128)S(1)}, u32[]{:S(2)}, u32[]{:S(2)}) %all-to-all-start.3) | async-done | bytes 1179680 | tf_op jit(solution)/shard_map/all_to_all | solution.py:443
  109.9 0.0 copy-start.3
  109.9 3.6 %all-to-all-start.1 = ((f32[32,72,128]{2,1,0:T(8,128)}), f32[32,72,128]{2,1,0:T(8,128)S(1)}, u32[]{:S(2)}, u32[]{:S(2)}) async-start(f32[32,72,128]{2,1,0:T(8,128)} %middle_1.1), calls=%async_computation.1 | async-start | bytes 2359296 | tf_op jit(solution)/shard_map/all_to_all | solution.py:443
  113.5 0.0 copy-done.3
  113.5 8.0 %inverse_x.2.refs_0_ = f32[3,184,1472]{2,1,0:T(8,128)} custom-call(s32[1]{0:T(128)} %bitcast.odd, f32[32,72,128]{2,1,0:T(8,128)} %copy-done.3, bf16[512,1536]{1,0:T(8,128)(2,1)} %get-tuple-element.19.high, bf16[512,1536]{1,0:T(8,128)(2,1)} %get-tuple-element.20.low), custom_call_target="tpu_custom_call" | custom-call | flops 2717908992 | bytes 8388608 | tf_op jit(solution)/shard_map/inverse_x/pallas_call | solution.py:430
  121.5 21.0 %all-to-all-done.1.got = f32[32,72,128]{2,1,0:T(8,128)S(1)} async-done(((f32[32,72,128]{2,1,0:T(8,128)}), f32[32,72,128]{2,1,0:T(8,128)S(1)}, u32[]{:S(2)}, u32[]{:S(2)}) %all-to-all-start.1) | async-done | bytes 1179680 | tf_op jit(solution)/shard_map/all_to_all | solution.py:443
  142.5 0.0 copy-start
  142.5 1.0 copy-done
  143.5 8.6 %inverse_x.3 = f32[3,184,1472]{2,1,0:T(8,128)} custom-call(s32[1]{0:T(128)} %bitcast.odd, f32[32,72,128]{2,1,0:T(8,128)} %copy-done, bf16[512,1536]{1,0:T(8,128)(2,1)} %get-tuple-element.16.high, bf16[512,1536]{1,0:T(8,128)(2,1)} %get-tuple-element.17.low, f32[3,184,1472]{2,1,0:T(8,128)} %inverse_x.2.refs_0_), custom_call_target="tpu_custom_call" | custom-call | flops 2717908992 | bytes 8388608 | tf_op jit(solution)/shard_map/inverse_x/pallas_call | solution.py:430
Async XLA Ops:
  8.2 36.3 %all-to-all-start.2 = ((f32[32,72,128]{2,1,0:T(8,128)}), f32[32,72,128]{2,1,0:T(8,128)S(1)}, u32[]{:S(2)}, u32[]{:S(2)}) async-start(f32[32,72,128]{2,1,0:T(8,128)} %get-tuple-element.18), calls=%async_computation.2 | async-start | bytes 2359296 | tf_op jit(solution)/shard_map/all_to_all | solution.py:443
  44.6 3.6 %copy-start.1 = (f32[32,72,128]{2,1,0:T(8,128)}, f32[32,72,128]{2,1,0:T(8,128)S(1)}, u32[]{:S(2)}) copy-start(f32[32,72,128]{2,1,0:T(8,128)S(1)} %all-to-all-done.2.got) | copy-start | bytes 3538948
  44.6 32.6 %all-to-all-start = ((f32[32,72,128]{2,1,0:T(8,128)}), f32[32,72,128]{2,1,0:T(8,128)S(1)}, u32[]{:S(2)}, u32[]{:S(2)}) async-start(f32[32,72,128]{2,1,0:T(8,128)} %get-tuple-element.13), calls=%async_computation | async-start | bytes 2359296 | tf_op jit(solution)/shard_map/all_to_all | solution.py:443
  77.2 3.6 %copy-start.2 = (f32[32,72,128]{2,1,0:T(8,128)}, f32[32,72,128]{2,1,0:T(8,128)S(1)}, u32[]{:S(2)}) copy-start(f32[32,72,128]{2,1,0:T(8,128)S(1)} %all-to-all-done.got) | copy-start | bytes 3538948
  77.2 32.6 %all-to-all-start.3 = ((f32[32,72,128]{2,1,0:T(8,128)}), f32[32,72,128]{2,1,0:T(8,128)S(1)}, u32[]{:S(2)}, u32[]{:S(2)}) async-start(f32[32,72,128]{2,1,0:T(8,128)} %middle_0.1), calls=%async_computation.3 | async-start | bytes 2359296 | tf_op jit(solution)/shard_map/all_to_all | solution.py:443
  109.9 3.6 %copy-start.3 = (f32[32,72,128]{2,1,0:T(8,128)}, f32[32,72,128]{2,1,0:T(8,128)S(1)}, u32[]{:S(2)}) copy-start(f32[32,72,128]{2,1,0:T(8,128)S(1)} %all-to-all-done.3.got) | copy-start | bytes 3538948
  109.9 32.6 %all-to-all-start.1 = ((f32[32,72,128]{2,1,0:T(8,128)}), f32[32,72,128]{2,1,0:T(8,128)S(1)}, u32[]{:S(2)}, u32[]{:S(2)}) async-start(f32[32,72,128]{2,1,0:T(8,128)} %middle_1.1), calls=%async_computation.1 | async-start | bytes 2359296 | tf_op jit(solution)/shard_map/all_to_all | solution.py:443
  142.5 1.0 copy-start

commit v3 on v1

--- a/solution.py
+++ b/solution.py
@@ -1,15 +1,20 @@
-import math
+import functools
 
 import jax
 import jax.numpy as jnp
 import numpy as np
 from jax import lax
+from jax.experimental import pallas as pl
+from jax.experimental.pallas import tpu as pltpu
 from jax.sharding import PartitionSpec as P
 
 I = 1472
 E = 64
 KT = 512
 STEP = 16
+LANES = 128
+HALF = 64
+TILE = 256
 
 HIGH = lax.Precision.HIGH
 HIGHEST = lax.Precision.HIGHEST
@@ -80,8 +85,550 @@
     return jnp.einsum("qlr,qn->lrn", back, table[:, :I], precision=HIGH) / (length * length)
 
 
+LIMITS = (16, 16, 10, 16)
+
+
+def split(value):
+    high = value.astype(jnp.bfloat16)
+    return high, (value - high.astype(jnp.float32)).astype(jnp.bfloat16)
+
+
+def dot(a, b, contract):
+    return lax.dot_general(a, b, (contract, ((), ())), preferred_element_type=jnp.float32)
+
+
+def left_half():
+    return lax.broadcasted_iota(jnp.int32, (1, LANES), 1) < HALF
+
+
+def swap(value):
+    return pltpu.roll(value, HALF, 1)
+
+
+def mirror(value):
+    order = LANES - 1 - lax.broadcasted_iota(jnp.int32, value.shape, 1)
+    return jnp.take_along_axis(value, order, axis=1)
+
+
+def at(start, size, unit):
+    return pl.ds(start if isinstance(start, int) else pl.multiple_of(start, unit), size)
+
+
+def fill_tables(seeds, first, cos_high, cos_low, sin_high, sin_low):
+    coarse_cos, coarse_sin, fine_cos, fine_sin = seeds
+    for lane in range(0, cos_high.shape[-1], TILE):
+        lanes = slice(lane, lane + TILE)
+        fine_c, fine_s = fine_cos[:, lanes], fine_sin[:, lanes]
+        for group in range(cos_high.shape[0] // STEP):
+            rows = slice(group * STEP, (group + 1) * STEP)
+            pick = pl.ds(first + group, 1)
+            coarse_c, coarse_s = coarse_cos[pick, lanes], coarse_sin[pick, lanes]
+            cos_high[rows, lanes], cos_low[rows, lanes] = split(coarse_c * fine_c - coarse_s * fine_s)
+            sin_high[rows, lanes], sin_low[rows, lanes] = split(coarse_s * fine_c + coarse_c * fine_s)
+
+
+def make_tables(order, *refs):
+    seeds_x, seeds_y, tables_x, (high, low) = refs[:4], refs[4:8], refs[8:12], refs[12:]
+    first = pl.program_id(0) * (tables_x[0].shape[0] // STEP)
+    fill_tables(seeds_x, first, *tables_x)
+    fill_tables(seeds_y, first, high.at[0], low.at[0], high.at[1], low.at[1])
+
+
+def forward_x(chunk, place, x, edge, *refs):
+    seeds, (out, *tables, even, uneven, buffer, packed, in_sems, out_sems) = refs[:4], refs[4:]
+    levels, rows, cols = x.shape
+    waves = tables[0].shape[0]
+    groups = waves // 8
+    size = LANES + HALF
+    half = tables[0].shape[1]
+    step = pl.program_id(0)
+    odd, upper = place[0], place[1]
+    rest = rows - LANES
+    block = 32
+
+    def fetch(level):
+        return pltpu.make_async_copy(x.at[level], buffer.at[level], in_sems.at[level])
+
+    def send(level):
+        first = level * STEP
+        count = STEP if level < levels - 1 else packed.shape[1] - first
+        piece = slice(first, first + count)
+        return pltpu.make_async_copy(packed.at[:, piece], out.at[:, piece], out_sems.at[level])
+
+    @pl.when(step == 0)
+    def _():
+        for level in range(levels):
+            fetch(level).start()
+        fill_tables(seeds, chunk * (waves // STEP), *tables)
+
+    for level in range(levels):
+
+        @pl.when(step == level)
+        def _():
+            fetch(level).wait()
+            for r in range(0, size, block):
+
+                def read(lanes):
+                    if r < LANES:
+                        return buffer[level, at(rest * upper + r, block, 8), lanes]
+                    first = r - LANES
+                    live = min(block, rest - first)
+                    low = buffer[level, LANES + first : LANES + first + live, lanes]
+                    if live < block:
+                        low = jnp.concatenate([low, jnp.zeros((block - live, low.shape[1]), low.dtype)], axis=0)
+                    shift = HALF - rest
+                    if first < shift:
+                        high = buffer[level, 0 : block - shift, lanes]
+                        high = jnp.concatenate([jnp.zeros((shift, high.shape[1]), high.dtype), high], axis=0)
+                    else:
+                        high = buffer[level, first - shift : first - shift + block, lanes]
+                    return jnp.where(upper == 1, high, low)
+
+                where = slice(r, r + block)
+                above = slice(size + r, size + r + block)
+                for tile in range(half // LANES):
+                    lanes = slice(tile * LANES, (tile + 1) * LANES)
+                    value = read(lanes)
+                    start = cols + HALF - (tile + 1) * LANES
+                    other = read(slice(start, min(start + LANES, cols)))
+                    if tile == 0:
+                        ends = (value[:, 0:1], value[:, 1:2], other[:, HALF - 2 : HALF - 1], other[:, HALF - 1 : HALF])
+                        other = jnp.concatenate([other, jnp.zeros_like(other)], axis=1)
+                        for i, end in enumerate(ends):
+                            other = other + end * edge[i : i + 1]
+                    other = mirror(other)
+                    even[where, lanes], even[above, lanes] = split(value + other)
+                    uneven[where, lanes], uneven[above, lanes] = split(value - other)
+
+            across = ((1,), (1,))
+            blank = jnp.zeros((HALF, waves), jnp.float32)
+            for part, (source, high, low) in enumerate(((even, *tables[:2]), (uneven, *tables[2:]))):
+                both = dot(source[...], high[...], across)
+                spec = both[:size] + (both[size:] + dot(source[:size], low[...], across))
+                full = spec[:LANES].T
+                first = level * STEP + part * 8
+                packed[:, first : first + 8] = full.reshape(groups, 8, LANES)
+                if level < 2:
+                    first = levels * STEP + part * 8
+                    if level == 0:
+                        turned = jnp.concatenate([spec[LANES:], blank], axis=0).T
+                        packed[:, first : first + 8] = turned.reshape(groups, 8, LANES)
+                    else:
+                        turned = jnp.concatenate([blank, spec[LANES:]], axis=0).T
+                        value = packed[:, first : first + 8].reshape(waves, LANES) + turned
+                        value = jnp.where(odd == 1, swap(value), value)
+                        packed[:, first : first + 8] = value.reshape(groups, 8, LANES)
+                else:
+                    pieces = [spec[LANES:], blank] if part == 0 else [blank, spec[LANES:]]
+                    turned = jnp.concatenate(pieces, axis=0).T.reshape(groups, 8, LANES)
+                    first = (levels + 1) * STEP
+                    if part == 0:
+                        packed[:, first : first + 8] = turned
+                    else:
+                        packed[:, first : first + 8] = packed[:, first : first + 8] + turned
+            send(level).start()
+
+    @pl.when(step == levels - 1)
+    def _():
+        for level in range(levels):
+            send(level).wait()
+
+
+def middle(
+    chunk, devices, me, to_modes, from_modes, depth, got, *refs, wide
+):
+    high, low, edge, own, line, out, xs, ms, ends = refs
+    count = got.shape[0]
+    lev = count // wide
+    total = to_modes.shape[0]
+    levels = total // lev
+    span = total * STEP
+    pairs = wide // 2
+    left = left_half()
+    rem = slice(levels * STEP, (levels + 1) * STEP)
+    rem2 = slice((levels + 1) * STEP, (levels + 1) * STEP + STEP // 2)
+    half = high.shape[1]
+    waves = high.shape[0] // 2
+
+    def rows_of(lv, level):
+        start = (lv * levels + level) * STEP
+        return start, slice(start, start + STEP)
+
+    for lv in range(lev):
+        for level in range(levels):
+            rows = rows_of(lv, level)[1]
+            full = slice(level * STEP, (level + 1) * STEP)
+            ends[rows, 0:2] = got[lv, full, 0:2]
+            ends[rows, 2:4] = got[(wide - 1) * lev + lv, full, LANES - 2 : LANES]
+
+    def put(part, start, lanes, value):
+        for base, piece in zip((0, span), split(value)):
+            xs[part, base + start : base + start + value.shape[0], lanes] = piece
+
+    def gather(pair, carry):
+        weights = edge[:, :, at(pair * LANES, LANES, LANES)]
+        for lv in range(lev):
+            a, b = 2 * pair, 2 * pair + 1
+            low_a, low_b = a * lev + lv, b * lev + lv
+            top_a, top_b = (wide - 1 - a) * lev + lv, (wide - 1 - b) * lev + lv
+            for level in range(levels):
+                start = rows_of(lv, level)[0]
+                full = slice(level * STEP, (level + 1) * STEP)
+                for w, src, top in ((a, low_a, top_a), (b, low_b, top_b)):
+                    value, other = got[src, full], mirror(got[top, full])
+                    lanes = at(w * LANES, LANES, LANES)
+                    put(0, start, lanes, value + other)
+                    put(1, start, lanes, value - other)
+            turned = mirror(got[top_a, rem]), mirror(got[top_b, rem])
+            turned2 = swap(mirror(got[top_a, rem2])), swap(mirror(got[top_b, rem2]))
+            for part, sign in ((0, 1.0), (1, -1.0)):
+                fa, fb = got[low_a, rem] + sign * turned[0], got[low_b, rem] + sign * turned[1]
+                ga, gb = got[low_a, rem2] + sign * turned2[0], got[low_b, rem2] + sign * turned2[1]
+                values = (
+                    jnp.where(left, fa, fb),
+                    swap(jnp.where(left, fb, fa)),
+                    jnp.concatenate([jnp.where(left, ga, swap(gb)), jnp.where(left, swap(ga), gb)], axis=0),
+                )
+                for level, value in enumerate(values):
+                    start, rows = rows_of(lv, level)
+                    for i in range(4):
+                        value = value + ends[rows, i : i + 1] * weights[part, i : i + 1]
+                    put(part, start, at(pairs * LANES + pair * LANES, LANES, LANES), value)
+        return carry
+
+    lax.fori_loop(0, pairs // 2, gather, 0)
+
+    group = chunk * devices + me[0]
+    mine = lax.broadcasted_iota(jnp.int32, (1, LANES), 1) == group
+    lap_q, square_q, weight_q = (
+        jnp.sum(jnp.where(mine, own[i], 0.0), axis=1, keepdims=True) for i in range(3)
+    )
+
+    def solve(tile, carry):
+        where = at(tile * TILE, TILE, TILE)
+        part = tile // (waves // TILE)
+        across = ((1,), (1,))
+        both = dot(xs[part], high[where], across)
+        spec = both[:span] + (both[span:] + dot(xs[part, :span], low[where], across))
+        for piece in range(TILE // LANES):
+            lanes = slice(piece * LANES, (piece + 1) * LANES)
+            here = at(tile * TILE + piece * LANES, LANES, LANES)
+            lap = lap_q + line[0:1, here]
+            scale = jnp.where(square_q + line[1:2, here] < float(KT * KT), weight_q * line[2:3, here], 0.0)
+            parts = [spec[l * STEP : (l + 1) * STEP, lanes] for l in range(total)]
+            solved = []
+            for m in range(total):
+                mode = sum(to_modes[m, l] * parts[l] for l in range(total))
+                solved.append(mode * scale / (1.0 + depth[m] * lap))
+            for l in range(total):
+                mixed = sum(from_modes[l, m] * solved[m] for m in range(total))
+                for base, value in zip((0, span), split(mixed)):
+                    ms[base + l * STEP : base + (l + 1) * STEP, here] = value
+        return carry
+
+    lax.fori_loop(0, 2 * waves // TILE, solve, 0)
+
+    def back(start):
+        where = at(start, TILE, TILE)
+        down = ((1,), (0,))
+        sums = []
+        for part in range(2):
+            k = slice(part * waves, (part + 1) * waves)
+            both = dot(ms[:, k], high[k, where], down)
+            sums.append(both[:span] + (both[span:] + dot(ms[:span, k], low[k, where], down)))
+        return sums[0] + sums[1], sums[0] - sums[1]
+
+    def scatter(pair, carry):
+        values = back(pair * TILE)
+        for piece in range(2):
+            w = 2 * pair + piece
+            lanes = slice(piece * LANES, (piece + 1) * LANES)
+            for lv in range(lev):
+                for level in range(levels):
+                    rows = rows_of(lv, level)[1]
+                    full = slice(level * STEP, (level + 1) * STEP)
+                    out[w * lev + lv, full] = values[0][rows, lanes]
+                    out[(wide - 1 - w) * lev + lv, full] = mirror(values[1][rows, lanes])
+        return carry
+
+    lax.fori_loop(0, pairs // 2, scatter, 0)
+
+    for quad in range(pairs // 4):
+        values = back(pairs * LANES + quad * TILE)
+        for piece in range(2):
+            pair = 2 * quad + piece
+            lanes = slice(piece * LANES, (piece + 1) * LANES)
+            for lv in range(lev):
+                packs_of = []
+                for value in values:
+                    zero, one, two = (value[rows_of(lv, level)[1], lanes] for level in range(3))
+                    one = swap(one)
+                    cos, sin = two[: STEP // 2], two[STEP // 2 :]
+                    packs_of.append(
+                        (
+                            (jnp.where(left, zero, one), jnp.where(left, cos, swap(sin))),
+                            (jnp.where(left, one, zero), jnp.where(left, swap(cos), sin)),
+                        )
+                    )
+                for i in range(2):
+                    w = 2 * pair + i
+                    out[w * lev + lv, rem], out[w * lev + lv, rem2] = packs_of[0][i]
+                    top = (wide - 1 - w) * lev + lv
+                    out[top, rem], out[top, rem2] = mirror(packs_of[1][i][0]), swap(mirror(packs_of[1][i][1]))
+
+
+def inverse_x(chunk, place, got, *refs, more):
+    sources, refs = refs[:4], refs[4:]
+    prior, refs = (refs[0], refs[1:]) if more else (None, refs)
+    out, zs, rems, *tables, sems = refs
+    _, rows, cols = out.shape
+    waves, half = tables[0].shape
+    levels = 3
+    size = LANES + HALF
+    step = pl.program_id(0)
+    odd, upper = place[0], place[1]
+    rest = rows - LANES
+    fetches = [
+        pltpu.make_async_copy(source.at[pl.ds(chunk * waves, waves)], target, sems.at[i])
+        for i, (source, target) in enumerate(zip(sources, tables))
+    ]
+
+    def turn(start, part):
+        return got[:, pl.ds(start + part * 8, 8)].reshape(waves, LANES).T
+
+    @pl.when(step == 0)
+    def _():
+        for fetch in fetches:
+            fetch.start()
+        for part in range(2):
+            value = turn(levels * STEP, part)
+            for i in range(2):
+                rems[part, i] = value[i * HALF : (i + 1) * HALF]
+        last = got[:, (levels + 1) * STEP :].reshape(waves, LANES).T
+        for part in range(2):
+            rems[part, 2] = last[part * HALF : (part + 1) * HALF]
+
+    which = jnp.where(step == 2, 2, jnp.where(step == 0, odd, 1 - odd))
+    for part in range(2):
+        value = turn(pl.multiple_of(step * STEP, STEP), part)
+        for base, piece in zip((0, size), split(value)):
+            zs[part, base : base + LANES] = piece
+        for base, piece in zip((0, size), split(rems[part, which])):
+            zs[part, base + LANES : base + size] = piece
+
+    @pl.when(step == 0)
+    def _():
+        for fetch in fetches:
+            fetch.wait()
+
+    down = ((1,), (0,))
+    shift = HALF - rest
+
+    def store(lanes, value):
+        extra = value.shape[1]
+        full, tail = value[:LANES], value[LANES:]
+        tail = jnp.where(upper == 1, tail[shift:], tail[:rest])
+        for start, piece in ((rest * upper, full), (LANES * (1 - upper), tail)):
+            where = at(start, piece.shape[0], 8)
+            out[0, where, lanes] = piece + prior[0, where, lanes] if more else piece
+
+    for tile in range(half // TILE):
+        where = slice(tile * TILE, (tile + 1) * TILE)
+        sums = []
+        for part in range(2):
+            high, low = tables[2 * part], tables[2 * part + 1]
+            both = dot(zs[part], high[:, where], down)
+            sums.append(both[:size] + (both[size:] + dot(zs[part, :size], low[:, where], down)))
+        store(where, sums[0] + sums[1])
+        other = sums[0] - sums[1]
+        for piece in range(TILE // LANES):
+            start = 2 * half - tile * TILE - (piece + 1) * LANES
+            end = min(start + LANES, cols)
+            store(slice(start, end), mirror(other[:, piece * LANES : (piece + 1) * LANES])[:, : end - start])
+
+
+def packs(wide, lev, levels, rows, cols):
+    share = 2 * KT // (wide * lev)
+    return (
+        levels == 3
+        and wide % 8 == 0
+        and LANES < rows <= LANES + HALF
+        and rows % 8 == 0
+        and (LANES + HALF - rows) * wide == E
+        and cols % LANES == HALF == E
+        and (cols + E) % (2 * TILE) == 0
+        and (wide * lev * 8) % TILE == 0
+        and share % STEP == 0
+        and KT // 8 <= LANES
+    )
+
+
+def wave_seeds(doubled, length):
+    turn = np.pi / length
+    seeds = []
+    for waves in (np.arange(0, KT, STEP), np.arange(STEP)):
+        angle = turn * ((waves[:, None] * doubled[None, :]) % (2 * length))
+        seeds += [np.cos(angle), np.sin(angle)]
+    return [np.asarray(a, np.float32) for a in seeds]
+
+
+def packed(state, to_modes, from_modes, mode_depth):
+    wide, lev = lax.axis_size("wide"), lax.axis_size("lev")
+    levels, rows, cols = state.shape
+    devices = wide * lev
+    length = cols + E
+    half = length // 2
+    chunks = 2 * KT // (devices * STEP)
+    width = devices * 8
+    tail = rows - LANES
+    extra = E // wide
+    block = (levels + 1) * STEP + STEP // 2
+    total = lev * levels
+    f32, bf16 = jnp.float32, jnp.bfloat16
+
+    starts = np.arange(wide // 2)[:, None]
+    order = np.concatenate(
+        [
+            (starts * rows + np.arange(LANES)).reshape(-1),
+            np.concatenate(
+                [starts * rows + LANES + np.arange(tail), cols + starts * extra + np.arange(extra)], axis=1
+            ).reshape(-1),
+        ]
+    )
+    seeds_x = wave_seeds(2 * np.arange(half) + 1, length)
+    seeds_y = wave_seeds(2 * order - (cols - 1), length)
+    weights = edge_weights(E)
+    edge_x = np.concatenate([np.zeros((4, HALF), np.float32), weights], axis=1)
+    edge_y = np.zeros((2, 4, half), np.float32)
+    outside = order >= cols
+    ahead, behind = weights[:, order[outside] - cols], weights[:, E - 1 - (order[outside] - cols)]
+    edge_y[0][:, outside], edge_y[1][:, outside] = ahead + behind, ahead - behind
+    edge_y = edge_y[:, :, wide // 2 * LANES :]
+    waves = np.arange(KT)
+    lap = 4.0 * np.sin(np.pi * waves / length) ** 2
+    facts = np.stack([lap, waves * waves, np.where(waves == 0, 1.0, 2.0)]).astype(np.float32)
+    own = np.zeros((3, STEP, LANES), np.float32)
+    own[:, :, : KT // 8] = np.tile(facts.reshape(3, -1, 8).transpose(0, 2, 1), (1, 2, 1))
+    line = np.tile(facts, (1, 2))
+    line[2] /= length * length
+
+    wide_index = lax.axis_index("wide")
+    place = jnp.stack([lax.rem(wide_index, 2), (wide_index >= wide // 2).astype(jnp.int32)])
+    me = (wide_index * lev + lax.axis_index("lev")).reshape(1)
+    smem = pl.BlockSpec(memory_space=pltpu.SMEM)
+    vmem = pl.BlockSpec(memory_space=pltpu.VMEM)
+    anywhere = pl.BlockSpec(memory_space=pl.ANY)
+    table = (KT, half)
+
+    def params(mib):
+        return pltpu.CompilerParams(vmem_limit_bytes=mib << 20)
+
+    def whole(a):
+        return pl.BlockSpec(a.shape, lambda i: (0,) * a.ndim)
+
+    def cost(flops, size):
+        return pl.CostEstimate(flops=flops, bytes_accessed=size, transcendentals=0)
+
+    def hbm(a):
+        return pltpu.with_memory_space_constraint(a, pltpu.HBM)
+
+    def to_columns(chunk):
+        operands = [hbm(jnp.asarray(a)) for a in (edge_x, *seeds_x)]
+        size = LANES + HALF
+        return pl.pallas_call(
+            functools.partial(forward_x, chunk),
+            grid=(levels,),
+            in_specs=[smem, anywhere] + [whole(a) for a in operands],
+            out_specs=anywhere,
+            out_shape=jax.ShapeDtypeStruct((devices, block, LANES), f32),
+            scratch_shapes=[
+                *[pltpu.VMEM((width, half), bf16)] * 4,
+                *[pltpu.VMEM((2 * size, half), bf16)] * 2,
+                pltpu.VMEM(state.shape, f32),
+                pltpu.VMEM((devices, block, LANES), f32),
+                pltpu.SemaphoreType.DMA((levels,)),
+                pltpu.SemaphoreType.DMA((levels,)),
+            ],
+            compiler_params=params(LIMITS[0]),
+            cost_estimate=cost(12 * width * levels * size * half, 8 << 20),
+            name=f"forward_x_{chunk}",
+        )(place, hbm(state), *operands)
+
+    def all_tables(after):
+        operands = [hbm(jnp.asarray(a)) for a in (*seeds_x, *seeds_y)]
+        steps = KT // TILE
+        return pl.pallas_call(
+            make_tables,
+            grid=(steps,),
+            in_specs=[anywhere] + [whole(a) for a in operands],
+            out_specs=[pl.BlockSpec((TILE, half), lambda i: (i, 0))] * 4
+            + [pl.BlockSpec((2, TILE, half), lambda i: (0, i, 0))] * 2,
+            out_shape=[pltpu.HBM(table, bf16)] * 4 + [jax.ShapeDtypeStruct((2, *table), bf16)] * 2,
+            compiler_params=params(LIMITS[1]),
+            cost_estimate=cost(32 * KT * half, 8 << 20),
+            name="make_tables",
+        )(after, *operands)
+
+    def through(chunk, got, high, low):
+        operands = [got, high, low, *(jnp.asarray(a) for a in (edge_y, own, line))]
+        span = total * STEP
+        return pl.pallas_call(
+            functools.partial(middle, chunk, devices, wide=wide),
+            in_specs=[smem] * 4 + [vmem] * len(operands),
+            out_specs=vmem,
+            out_shape=jax.ShapeDtypeStruct(got.shape, f32),
+            scratch_shapes=[
+                pltpu.VMEM((2, 2 * span, half), bf16),
+                pltpu.VMEM((2 * span, 2 * KT), bf16),
+                pltpu.VMEM((span, LANES), f32),
+            ],
+            compiler_params=params(LIMITS[2]),
+            cost_estimate=cost(24 * span * KT * half, 6 << 20),
+            name=f"middle_{chunk}",
+        )(me, to_modes, from_modes, mode_depth, *operands)
+
+    def to_rows(chunk, got, tables, prior):
+        size = LANES + HALF
+        sums = pl.BlockSpec((1, rows, cols), lambda i: (i, 0, 0))
+        more = prior is not None
+        return pl.pallas_call(
+            functools.partial(inverse_x, chunk, more=more),
+            grid=(levels,),
+            in_specs=[smem, whole(got)] + [anywhere] * 4 + [sums] * more,
+            out_specs=sums,
+            out_shape=jax.ShapeDtypeStruct(state.shape, f32),
+            scratch_shapes=[
+                pltpu.VMEM((2, 2 * size, width), bf16),
+                pltpu.VMEM((2, levels, HALF, width), f32),
+                *[pltpu.VMEM((width, half), bf16)] * 4,
+                pltpu.SemaphoreType.DMA((4,)),
+            ],
+            compiler_params=params(LIMITS[3]),
+            cost_estimate=cost(12 * width * levels * size * half, 8 << 20),
+            name=f"inverse_x_{chunk}",
+        )(place, got, *map(hbm, tables), *([prior] if more else []))
+
+    def exchange(sent):
+        return lax.all_to_all(sent, AXES, 0, 0, tiled=True)
+
+    sent = [to_columns(chunk) for chunk in range(chunks)]
+    tables = all_tables(sent[-1])
+    high, low = (a.reshape(2 * KT, half) for a in tables[4:])
+    arrived = [exchange(part) for part in sent]
+    returned = [exchange(through(chunk, got, high, low)) for chunk, got in enumerate(arrived)]
+    value = None
+    for chunk, got in enumerate(returned):
+        value = to_rows(chunk, got, tables[:4], value)
+    return value
+
+
 def solution(mesh):
     placed = (P("lev", "wide", None), P(), P(), P())
+
+    def shards(state, *rest):
+        fits = packs(lax.axis_size("wide"), lax.axis_size("lev"), *state.shape)
+        return (packed if fits else plain)(state, *rest)
+
     return jax.shard_map(
-        plain, mesh=mesh, in_specs=placed, out_specs=P("lev", "wide", None), check_vma=False
+        shards, mesh=mesh, in_specs=placed, out_specs=P("lev", "wide", None), check_vma=False
     )

time: 216 us -> 149 us (0.69)
  blocking collectives: 64.4 us -> 0 us
  Pallas kernels: 0 us -> 46.6 us
  matrix products: 40.6 us -> 0 us
  local copies, waits for them, and re-layouts: 37.5 us -> 7.42 us
  waiting for transfers between devices: 59.7 us -> 75.8 us
  starting transfers between devices: 7.5 us -> 18.3 us
  other arithmetic: 4.95 us -> 0.07 us
    all_to_all x1 -> x0, blocking collectives: 64.4 us -> none  [plain(): lax.all_to_all(back.reshape(devices, share, levels * rows), AXES, 0, 0, t...]
    pallas_call x0 -> x7, Pallas kernels: none -> 46.6 us  [the longest x2 19 us: through(): pl.pallas_call(functools.partial(middle, chunk, devices, wide=wide), in_s...]
    dot_general x6 -> x0, matrix products: 40.6 us -> none  [the longest x1 12.1 us: plain(): jnp.einsum('qlr,qn->lrn', back, table[:, :I], precision=HIGH)]
    reshape x6 -> x0, local copies, waits for them, and re-layouts: 26.5 us -> none  [the longest x2 8.05 us: plain(): back = back.reshape(lev, levels, share, wide, rows).transpose(3, 0, 2, 1, 4)]
    all_to_all x1 -> x4, waiting for transfers between devices: 59.7 us -> 75.8 us  [exchange(): return lax.all_to_all(sent, AXES, 0, 0, tiled=True)]
    all_to_all x1 -> x4, starting transfers between devices: 7.5 us -> 18.3 us  [exchange(): return lax.all_to_all(sent, AXES, 0, 0, tiled=True)]
    transpose x1 -> x0, local copies, waits for them, and re-layouts: 5.67 us -> none  [plain(): spec = spec.reshape(wide, lev, share, levels, rows).transpose(1, 3, 2, 0, 4)]
    unnamed x32 -> x24, local copies, waits for them, and re-layouts: 2.73 us -> 7.42 us
  transfers between devices with their start and end apart: 1 -> 4, of which waited for: 1 -> 4; matrix products, arithmetic and copies ran while one was open for 0% -> 0% of each run, Pallas kernels for 0% -> 23%
where the time goes in v3:
time: 149 us; the launch traced here: 148 us
  waiting for transfers between devices  75.8 us (51%)
  Pallas kernels  46.6 us (31%)
  starting transfers between devices  18.3 us (12%)
  local copies, waits for them, and re-layouts  7.42 us (5%)
    all_to_all x4, waiting for transfers between devices, exchange(): return lax.all_to_all(sent, AXES, 0, 0, tiled=True)  75.8 us
    pallas_call x2, Pallas kernels, through(): pl.pallas_call(functools.partial(middle, chunk, devices, wide=wide), in_s...  19 us
    all_to_all x4, starting transfers between devices, exchange(): return lax.all_to_all(sent, AXES, 0, 0, tiled=True)  18.3 us
    pallas_call x2, Pallas kernels, to_columns(): pl.pallas_call(functools.partial(forward_x, chunk), grid=(levels,), in_sp...  13.4 us
    pallas_call x2, Pallas kernels, to_rows(): pl.pallas_call(functools.partial(inverse_x, chunk, more=more), grid=(leve...  10.6 us
    unnamed x24, local copies, waits for them, and re-layouts  7.42 us
    pallas_call x1, Pallas kernels, all_tables(): pl.pallas_call(make_tables, grid=(steps,), in_specs=[anywhere] + [whole(a...  3.66 us
  transfers between devices with their start and end apart: 4, of which 4 were waited for; matrix products, arithmetic and copies ran while one was open for 0% of the time, Pallas kernels for 23%

profile of v3, /device:TPU:0, one launch (start us, length us, event | category | flops | bytes accessed | tf_op | source)
XLA Modules:
  0.0 148.4 jit_solution(8339248761302952689)
XLA Ops:
  0.0 0.1 pad_add_fusion.place
  0.1 6.7 %forward_x_0.1 = f32[32,72,128]{2,1,0:T(8,128)} custom-call(s32[2]{0:T(128)S(1)} %pad_add_fusion.place, f32[3,184,1472]{2,1,0:T(8,128)} %x.3, f32[4,128]{1,0:T(4,128)} %constant.40.clone.edge, f32[32,768]{1,0:T(8,128)} %constant.41.clone.refs_0_, f32[32,768]{1,0:T(8,128)} %constant.42.clone.refs_1_, f32[16,768]{1,0:T(8,128)} %constant.43.clone.refs_2_, ...), custom_call_target="tpu_custom_call" | custom-call | flops 1358954496 | bytes 8388608 | tf_op jit(solution)/shard_map/forward_x_0/pallas_call | solution.py:538
  6.8 7.3 %all-to-all-start.2 = ((f32[32,72,128]{2,1,0:T(8,128)}), f32[32,72,128]{2,1,0:T(8,128)S(1)}, u32[]{:S(2)}, u32[]{:S(2)}) async-start(f32[32,72,128]{2,1,0:T(8,128)} %forward_x_0.1), calls=%async_computation.2 | async-start | bytes 2359296 | tf_op jit(solution)/shard_map/all_to_all | solution.py:612
  14.1 6.8 %forward_x_1.1.order = f32[32,72,128]{2,1,0:T(8,128)} custom-call(s32[2]{0:T(128)S(1)} %pad_add_fusion.place, f32[3,184,1472]{2,1,0:T(8,128)} %x.3, f32[4,128]{1,0:T(4,128)} %constant.40.clone.edge, f32[32,768]{1,0:T(8,128)} %constant.41.clone.refs_0_, f32[32,768]{1,0:T(8,128)} %constant.42.clone.refs_1_, f32[16,768]{1,0:T(8,128)} %constant.43.clone.refs_2_, ...), custom_call_target="tpu_custom_call" | custom-call | flops 1358954496 | bytes 8388608 | tf_op jit(solution)/shard_map/forward_x_1/pallas_call | solution.py:538
  20.9 22.3 %all-to-all-done.2.got = f32[32,72,128]{2,1,0:T(8,128)S(1)} async-done(((f32[32,72,128]{2,1,0:T(8,128)}), f32[32,72,128]{2,1,0:T(8,128)S(1)}, u32[]{:S(2)}, u32[]{:S(2)}) %all-to-all-start.2) | async-done | bytes 1179680 | tf_op jit(solution)/shard_map/all_to_all | solution.py:612
  43.1 3.6 %all-to-all-start = ((f32[32,72,128]{2,1,0:T(8,128)}), f32[32,72,128]{2,1,0:T(8,128)S(1)}, u32[]{:S(2)}, u32[]{:S(2)}) async-start(f32[32,72,128]{2,1,0:T(8,128)} %forward_x_1.1.order), calls=%async_computation | async-start | bytes 2359296 | tf_op jit(solution)/shard_map/all_to_all | solution.py:612
  46.8 0.0 copy-start.6
  46.8 0.0 copy-start.7
  46.8 0.0 copy-start.8
  46.8 0.0 copy-start.9
  46.8 0.0 copy-start.10
  46.8 0.0 copy-start.11
  46.8 3.7 %make_tables.1 = (bf16[512,768]{1,0:T(8,128)(2,1)}, bf16[512,768]{1,0:T(8,128)(2,1)}, bf16[512,768]{1,0:T(8,128)(2,1)}, bf16[512,768]{1,0:T(8,128)(2,1)}, bf16[2...) custom-call(f32[32,72,128]{2,1,0:T(8,128)} %forward_x_1.1.order, f32[32,768]{1,0:T(8,128)} %constant.41.clone.refs_0_, ...), custom_call_target="tpu_custom_call" | custom-call | flops 12582912 | bytes 8388608 | tf_op jit(solution)/shard_map/make_tables/pallas_call | solution.py:560
  50.5 0.0 copy-done.6
  50.5 0.0 copy-done.7
  50.5 0.0 copy-done.8
  50.5 0.0 copy-done.9
  50.5 0.0 copy-done.10
  50.5 0.0 copy-done.11
  50.5 9.5 %middle_0.1 = f32[32,72,128]{2,1,0:T(8,128)} custom-call(s32[1]{0:T(128)} %bitcast.2.me, f32[12,12]{1,0:T(8,128)S(1)} %copy-done.6, f32[12,12]{1,0:T(8,128)S(1)} %copy-done.7, f32[12]{0:T(128)S(1)} %copy-done.8, f32[32,72,128]{2,1,0:T(8,128)S(1)} %all-to-all-done.2.got, bf16[1024,768]{1,0:T(8,128)(2,1)S(1)} %bitcast.5, bf16[1024,768]{1,0:T(8,128)(2,1)S(1)} %bitcast.7, ...), custom_call_target="tpu_custom_call" | custom-call | flops 1811939328 | bytes 6291456 | tf_op jit(solution)/shard_map/middle_0/pallas_call | solution.py:575
  60.0 0.0 copy-start.2
  60.0 1.1 copy-done.2
  61.2 0.0 copy-start.4
  61.2 1.2 copy-done.4
  62.3 13.4 %all-to-all-done.got = f32[32,72,128]{2,1,0:T(8,128)S(1)} async-done(((f32[32,72,128]{2,1,0:T(8,128)}), f32[32,72,128]{2,1,0:T(8,128)S(1)}, u32[]{:S(2)}, u32[]{:S(2)}) %all-to-all-start) | async-done | bytes 1179680 | tf_op jit(solution)/shard_map/all_to_all | solution.py:612
  75.8 3.6 %all-to-all-start.3 = ((f32[32,72,128]{2,1,0:T(8,128)}), f32[32,72,128]{2,1,0:T(8,128)S(1)}, u32[]{:S(2)}, u32[]{:S(2)}) async-start(f32[32,72,128]{2,1,0:T(8,128)} %middle_0.1), calls=%async_computation.3 | async-start | bytes 2359296 | tf_op jit(solution)/shard_map/all_to_all | solution.py:612
  79.4 0.0 copy-start.3
  79.4 1.4 copy-done.3
  80.8 0.0 copy-start.5
  80.8 1.4 copy-done.5
  82.2 9.5 %middle_1.1 = f32[32,72,128]{2,1,0:T(8,128)} custom-call(s32[1]{0:T(128)} %bitcast.2.me, f32[12,12]{1,0:T(8,128)S(1)} %copy-done.6, f32[12,12]{1,0:T(8,128)S(1)} %copy-done.7, f32[12]{0:T(128)S(1)} %copy-done.8, f32[32,72,128]{2,1,0:T(8,128)S(1)} %all-to-all-done.got, bf16[1024,768]{1,0:T(8,128)(2,1)S(1)} %bitcast.6, bf16[1024,768]{1,0:T(8,128)(2,1)S(1)} %bitcast.8, ...), custom_call_target="tpu_custom_call" | custom-call | flops 1811939328 | bytes 6291456 | tf_op jit(solution)/shard_map/middle_1/pallas_call | solution.py:575
  91.7 16.7 %all-to-all-done.3.got = f32[32,72,128]{2,1,0:T(8,128)S(1)} async-done(((f32[32,72,128]{2,1,0:T(8,128)}), f32[32,72,128]{2,1,0:T(8,128)S(1)}, u32[]{:S(2)}, u32[]{:S(2)}) %all-to-all-start.3) | async-done | bytes 1179680 | tf_op jit(solution)/shard_map/all_to_all | solution.py:612
  108.4 0.0 copy-start
  108.4 1.0 copy-done
  109.4 3.7 %all-to-all-start.1 = ((f32[32,72,128]{2,1,0:T(8,128)}), f32[32,72,128]{2,1,0:T(8,128)}, u32[]{:S(2)}, u32[]{:S(2)}) async-start(f32[32,72,128]{2,1,0:T(8,128)} %middle_1.1), calls=%async_computation.1 | async-start | bytes 2359296 | tf_op jit(solution)/shard_map/all_to_all | solution.py:612
  113.1 0.0 copy-start.1
  113.2 1.3 copy-done.1
  114.4 4.4 %inverse_x_0.1.refs_4_ = f32[3,184,1472]{2,1,0:T(8,128)S(1)} custom-call(s32[2]{0:T(128)S(1)} %pad_add_fusion.place, f32[32,72,128]{2,1,0:T(8,128)S(1)} %copy-done.1, bf16[512,768]{1,0:T(8,128)(2,1)} %get-tuple-element.13.refs_0_, bf16[512,768]{1,0:T(8,128)(2,1)} %get-tuple-element.14.refs_1_, bf16[512,768]{1,0:T(8,128)(2,1)} %get-tuple-element.15.refs_2_, ...), custom_call_target="tpu_custom_call" | custom-call | flops 1358954496 | bytes 8388608 | tf_op jit(solution)/shard_map/inverse_x_0/pallas_call | solution.py:594
  118.8 23.4 %all-to-all-done.1.got = f32[32,72,128]{2,1,0:T(8,128)} async-done(((f32[32,72,128]{2,1,0:T(8,128)}), f32[32,72,128]{2,1,0:T(8,128)}, u32[]{:S(2)}, u32[]{:S(2)}) %all-to-all-start.1) | async-done | bytes 1179680 | tf_op jit(solution)/shard_map/all_to_all | solution.py:612
  142.1 6.2 %inverse_x_1.1 = f32[3,184,1472]{2,1,0:T(8,128)} custom-call(s32[2]{0:T(128)S(1)} %pad_add_fusion.place, f32[32,72,128]{2,1,0:T(8,128)} %all-to-all-done.1.got, bf16[512,768]{1,0:T(8,128)(2,1)} %get-tuple-element.13.refs_0_, bf16[512,768]{1,0:T(8,128)(2,1)} %get-tuple-element.14.refs_1_, bf16[512,768]{1,0:T(8,128)(2,1)} %get-tuple-element.15.refs_2_, ...), custom_call_target="tpu_custom_call" | custom-call | flops 1358954496 | bytes 8388608 | tf_op jit(solution)/shard_map/inverse_x_1/pallas_call | solution.py:594
Async XLA Ops:
  6.8 36.4 %all-to-all-start.2 = ((f32[32,72,128]{2,1,0:T(8,128)}), f32[32,72,128]{2,1,0:T(8,128)S(1)}, u32[]{:S(2)}, u32[]{:S(2)}) async-start(f32[32,72,128]{2,1,0:T(8,128)} %forward_x_0.1), calls=%async_computation.2 | async-start | bytes 2359296 | tf_op jit(solution)/shard_map/all_to_all | solution.py:612
  43.1 32.6 %all-to-all-start = ((f32[32,72,128]{2,1,0:T(8,128)}), f32[32,72,128]{2,1,0:T(8,128)S(1)}, u32[]{:S(2)}, u32[]{:S(2)}) async-start(f32[32,72,128]{2,1,0:T(8,128)} %forward_x_1.1.order), calls=%async_computation | async-start | bytes 2359296 | tf_op jit(solution)/shard_map/all_to_all | solution.py:612
  46.8 3.7 %copy-start.6 = (f32[12,12]{1,0:T(8,128)S(1)}, f32[12,12]{1,0:T(8,128)}, u32[]{:S(2)}) copy-start(f32[12,12]{1,0:T(8,128)} %to_modes.3) | copy-start | bytes 1732
  46.8 3.7 %copy-start.7 = (f32[12,12]{1,0:T(8,128)S(1)}, f32[12,12]{1,0:T(8,128)}, u32[]{:S(2)}) copy-start(f32[12,12]{1,0:T(8,128)} %from_modes.3) | copy-start | bytes 1732
  46.8 3.7 %copy-start.8 = (f32[12]{0:T(128)S(1)}, f32[12]{0:T(128)}, u32[]{:S(2)}) copy-start(f32[12]{0:T(128)} %depth.3) | copy-start | bytes 148
  46.8 3.7 %copy-start.9 = (f32[3,16,128]{2,1,0:T(8,128)S(1)}, f32[3,16,128]{2,1,0:T(8,128)}, u32[]{:S(2)}) copy-start(f32[3,16,128]{2,1,0:T(8,128)} %constant.50.clone.refs_3_) | copy-start | bytes 73732
  46.8 3.7 %copy-start.10 = (f32[3,1024]{1,0:T(4,128)S(1)}, f32[3,1024]{1,0:T(4,128)}, u32[]{:S(2)}) copy-start(f32[3,1024]{1,0:T(4,128)} %constant.51.clone.refs_4_) | copy-start | bytes 36868
  46.8 3.7 %copy-start.11 = (f32[2,4,256]{2,1,0:T(4,128)S(1)}, f32[2,4,256]{2,1,0:T(4,128)}, u32[]{:S(2)}) copy-start(f32[2,4,256]{2,1,0:T(4,128)} %constant.49.clone.refs_2_) | copy-start | bytes 24580
  60.0 1.1 copy-start.2
  61.2 1.2 copy-start.4
  75.8 32.6 %all-to-all-start.3 = ((f32[32,72,128]{2,1,0:T(8,128)}), f32[32,72,128]{2,1,0:T(8,128)S(1)}, u32[]{:S(2)}, u32[]{:S(2)}) async-start(f32[32,72,128]{2,1,0:T(8,128)} %middle_0.1), calls=%async_computation.3 | async-start | bytes 2359296 | tf_op jit(solution)/shard_map/all_to_all | solution.py:612
  79.4 1.4 copy-start.3
  80.8 1.4 copy-start.5
  108.4 1.0 copy-start
  109.4 32.7 %all-to-all-start.1 = ((f32[32,72,128]{2,1,0:T(8,128)}), f32[32,72,128]{2,1,0:T(8,128)}, u32[]{:S(2)}, u32[]{:S(2)}) async-start(f32[32,72,128]{2,1,0:T(8,128)} %middle_1.1), calls=%async_computation.1 | async-start | bytes 2359296 | tf_op jit(solution)/shard_map/all_to_all | solution.py:612
  113.1 1.3 copy-start.1

commit v4 on v3

--- a/solution.py
+++ b/solution.py
@@ -85,7 +85,7 @@
     return jnp.einsum("qlr,qn->lrn", back, table[:, :I], precision=HIGH) / (length * length)
 
 
-LIMITS = (16, 16, 10, 16)
+LIMITS = (16, 16, 20, 16)
 
 
 def split(value):
@@ -108,6 +108,36 @@
 def mirror(value):
     order = LANES - 1 - lax.broadcasted_iota(jnp.int32, value.shape, 1)
     return jnp.take_along_axis(value, order, axis=1)
+
+
+def empty_lanes(upper, rest):
+    lane = lax.broadcasted_iota(jnp.int32, (1, LANES), 1) + rest * upper
+    return lax.rem(lane, HALF) >= rest
+
+
+def dense_rows(rest):
+    lasting = STEP + STEP // 2
+    return lasting - lasting * (HALF - rest) // HALF, HALF - rest
+
+
+def fold_rows(read, write, empty, rest):
+    kept, gap = dense_rows(rest)
+    each = rest // gap
+    for j in range(kept):
+        moved = pltpu.roll(read(kept + j // each), rest - gap * (j % each), 1)
+        write(j, jnp.where(empty, moved, read(j)))
+
+
+def unfold_rows(read, write, empty, rest):
+    kept, gap = dense_rows(rest)
+    each = rest // gap
+    for i in range(kept // each):
+        back = 0.0
+        for j in range(i * each, (i + 1) * each):
+            value = read(j)
+            write(j, jnp.where(empty, 0.0, value))
+            back = back + pltpu.roll(jnp.where(empty, value, 0.0), LANES - rest + gap * (j % each), 1)
+        write(kept + i, back)
 
 
 def at(start, size, unit):
@@ -135,7 +165,7 @@
 
 
 def forward_x(chunk, place, x, edge, *refs):
-    seeds, (out, *tables, even, uneven, buffer, packed, in_sems, out_sems) = refs[:4], refs[4:]
+    seeds, (out, *tables, even, uneven, buffer, packed, in_sems) = refs[:4], refs[4:]
     levels, rows, cols = x.shape
     waves = tables[0].shape[0]
     groups = waves // 8
@@ -149,11 +179,7 @@
     def fetch(level):
         return pltpu.make_async_copy(x.at[level], buffer.at[level], in_sems.at[level])
 
-    def send(level):
-        first = level * STEP
-        count = STEP if level < levels - 1 else packed.shape[1] - first
-        piece = slice(first, first + count)
-        return pltpu.make_async_copy(packed.at[:, piece], out.at[:, piece], out_sems.at[level])
+    height = out.shape[0] // groups
 
     @pl.when(step == 0)
     def _():
@@ -207,9 +233,10 @@
                 spec = both[:size] + (both[size:] + dot(source[:size], low[...], across))
                 full = spec[:LANES].T
                 first = level * STEP + part * 8
-                packed[:, first : first + 8] = full.reshape(groups, 8, LANES)
+                for d in range(groups):
+                    out[d * height + first : d * height + first + 8] = full[d * 8 : d * 8 + 8]
                 if level < 2:
-                    first = levels * STEP + part * 8
+                    first = part * 8
                     if level == 0:
                         turned = jnp.concatenate([spec[LANES:], blank], axis=0).T
                         packed[:, first : first + 8] = turned.reshape(groups, 8, LANES)
@@ -221,23 +248,24 @@
                 else:
                     pieces = [spec[LANES:], blank] if part == 0 else [blank, spec[LANES:]]
                     turned = jnp.concatenate(pieces, axis=0).T.reshape(groups, 8, LANES)
-                    first = (levels + 1) * STEP
+                    first = STEP
                     if part == 0:
                         packed[:, first : first + 8] = turned
                     else:
                         packed[:, first : first + 8] = packed[:, first : first + 8] + turned
-            send(level).start()
 
     @pl.when(step == levels - 1)
     def _():
-        for level in range(levels):
-            send(level).wait()
+        def write(j, value):
+            out[pl.ds(levels * STEP + j, groups, stride=height)] = value
+
+        fold_rows(lambda j: packed[:, j], write, empty_lanes(upper, rest), rest)
 
 
 def middle(
-    chunk, devices, me, to_modes, from_modes, depth, got, *refs, wide
+    chunk, devices, me, to_modes, from_modes, depth, arrived, *refs, wide, tail
 ):
-    high, low, edge, own, line, out, xs, ms, ends = refs
+    high, low, edge, own, line, leaving, xs, ms, ends, got, out = refs
     count = got.shape[0]
     lev = count // wide
     total = to_modes.shape[0]
@@ -253,6 +281,21 @@
     def rows_of(lv, level):
         start = (lv * levels + level) * STEP
         return start, slice(start, start + STEP)
+
+    height = arrived.shape[0] // count
+    block_index = lax.broadcasted_iota(jnp.int32, (count, 1), 0)
+    empty = empty_lanes((block_index >= count // 2).astype(jnp.int32), tail)
+    fulls = levels * STEP
+    for d in range(count):
+        got[d, :fulls] = arrived[d * height : d * height + fulls]
+
+    def keep_row(j, value):
+        got[:, fulls + j] = value
+
+    def send_row(j, value):
+        leaving[pl.ds(fulls + j, count, stride=height)] = value
+
+    unfold_rows(lambda j: arrived[pl.ds(fulls + j, count, stride=height)], keep_row, empty, tail)
 
     for lv in range(lev):
         for level in range(levels):
@@ -376,11 +419,15 @@
                     top = (wide - 1 - w) * lev + lv
                     out[top, rem], out[top, rem2] = mirror(packs_of[1][i][0]), swap(mirror(packs_of[1][i][1]))
 
+    for d in range(count):
+        leaving[d * height : d * height + fulls] = out[d, :fulls]
+    fold_rows(lambda j: out[:, fulls + j], send_row, empty, tail)
+
 
 def inverse_x(chunk, place, got, *refs, more):
     sources, refs = refs[:4], refs[4:]
     prior, refs = (refs[0], refs[1:]) if more else (None, refs)
-    out, zs, rems, *tables, sems = refs
+    out, zs, rems, *tables, unpacked, sems = refs
     _, rows, cols = out.shape
     waves, half = tables[0].shape
     levels = 3
@@ -393,18 +440,29 @@
         for i, (source, target) in enumerate(zip(sources, tables))
     ]
 
+    groups = waves // 8
+    height = got.shape[0] // groups
+
     def turn(start, part):
-        return got[:, pl.ds(start + part * 8, 8)].reshape(waves, LANES).T
+        first = start + part * 8
+        return jnp.concatenate([got[pl.ds(first + d * height, 8)] for d in range(groups)], axis=0).T
 
     @pl.when(step == 0)
     def _():
         for fetch in fetches:
             fetch.start()
+
+        def keep_row(j, value):
+            unpacked[:, j] = value
+
+        unfold_rows(
+            lambda j: got[pl.ds(levels * STEP + j, groups, stride=height)], keep_row, empty_lanes(upper, rest), rest
+        )
         for part in range(2):
-            value = turn(levels * STEP, part)
+            value = unpacked[:, part * 8 : part * 8 + 8].reshape(waves, LANES).T
             for i in range(2):
                 rems[part, i] = value[i * HALF : (i + 1) * HALF]
-        last = got[:, (levels + 1) * STEP :].reshape(waves, LANES).T
+        last = unpacked[:, STEP:].reshape(waves, LANES).T
         for part in range(2):
             rems[part, 2] = last[part * HALF : (part + 1) * HALF]
 
@@ -459,6 +517,8 @@
         and (cols + E) % (2 * TILE) == 0
         and (wide * lev * 8) % TILE == 0
         and share % STEP == 0
+        and (STEP + STEP // 2) * (LANES + HALF - rows) % HALF == 0
+        and (rows - LANES) % (LANES + HALF - rows) == 0
         and KT // 8 <= LANES
     )
 
@@ -482,7 +542,7 @@
     width = devices * 8
     tail = rows - LANES
     extra = E // wide
-    block = (levels + 1) * STEP + STEP // 2
+    block = levels * STEP + dense_rows(tail)[0]
     total = lev * levels
     f32, bf16 = jnp.float32, jnp.bfloat16
 
@@ -539,14 +599,13 @@
             functools.partial(forward_x, chunk),
             grid=(levels,),
             in_specs=[smem, anywhere] + [whole(a) for a in operands],
-            out_specs=anywhere,
-            out_shape=jax.ShapeDtypeStruct((devices, block, LANES), f32),
+            out_specs=pl.BlockSpec((devices * block, LANES), lambda i: (0, 0)),
+            out_shape=jax.ShapeDtypeStruct((devices * block, LANES), f32),
             scratch_shapes=[
                 *[pltpu.VMEM((width, half), bf16)] * 4,
                 *[pltpu.VMEM((2 * size, half), bf16)] * 2,
                 pltpu.VMEM(state.shape, f32),
-                pltpu.VMEM((devices, block, LANES), f32),
-                pltpu.SemaphoreType.DMA((levels,)),
+                pltpu.VMEM((devices, STEP + STEP // 2, LANES), f32),
                 pltpu.SemaphoreType.DMA((levels,)),
             ],
             compiler_params=params(LIMITS[0]),
@@ -563,17 +622,17 @@
             in_specs=[anywhere] + [whole(a) for a in operands],
             out_specs=[pl.BlockSpec((TILE, half), lambda i: (i, 0))] * 4
             + [pl.BlockSpec((2, TILE, half), lambda i: (0, i, 0))] * 2,
-            out_shape=[pltpu.HBM(table, bf16)] * 4 + [jax.ShapeDtypeStruct((2, *table), bf16)] * 2,
+            out_shape=[pltpu.HBM(table, bf16)] * 4 + [pltpu.HBM((2, *table), bf16)] * 2,
             compiler_params=params(LIMITS[1]),
             cost_estimate=cost(32 * KT * half, 8 << 20),
             name="make_tables",
         )(after, *operands)
 
     def through(chunk, got, high, low):
-        operands = [got, high, low, *(jnp.asarray(a) for a in (edge_y, own, line))]
+        operands = [got, hbm(high), hbm(low), *(jnp.asarray(a) for a in (edge_y, own, line))]
         span = total * STEP
         return pl.pallas_call(
-            functools.partial(middle, chunk, devices, wide=wide),
+            functools.partial(middle, chunk, devices, wide=wide, tail=tail),
             in_specs=[smem] * 4 + [vmem] * len(operands),
             out_specs=vmem,
             out_shape=jax.ShapeDtypeStruct(got.shape, f32),
@@ -581,6 +640,7 @@
                 pltpu.VMEM((2, 2 * span, half), bf16),
                 pltpu.VMEM((2 * span, 2 * KT), bf16),
                 pltpu.VMEM((span, LANES), f32),
+                *[pltpu.VMEM((devices, (levels + 1) * STEP + STEP // 2, LANES), f32)] * 2,
             ],
             compiler_params=params(LIMITS[2]),
             cost_estimate=cost(24 * span * KT * half, 6 << 20),
@@ -596,20 +656,21 @@
             grid=(levels,),
             in_specs=[smem, whole(got)] + [anywhere] * 4 + [sums] * more,
             out_specs=sums,
-            out_shape=jax.ShapeDtypeStruct(state.shape, f32),
+            out_shape=pltpu.HBM(state.shape, f32) if not more else jax.ShapeDtypeStruct(state.shape, f32),
             scratch_shapes=[
                 pltpu.VMEM((2, 2 * size, width), bf16),
                 pltpu.VMEM((2, levels, HALF, width), f32),
                 *[pltpu.VMEM((width, half), bf16)] * 4,
+                pltpu.VMEM((devices, STEP + STEP // 2, LANES), f32),
                 pltpu.SemaphoreType.DMA((4,)),
             ],
             compiler_params=params(LIMITS[3]),
             cost_estimate=cost(12 * width * levels * size * half, 8 << 20),
             name=f"inverse_x_{chunk}",
-        )(place, got, *map(hbm, tables), *([prior] if more else []))
+        )(place, got, *map(hbm, tables), *([hbm(prior)] if more else []))
 
     def exchange(sent):
-        return lax.all_to_all(sent, AXES, 0, 0, tiled=True)
+        return lax.all_to_all(sent.reshape(-1, 1, LANES), AXES, 0, 0, tiled=True).reshape(sent.shape)
 
     sent = [to_columns(chunk) for chunk in range(chunks)]
     tables = all_tables(sent[-1])

time: 149 us -> 145 us (0.973)
  local copies, waits for them, and re-layouts: 7.42 us -> 0.04 us
  Pallas kernels: 46.6 us -> 53.3 us
  waiting for transfers between devices: 75.8 us -> 72.4 us
    unnamed x24 -> x12, local copies, waits for them, and re-layouts: 7.42 us -> 0.04 us
    all_to_all x4, waiting for transfers between devices: 75.8 us -> 72.4 us  [exchange(): lax.all_to_all(sent.reshape(-1, 1, LANES), AXES, 0, 0, tiled=True)]
    pallas_call x2, Pallas kernels: 19 us -> 22 us  [through(): pl.pallas_call(functools.partial(middle, chunk, devices, wide=wide, tail=...]
    pallas_call x2, Pallas kernels: 10.6 us -> 12.9 us  [to_rows(): pl.pallas_call(functools.partial(inverse_x, chunk, more=more), grid=(leve...]
  transfers between devices with their start and end apart: 4 -> 4, of which waited for: 4 -> 4; matrix products, arithmetic and copies ran while one was open for 0% -> 0% of each run, Pallas kernels for 23% -> 27%
where the time goes in v4:
time: 145 us; the launch traced here: 144 us
  waiting for transfers between devices  72.4 us (50%)
  Pallas kernels  53.3 us (37%)
  starting transfers between devices  18.4 us (13%)
    all_to_all x4, waiting for transfers between devices, exchange(): lax.all_to_all(sent.reshape(-1, 1, LANES), AXES, 0, 0, tiled=True)  72.4 us
    pallas_call x2, Pallas kernels, through(): pl.pallas_call(functools.partial(middle, chunk, devices, wide=wide, tail=...  22 us
    all_to_all x4, starting transfers between devices, exchange(): lax.all_to_all(sent.reshape(-1, 1, LANES), AXES, 0, 0, tiled=True)  18.4 us
    pallas_call x2, Pallas kernels, to_columns(): pl.pallas_call(functools.partial(forward_x, chunk), grid=(levels,), in_sp...  14.1 us
    pallas_call x2, Pallas kernels, to_rows(): pl.pallas_call(functools.partial(inverse_x, chunk, more=more), grid=(leve...  12.9 us
    pallas_call x1, Pallas kernels, all_tables(): pl.pallas_call(make_tables, grid=(steps,), in_specs=[anywhere] + [whole(a...  4.33 us
  transfers between devices with their start and end apart: 4, of which 4 were waited for; matrix products, arithmetic and copies ran while one was open for 0% of the time, Pallas kernels for 27%

profile of v4, /device:TPU:0, one launch (start us, length us, event | category | flops | bytes accessed | tf_op | source)
XLA Modules:
  0.0 144.5 jit_solution(3204442811260283025)
XLA Ops:
  0.0 0.1 pad_add_fusion.place
  0.1 7.0 %forward_x_0.1 = f32[2208,128]{1,0:T(8,128)} custom-call(s32[2]{0:T(128)S(1)} %pad_add_fusion.place, f32[3,184,1472]{2,1,0:T(8,128)} %x.3, f32[4,128]{1,0:T(4,128)} %constant.40.clone.edge, f32[32,768]{1,0:T(8,128)} %constant.41.clone.refs_0_, f32[32,768]{1,0:T(8,128)} %constant.42.clone.refs_1_, f32[16,768]{1,0:T(8,128)} %constant.43.clone.refs_2_, ...), custom_call_target="tpu_custom_call" | custom-call | flops 1358954496 | bytes 8388608 | tf_op jit(solution)/shard_map/forward_x_0/pallas_call | solution.py:598
  7.1 7.3 %all-to-all-start.2 = ((f32[2208,1,128]{2,1,0:T(1,128)}), f32[2208,1,128]{2,1,0:T(1,128)S(1)}, u32[]{:S(2)}, u32[]{:S(2)}) async-start(f32[2208,1,128]{2,1,0:T(1,128)} %bitcast.12), calls=%async_computation.2 | async-start | bytes 2260992 | tf_op jit(solution)/shard_map/all_to_all | solution.py:673
  14.5 7.1 %forward_x_1.1.order = f32[2208,128]{1,0:T(8,128)} custom-call(s32[2]{0:T(128)S(1)} %pad_add_fusion.place, f32[3,184,1472]{2,1,0:T(8,128)} %x.3, f32[4,128]{1,0:T(4,128)} %constant.40.clone.edge, f32[32,768]{1,0:T(8,128)} %constant.41.clone.refs_0_, f32[32,768]{1,0:T(8,128)} %constant.42.clone.refs_1_, f32[16,768]{1,0:T(8,128)} %constant.43.clone.refs_2_, ...), custom_call_target="tpu_custom_call" | custom-call | flops 1358954496 | bytes 8388608 | tf_op jit(solution)/shard_map/forward_x_1/pallas_call | solution.py:598
  21.6 20.9 %all-to-all-done.2 = f32[2208,1,128]{2,1,0:T(1,128)S(1)} async-done(((f32[2208,1,128]{2,1,0:T(1,128)}), f32[2208,1,128]{2,1,0:T(1,128)S(1)}, u32[]{:S(2)}, u32[]{:S(2)}) %all-to-all-start.2) | async-done | bytes 1130528 | tf_op jit(solution)/shard_map/all_to_all | solution.py:673
  42.4 3.6 %all-to-all-start = ((f32[2208,1,128]{2,1,0:T(1,128)}), f32[2208,1,128]{2,1,0:T(1,128)S(1)}, u32[]{:S(2)}, u32[]{:S(2)}) async-start(f32[2208,1,128]{2,1,0:T(1,128)} %bitcast.4), calls=%async_computation | async-start | bytes 2260992 | tf_op jit(solution)/shard_map/all_to_all | solution.py:673
  46.1 0.0 copy-start
  46.1 0.0 copy-start.1
  46.1 0.0 copy-start.2
  46.1 0.0 copy-start.3
  46.1 0.0 copy-start.4
  46.1 0.0 copy-start.5
  46.1 4.3 %make_tables.1 = (bf16[512,768]{1,0:T(8,128)(2,1)}, bf16[512,768]{1,0:T(8,128)(2,1)}, bf16[512,768]{1,0:T(8,128)(2,1)}, bf16[512,768]{1,0:T(8,128)(2,1)}, bf16[2...) custom-call(f32[2208,128]{1,0:T(8,128)} %forward_x_1.1.order, f32[32,768]{1,0:T(8,128)} %constant.41.clone.refs_0_, ...), custom_call_target="tpu_custom_call" | custom-call | flops 12582912 | bytes 8388608 | tf_op jit(solution)/shard_map/make_tables/pallas_call | solution.py:619
  50.5 0.0 copy-done
  50.5 0.0 copy-done.1
  50.5 0.0 copy-done.2
  50.5 0.0 copy-done.3
  50.5 0.0 copy-done.4
  50.5 0.0 copy-done.5
  50.5 11.0 %middle_0.1 = f32[2208,128]{1,0:T(8,128)} custom-call(s32[1]{0:T(128)} %bitcast.2.me, f32[12,12]{1,0:T(8,128)S(1)} %copy-done, f32[12,12]{1,0:T(8,128)S(1)} %copy-done.1, f32[12]{0:T(128)S(1)} %copy-done.2, f32[2208,128]{1,0:T(8,128)S(1)} %bitcast.24, bf16[1024,768]{1,0:T(8,128)(2,1)} %bitcast.25, bf16[1024,768]{1,0:T(8,128)(2,1)} %bitcast.27, ...), custom_call_target="tpu_custom_call" | custom-call | flops 1811939328 | bytes 6291456 | tf_op jit(solution)/shard_map/middle_0/pallas_call | solution.py:634
  61.5 12.5 %all-to-all-done = f32[2208,1,128]{2,1,0:T(1,128)S(1)} async-done(((f32[2208,1,128]{2,1,0:T(1,128)}), f32[2208,1,128]{2,1,0:T(1,128)S(1)}, u32[]{:S(2)}, u32[]{:S(2)}) %all-to-all-start) | async-done | bytes 1130528 | tf_op jit(solution)/shard_map/all_to_all | solution.py:673
  74.0 3.8 %all-to-all-start.3 = ((f32[2208,1,128]{2,1,0:T(1,128)}), f32[2208,1,128]{2,1,0:T(1,128)S(1)}, u32[]{:S(2)}, u32[]{:S(2)}) async-start(f32[2208,1,128]{2,1,0:T(1,128)} %bitcast.15), calls=%async_computation.3 | async-start | bytes 2260992 | tf_op jit(solution)/shard_map/all_to_all | solution.py:673
  77.8 11.0 %middle_1.1 = f32[2208,128]{1,0:T(8,128)} custom-call(s32[1]{0:T(128)} %bitcast.2.me, f32[12,12]{1,0:T(8,128)S(1)} %copy-done, f32[12,12]{1,0:T(8,128)S(1)} %copy-done.1, f32[12]{0:T(128)S(1)} %copy-done.2, f32[2208,128]{1,0:T(8,128)S(1)} %bitcast.23, bf16[1024,768]{1,0:T(8,128)(2,1)} %bitcast.26, bf16[1024,768]{1,0:T(8,128)(2,1)} %bitcast.28, ...), custom_call_target="tpu_custom_call" | custom-call | flops 1811939328 | bytes 6291456 | tf_op jit(solution)/shard_map/middle_1/pallas_call | solution.py:634
  88.8 16.8 %all-to-all-done.3 = f32[2208,1,128]{2,1,0:T(1,128)S(1)} async-done(((f32[2208,1,128]{2,1,0:T(1,128)}), f32[2208,1,128]{2,1,0:T(1,128)S(1)}, u32[]{:S(2)}, u32[]{:S(2)}) %all-to-all-start.3) | async-done | bytes 1130528 | tf_op jit(solution)/shard_map/all_to_all | solution.py:673
  105.6 3.6 %all-to-all-start.1 = ((f32[2208,1,128]{2,1,0:T(1,128)}), f32[2208,1,128]{2,1,0:T(1,128)S(1)}, u32[]{:S(2)}, u32[]{:S(2)}) async-start(f32[2208,1,128]{2,1,0:T(1,128)} %bitcast.9), calls=%async_computation.1 | async-start | bytes 2260992 | tf_op jit(solution)/shard_map/all_to_all | solution.py:673
  109.2 5.8 %inverse_x_0.1.refs_4_ = f32[3,184,1472]{2,1,0:T(8,128)} custom-call(s32[2]{0:T(128)S(1)} %pad_add_fusion.place, f32[2208,128]{1,0:T(8,128)S(1)} %bitcast.21, bf16[512,768]{1,0:T(8,128)(2,1)} %get-tuple-element.13.refs_0_, bf16[512,768]{1,0:T(8,128)(2,1)} %get-tuple-element.14.refs_1_, bf16[512,768]{1,0:T(8,128)(2,1)} %get-tuple-element.15.refs_2_, ...), custom_call_target="tpu_custom_call" | custom-call | flops 1358954496 | bytes 8388608 | tf_op jit(solution)/shard_map/inverse_x_0/pallas_call | solution.py:654
  115.0 22.2 %all-to-all-done.1 = f32[2208,1,128]{2,1,0:T(1,128)S(1)} async-done(((f32[2208,1,128]{2,1,0:T(1,128)}), f32[2208,1,128]{2,1,0:T(1,128)S(1)}, u32[]{:S(2)}, u32[]{:S(2)}) %all-to-all-start.1) | async-done | bytes 1130528 | tf_op jit(solution)/shard_map/all_to_all | solution.py:673
  137.2 7.1 %inverse_x_1.1 = f32[3,184,1472]{2,1,0:T(8,128)} custom-call(s32[2]{0:T(128)S(1)} %pad_add_fusion.place, f32[2208,128]{1,0:T(8,128)S(1)} %bitcast.22, bf16[512,768]{1,0:T(8,128)(2,1)} %get-tuple-element.13.refs_0_, bf16[512,768]{1,0:T(8,128)(2,1)} %get-tuple-element.14.refs_1_, bf16[512,768]{1,0:T(8,128)(2,1)} %get-tuple-element.15.refs_2_, ...), custom_call_target="tpu_custom_call" | custom-call | flops 1358954496 | bytes 8388608 | tf_op jit(solution)/shard_map/inverse_x_1/pallas_call | solution.py:654
Async XLA Ops:
  7.1 35.3 %all-to-all-start.2 = ((f32[2208,1,128]{2,1,0:T(1,128)}), f32[2208,1,128]{2,1,0:T(1,128)S(1)}, u32[]{:S(2)}, u32[]{:S(2)}) async-start(f32[2208,1,128]{2,1,0:T(1,128)} %bitcast.12), calls=%async_computation.2 | async-start | bytes 2260992 | tf_op jit(solution)/shard_map/all_to_all | solution.py:673
  42.4 31.6 %all-to-all-start = ((f32[2208,1,128]{2,1,0:T(1,128)}), f32[2208,1,128]{2,1,0:T(1,128)S(1)}, u32[]{:S(2)}, u32[]{:S(2)}) async-start(f32[2208,1,128]{2,1,0:T(1,128)} %bitcast.4), calls=%async_computation | async-start | bytes 2260992 | tf_op jit(solution)/shard_map/all_to_all | solution.py:673
  46.1 4.4 %copy-start = (f32[12,12]{1,0:T(8,128)S(1)}, f32[12,12]{1,0:T(8,128)}, u32[]{:S(2)}) copy-start(f32[12,12]{1,0:T(8,128)} %to_modes.3) | copy-start | bytes 1732
  46.1 4.4 %copy-start.1 = (f32[12,12]{1,0:T(8,128)S(1)}, f32[12,12]{1,0:T(8,128)}, u32[]{:S(2)}) copy-start(f32[12,12]{1,0:T(8,128)} %from_modes.3) | copy-start | bytes 1732
  46.1 4.4 %copy-start.2 = (f32[12]{0:T(128)S(1)}, f32[12]{0:T(128)}, u32[]{:S(2)}) copy-start(f32[12]{0:T(128)} %depth.3) | copy-start | bytes 148
  46.1 4.4 %copy-start.3 = (f32[3,16,128]{2,1,0:T(8,128)S(1)}, f32[3,16,128]{2,1,0:T(8,128)}, u32[]{:S(2)}) copy-start(f32[3,16,128]{2,1,0:T(8,128)} %constant.50.clone.refs_3_) | copy-start | bytes 73732
  46.1 4.4 %copy-start.4 = (f32[3,1024]{1,0:T(4,128)S(1)}, f32[3,1024]{1,0:T(4,128)}, u32[]{:S(2)}) copy-start(f32[3,1024]{1,0:T(4,128)} %constant.51.clone.refs_4_) | copy-start | bytes 36868
  46.1 4.4 %copy-start.5 = (f32[2,4,256]{2,1,0:T(4,128)S(1)}, f32[2,4,256]{2,1,0:T(4,128)}, u32[]{:S(2)}) copy-start(f32[2,4,256]{2,1,0:T(4,128)} %constant.49.clone.refs_2_) | copy-start | bytes 24580
  74.0 31.6 %all-to-all-start.3 = ((f32[2208,1,128]{2,1,0:T(1,128)}), f32[2208,1,128]{2,1,0:T(1,128)S(1)}, u32[]{:S(2)}, u32[]{:S(2)}) async-start(f32[2208,1,128]{2,1,0:T(1,128)} %bitcast.15), calls=%async_computation.3 | async-start | bytes 2260992 | tf_op jit(solution)/shard_map/all_to_all | solution.py:673
  105.6 31.6 %all-to-all-start.1 = ((f32[2208,1,128]{2,1,0:T(1,128)}), f32[2208,1,128]{2,1,0:T(1,128)S(1)}, u32[]{:S(2)}, u32[]{:S(2)}) async-start(f32[2208,1,128]{2,1,0:T(1,128)} %bitcast.9), calls=%async_computation.1 | async-start | bytes 2260992 | tf_op jit(solution)/shard_map/all_to_all | solution.py:673

commit v5 on v4

--- a/solution.py
+++ b/solution.py
@@ -171,7 +171,6 @@
     groups = waves // 8
     size = LANES + HALF
     half = tables[0].shape[1]
-    step = pl.program_id(0)
     odd, upper = place[0], place[1]
     rest = rows - LANES
     block = 32
@@ -181,85 +180,78 @@
 
     height = out.shape[0] // groups
 
-    @pl.when(step == 0)
-    def _():
-        for level in range(levels):
-            fetch(level).start()
-        fill_tables(seeds, chunk * (waves // STEP), *tables)
-
     for level in range(levels):
-
-        @pl.when(step == level)
-        def _():
-            fetch(level).wait()
-            for r in range(0, size, block):
-
-                def read(lanes):
-                    if r < LANES:
-                        return buffer[level, at(rest * upper + r, block, 8), lanes]
-                    first = r - LANES
-                    live = min(block, rest - first)
-                    low = buffer[level, LANES + first : LANES + first + live, lanes]
-                    if live < block:
-                        low = jnp.concatenate([low, jnp.zeros((block - live, low.shape[1]), low.dtype)], axis=0)
-                    shift = HALF - rest
-                    if first < shift:
-                        high = buffer[level, 0 : block - shift, lanes]
-                        high = jnp.concatenate([jnp.zeros((shift, high.shape[1]), high.dtype), high], axis=0)
-                    else:
-                        high = buffer[level, first - shift : first - shift + block, lanes]
-                    return jnp.where(upper == 1, high, low)
-
-                where = slice(r, r + block)
-                above = slice(size + r, size + r + block)
-                for tile in range(half // LANES):
-                    lanes = slice(tile * LANES, (tile + 1) * LANES)
-                    value = read(lanes)
-                    start = cols + HALF - (tile + 1) * LANES
-                    other = read(slice(start, min(start + LANES, cols)))
-                    if tile == 0:
-                        ends = (value[:, 0:1], value[:, 1:2], other[:, HALF - 2 : HALF - 1], other[:, HALF - 1 : HALF])
-                        other = jnp.concatenate([other, jnp.zeros_like(other)], axis=1)
-                        for i, end in enumerate(ends):
-                            other = other + end * edge[i : i + 1]
-                    other = mirror(other)
-                    even[where, lanes], even[above, lanes] = split(value + other)
-                    uneven[where, lanes], uneven[above, lanes] = split(value - other)
-
-            across = ((1,), (1,))
-            blank = jnp.zeros((HALF, waves), jnp.float32)
-            for part, (source, high, low) in enumerate(((even, *tables[:2]), (uneven, *tables[2:]))):
-                both = dot(source[...], high[...], across)
-                spec = both[:size] + (both[size:] + dot(source[:size], low[...], across))
-                full = spec[:LANES].T
-                first = level * STEP + part * 8
-                for d in range(groups):
-                    out[d * height + first : d * height + first + 8] = full[d * 8 : d * 8 + 8]
-                if level < 2:
-                    first = part * 8
-                    if level == 0:
-                        turned = jnp.concatenate([spec[LANES:], blank], axis=0).T
-                        packed[:, first : first + 8] = turned.reshape(groups, 8, LANES)
-                    else:
-                        turned = jnp.concatenate([blank, spec[LANES:]], axis=0).T
-                        value = packed[:, first : first + 8].reshape(waves, LANES) + turned
-                        value = jnp.where(odd == 1, swap(value), value)
-                        packed[:, first : first + 8] = value.reshape(groups, 8, LANES)
+        fetch(level).start()
+    fill_tables(seeds, chunk * (waves // STEP), *tables)
+
+    for level in range(levels):
+        fetch(level).wait()
+        for r in range(0, size, block):
+
+            def read(lanes):
+                if r < LANES:
+                    return buffer[level, at(rest * upper + r, block, 8), lanes]
+                first = r - LANES
+                live = min(block, rest - first)
+                low = buffer[level, LANES + first : LANES + first + live, lanes]
+                if live < block:
+                    low = jnp.concatenate([low, jnp.zeros((block - live, low.shape[1]), low.dtype)], axis=0)
+                shift = HALF - rest
+                if first < shift:
+                    high = buffer[level, 0 : block - shift, lanes]
+                    high = jnp.concatenate([jnp.zeros((shift, high.shape[1]), high.dtype), high], axis=0)
                 else:
-                    pieces = [spec[LANES:], blank] if part == 0 else [blank, spec[LANES:]]
-                    turned = jnp.concatenate(pieces, axis=0).T.reshape(groups, 8, LANES)
-                    first = STEP
-                    if part == 0:
-                        packed[:, first : first + 8] = turned
-                    else:
-                        packed[:, first : first + 8] = packed[:, first : first + 8] + turned
-
-    @pl.when(step == levels - 1)
-    def _():
-        def write(j, value):
-            out[pl.ds(levels * STEP + j, groups, stride=height)] = value
-
-        fold_rows(lambda j: packed[:, j], write, empty_lanes(upper, rest), rest)
+                    high = buffer[level, first - shift : first - shift + block, lanes]
+                return jnp.where(upper == 1, high, low)
+
+            where = slice(r, r + block)
+            above = slice(size + r, size + r + block)
+            for tile in range(half // LANES):
+                lanes = slice(tile * LANES, (tile + 1) * LANES)
+                value = read(lanes)
+                start = cols + HALF - (tile + 1) * LANES
+                other = read(slice(start, min(start + LANES, cols)))
+                if tile == 0:
+                    ends = (value[:, 0:1], value[:, 1:2], other[:, HALF - 2 : HALF - 1], other[:, HALF - 1 : HALF])
+                    other = jnp.concatenate([other, jnp.zeros_like(other)], axis=1)
+                    for i, end in enumerate(ends):
+                        other = other + end * edge[i : i + 1]
+                other = mirror(other)
+                even[where, lanes], even[above, lanes] = split(value + other)
+                uneven[where, lanes], uneven[above, lanes] = split(value - other)
+
+        across = ((1,), (1,))
+        blank = jnp.zeros((HALF, waves), jnp.float32)
+        for part, (source, high, low) in enumerate(((even, *tables[:2]), (uneven, *tables[2:]))):
+            both = dot(source[...], high[...], across)
+            spec = both[:size] + (both[size:] + dot(source[:size], low[...], across))
+            full = spec[:LANES].T
+            first = level * STEP + part * 8
+            for d in range(groups):
+                out[d * height + first : d * height + first + 8] = full[d * 8 : d * 8 + 8]
+            if level < 2:
+                first = part * 8
+                if level == 0:
+                    turned = jnp.concatenate([spec[LANES:], blank], axis=0).T
+                    packed[:, first : first + 8] = turned.reshape(groups, 8, LANES)
+                else:
+                    turned = jnp.concatenate([blank, spec[LANES:]], axis=0).T
+                    value = packed[:, first : first + 8].reshape(waves, LANES) + turned
+                    value = jnp.where(odd == 1, swap(value), value)
+                    packed[:, first : first + 8] = value.reshape(groups, 8, LANES)
+            else:
+                pieces = [spec[LANES:], blank] if part == 0 else [blank, spec[LANES:]]
+                turned = jnp.concatenate(pieces, axis=0).T.reshape(groups, 8, LANES)
+                first = STEP
+                if part == 0:
+                    packed[:, first : first + 8] = turned
+                else:
+                    packed[:, first : first + 8] = packed[:, first : first + 8] + turned
+
+    def write(j, value):
+        out[pl.ds(levels * STEP + j, groups, stride=height)] = value
+
+    fold_rows(lambda j: packed[:, j], write, empty_lanes(upper, rest), rest)
 
 
 def middle(
@@ -424,85 +416,94 @@
     fold_rows(lambda j: out[:, fulls + j], send_row, empty, tail)
 
 
-def inverse_x(chunk, place, got, *refs, more):
+def inverse_x(chunk, place, arrived, *refs, more):
     sources, refs = refs[:4], refs[4:]
     prior, refs = (refs[0], refs[1:]) if more else (None, refs)
-    out, zs, rems, *tables, unpacked, sems = refs
-    _, rows, cols = out.shape
+    final, got, out, zs, rems, *tables, unpacked, sems, sent_sems = refs
+    levels, rows, cols = out.shape
     waves, half = tables[0].shape
-    levels = 3
     size = LANES + HALF
-    step = pl.program_id(0)
     odd, upper = place[0], place[1]
     rest = rows - LANES
-    fetches = [
-        pltpu.make_async_copy(source.at[pl.ds(chunk * waves, waves)], target, sems.at[i])
-        for i, (source, target) in enumerate(zip(sources, tables))
-    ]
-
     groups = waves // 8
     height = got.shape[0] // groups
+
+    copies = [(arrived, got)]
+    copies += [(source.at[pl.ds(chunk * waves, waves)], target) for source, target in zip(sources, tables)]
+    copies += [(prior.at[level], out.at[level]) for level in range(levels)] if more else []
+    fetches = [pltpu.make_async_copy(*pair, sems.at[i]) for i, pair in enumerate(copies)]
+    for fetch in fetches:
+        fetch.start()
 
     def turn(start, part):
         first = start + part * 8
         return jnp.concatenate([got[pl.ds(first + d * height, 8)] for d in range(groups)], axis=0).T
 
-    @pl.when(step == 0)
-    def _():
-        for fetch in fetches:
-            fetch.start()
-
-        def keep_row(j, value):
-            unpacked[:, j] = value
-
-        unfold_rows(
-            lambda j: got[pl.ds(levels * STEP + j, groups, stride=height)], keep_row, empty_lanes(upper, rest), rest
-        )
-        for part in range(2):
-            value = unpacked[:, part * 8 : part * 8 + 8].reshape(waves, LANES).T
-            for i in range(2):
-                rems[part, i] = value[i * HALF : (i + 1) * HALF]
-        last = unpacked[:, STEP:].reshape(waves, LANES).T
-        for part in range(2):
-            rems[part, 2] = last[part * HALF : (part + 1) * HALF]
-
-    which = jnp.where(step == 2, 2, jnp.where(step == 0, odd, 1 - odd))
+    def keep_row(j, value):
+        unpacked[:, j] = value
+
+    fetches[0].wait()
+    unfold_rows(
+        lambda j: got[pl.ds(levels * STEP + j, groups, stride=height)], keep_row, empty_lanes(upper, rest), rest
+    )
+    last = unpacked[:, STEP:].reshape(waves, LANES).T
     for part in range(2):
-        value = turn(pl.multiple_of(step * STEP, STEP), part)
-        for base, piece in zip((0, size), split(value)):
-            zs[part, base : base + LANES] = piece
-        for base, piece in zip((0, size), split(rems[part, which])):
-            zs[part, base + LANES : base + size] = piece
-
-    @pl.when(step == 0)
-    def _():
-        for fetch in fetches:
-            fetch.wait()
+        value = unpacked[:, part * 8 : part * 8 + 8].reshape(waves, LANES).T
+        for i in range(2):
+            rems[part, i] = value[i * HALF : (i + 1) * HALF]
+        rems[part, 2] = last[part * HALF : (part + 1) * HALF]
 
     down = ((1,), (0,))
     shift = HALF - rest
-
-    def store(lanes, value):
-        extra = value.shape[1]
-        full, tail = value[:LANES], value[LANES:]
-        tail = jnp.where(upper == 1, tail[shift:], tail[:rest])
-        for start, piece in ((rest * upper, full), (LANES * (1 - upper), tail)):
-            where = at(start, piece.shape[0], 8)
-            out[0, where, lanes] = piece + prior[0, where, lanes] if more else piece
-
-    for tile in range(half // TILE):
-        where = slice(tile * TILE, (tile + 1) * TILE)
-        sums = []
+    sends = []
+
+    def send(level, lanes):
+        copy = pltpu.make_async_copy(out.at[level, :, lanes], final.at[level, :, lanes], sent_sems.at[len(sends)])
+        copy.start()
+        sends.append(copy)
+
+    for level in range(levels):
+        which = (odd, 1 - odd, 2)[level]
         for part in range(2):
-            high, low = tables[2 * part], tables[2 * part + 1]
-            both = dot(zs[part], high[:, where], down)
-            sums.append(both[:size] + (both[size:] + dot(zs[part, :size], low[:, where], down)))
-        store(where, sums[0] + sums[1])
-        other = sums[0] - sums[1]
-        for piece in range(TILE // LANES):
-            start = 2 * half - tile * TILE - (piece + 1) * LANES
-            end = min(start + LANES, cols)
-            store(slice(start, end), mirror(other[:, piece * LANES : (piece + 1) * LANES])[:, : end - start])
+            value = turn(level * STEP, part)
+            for base, piece in zip((0, size), split(value)):
+                zs[level, part, base : base + LANES] = piece
+            for base, piece in zip((0, size), split(rems[part, which])):
+                zs[level, part, base + LANES : base + size] = piece
+        if level == 0:
+            for fetch in fetches[1:5]:
+                fetch.wait()
+        if more:
+            fetches[5 + level].wait()
+
+        def store(lanes, value):
+            full, tail = value[:LANES], value[LANES:]
+            tail = jnp.where(upper == 1, tail[shift:], tail[:rest])
+            for start, piece in ((rest * upper, full), (LANES * (1 - upper), tail)):
+                where = at(start, piece.shape[0], 8)
+                out[level, where, lanes] = piece + out[level, where, lanes] if more else piece
+
+        for tile in range(half // TILE):
+            where = slice(tile * TILE, (tile + 1) * TILE)
+            sums = []
+            for part in range(2):
+                high, low = tables[2 * part], tables[2 * part + 1]
+                both = dot(zs[level, part], high[:, where], down)
+                sums.append(both[:size] + (both[size:] + dot(zs[level, part, :size], low[:, where], down)))
+            store(where, sums[0] + sums[1])
+            other = sums[0] - sums[1]
+            for piece in range(TILE // LANES):
+                start = 2 * half - tile * TILE - (piece + 1) * LANES
+                end = min(start + LANES, cols)
+                store(slice(start, end), mirror(other[:, piece * LANES : (piece + 1) * LANES])[:, : end - start])
+            if level == levels - 1:
+                send(level, pl.ds(tile * TILE, TILE))
+                start = 2 * half - (tile + 1) * TILE
+                send(level, pl.ds(start, min(start + TILE, cols) - start))
+        if level < levels - 1:
+            send(level, pl.ds(0, cols))
+    for copy in sends:
+        copy.wait()
 
 
 def packs(wide, lev, levels, rows, cols):
@@ -597,7 +598,7 @@
         size = LANES + HALF
         return pl.pallas_call(
             functools.partial(forward_x, chunk),
-            grid=(levels,),
+            grid=(1,),
             in_specs=[smem, anywhere] + [whole(a) for a in operands],
             out_specs=pl.BlockSpec((devices * block, LANES), lambda i: (0, 0)),
             out_shape=jax.ShapeDtypeStruct((devices * block, LANES), f32),
@@ -649,20 +650,21 @@
 
     def to_rows(chunk, got, tables, prior):
         size = LANES + HALF
-        sums = pl.BlockSpec((1, rows, cols), lambda i: (i, 0, 0))
         more = prior is not None
         return pl.pallas_call(
             functools.partial(inverse_x, chunk, more=more),
-            grid=(levels,),
-            in_specs=[smem, whole(got)] + [anywhere] * 4 + [sums] * more,
-            out_specs=sums,
-            out_shape=pltpu.HBM(state.shape, f32) if not more else jax.ShapeDtypeStruct(state.shape, f32),
+            in_specs=[smem] + [anywhere] * (5 + more),
+            out_specs=anywhere,
+            out_shape=jax.ShapeDtypeStruct(state.shape, f32) if more else pltpu.HBM(state.shape, f32),
             scratch_shapes=[
-                pltpu.VMEM((2, 2 * size, width), bf16),
+                pltpu.VMEM(got.shape, f32),
+                pltpu.VMEM(state.shape, f32),
+                pltpu.VMEM((levels, 2, 2 * size, width), bf16),
                 pltpu.VMEM((2, levels, HALF, width), f32),
                 *[pltpu.VMEM((width, half), bf16)] * 4,
                 pltpu.VMEM((devices, STEP + STEP // 2, LANES), f32),
-                pltpu.SemaphoreType.DMA((4,)),
+                pltpu.SemaphoreType.DMA((5 + levels,)),
+                pltpu.SemaphoreType.DMA((levels - 1 + 2 * (half // TILE),)),
             ],
             compiler_params=params(LIMITS[3]),
             cost_estimate=cost(12 * width * levels * size * half, 8 << 20),

time: 145 us -> 143 us (0.986)
  Pallas kernels: 53.3 us -> 50.6 us
    pallas_call x4, Pallas kernels: 27 us -> 24.3 us  [the longest x2 13.9 us: to_columns(): pl.pallas_call(functools.partial(forward_x, chunk), grid=(1,), in_specs=[...]
where the time goes in v5:
time: 143 us
  waiting for transfers between devices  73.4 us (51%)
  Pallas kernels  50.6 us (35%)
  starting transfers between devices  18.4 us (13%)
    all_to_all x4, waiting for transfers between devices, exchange(): lax.all_to_all(sent.reshape(-1, 1, LANES), AXES, 0, 0, tiled=True)  73.4 us
    pallas_call x2, Pallas kernels, through(): pl.pallas_call(functools.partial(middle, chunk, devices, wide=wide, tail=...  22 us
    all_to_all x4, starting transfers between devices, exchange(): lax.all_to_all(sent.reshape(-1, 1, LANES), AXES, 0, 0, tiled=True)  18.4 us
    pallas_call x2, Pallas kernels, to_columns(): pl.pallas_call(functools.partial(forward_x, chunk), grid=(1,), in_specs=[...  13.9 us
    pallas_call x2, Pallas kernels, to_rows(): pl.pallas_call(functools.partial(inverse_x, chunk, more=more), in_specs=[...  10.4 us
    pallas_call x1, Pallas kernels, all_tables(): pl.pallas_call(make_tables, grid=(steps,), in_specs=[anywhere] + [whole(a...  4.33 us
  transfers between devices with their start and end apart: 4, of which 4 were waited for; matrix products, arithmetic and copies ran while one was open for 0% of the time, Pallas kernels for 27%

profile of v5, /device:TPU:0, one launch (start us, length us, event | category | flops | bytes accessed | tf_op | source)
XLA Modules:
  0.0 142.8 jit_solution(15776386104519048259)
XLA Ops:
  0.0 0.1 pad_add_fusion.place
  0.1 7.0 %forward_x_0.1 = f32[2208,128]{1,0:T(8,128)} custom-call(s32[2]{0:T(128)S(1)} %pad_add_fusion.place, f32[3,184,1472]{2,1,0:T(8,128)} %x.3, f32[4,128]{1,0:T(4,128)} %constant.40.clone.edge, f32[32,768]{1,0:T(8,128)} %constant.41.clone.refs_0_, f32[32,768]{1,0:T(8,128)} %constant.42.clone.refs_1_, f32[16,768]{1,0:T(8,128)} %constant.43.clone.refs_2_, ...), custom_call_target="tpu_custom_call" | custom-call | flops 1358954496 | bytes 8388608 | tf_op jit(solution)/shard_map/forward_x_0/pallas_call | solution.py:599
  7.0 7.3 %all-to-all-start.2 = ((f32[2208,1,128]{2,1,0:T(1,128)}), f32[2208,1,128]{2,1,0:T(1,128)S(1)}, u32[]{:S(2)}, u32[]{:S(2)}) async-start(f32[2208,1,128]{2,1,0:T(1,128)} %bitcast.12), calls=%async_computation.2 | async-start | bytes 2260992 | tf_op jit(solution)/shard_map/all_to_all | solution.py:675
  14.4 7.0 %forward_x_1.1.order = f32[2208,128]{1,0:T(8,128)} custom-call(s32[2]{0:T(128)S(1)} %pad_add_fusion.place, f32[3,184,1472]{2,1,0:T(8,128)} %x.3, f32[4,128]{1,0:T(4,128)} %constant.40.clone.edge, f32[32,768]{1,0:T(8,128)} %constant.41.clone.refs_0_, f32[32,768]{1,0:T(8,128)} %constant.42.clone.refs_1_, f32[16,768]{1,0:T(8,128)} %constant.43.clone.refs_2_, ...), custom_call_target="tpu_custom_call" | custom-call | flops 1358954496 | bytes 8388608 | tf_op jit(solution)/shard_map/forward_x_1/pallas_call | solution.py:599
  21.4 21.0 %all-to-all-done.2 = f32[2208,1,128]{2,1,0:T(1,128)S(1)} async-done(((f32[2208,1,128]{2,1,0:T(1,128)}), f32[2208,1,128]{2,1,0:T(1,128)S(1)}, u32[]{:S(2)}, u32[]{:S(2)}) %all-to-all-start.2) | async-done | bytes 1130528 | tf_op jit(solution)/shard_map/all_to_all | solution.py:675
  42.4 3.6 %all-to-all-start = ((f32[2208,1,128]{2,1,0:T(1,128)}), f32[2208,1,128]{2,1,0:T(1,128)S(1)}, u32[]{:S(2)}, u32[]{:S(2)}) async-start(f32[2208,1,128]{2,1,0:T(1,128)} %bitcast.4), calls=%async_computation | async-start | bytes 2260992 | tf_op jit(solution)/shard_map/all_to_all | solution.py:675
  46.0 0.0 copy-start
  46.0 0.0 copy-start.1
  46.0 0.0 copy-start.2
  46.0 0.0 copy-start.3
  46.0 0.0 copy-start.4
  46.0 0.0 copy-start.5
  46.1 4.3 %make_tables.1 = (bf16[512,768]{1,0:T(8,128)(2,1)}, bf16[512,768]{1,0:T(8,128)(2,1)}, bf16[512,768]{1,0:T(8,128)(2,1)}, bf16[512,768]{1,0:T(8,128)(2,1)}, bf16[2...) custom-call(f32[2208,128]{1,0:T(8,128)} %forward_x_1.1.order, f32[32,768]{1,0:T(8,128)} %constant.41.clone.refs_0_, ...), custom_call_target="tpu_custom_call" | custom-call | flops 12582912 | bytes 8388608 | tf_op jit(solution)/shard_map/make_tables/pallas_call | solution.py:620
  50.4 0.0 copy-done
  50.4 0.0 copy-done.1
  50.4 0.0 copy-done.2
  50.4 0.0 copy-done.3
  50.4 0.0 copy-done.4
  50.4 0.0 copy-done.5
  50.5 11.0 %middle_0.1 = f32[2208,128]{1,0:T(8,128)} custom-call(s32[1]{0:T(128)} %bitcast.2.me, f32[12,12]{1,0:T(8,128)S(1)} %copy-done, f32[12,12]{1,0:T(8,128)S(1)} %copy-done.1, f32[12]{0:T(128)S(1)} %copy-done.2, f32[2208,128]{1,0:T(8,128)S(1)} %bitcast.24, bf16[1024,768]{1,0:T(8,128)(2,1)} %bitcast.25, bf16[1024,768]{1,0:T(8,128)(2,1)} %bitcast.27, ...), custom_call_target="tpu_custom_call" | custom-call | flops 1811939328 | bytes 6291456 | tf_op jit(solution)/shard_map/middle_0/pallas_call | solution.py:635
  61.5 12.5 %all-to-all-done = f32[2208,1,128]{2,1,0:T(1,128)S(1)} async-done(((f32[2208,1,128]{2,1,0:T(1,128)}), f32[2208,1,128]{2,1,0:T(1,128)S(1)}, u32[]{:S(2)}, u32[]{:S(2)}) %all-to-all-start) | async-done | bytes 1130528 | tf_op jit(solution)/shard_map/all_to_all | solution.py:675
  73.9 3.8 %all-to-all-start.3 = ((f32[2208,1,128]{2,1,0:T(1,128)}), f32[2208,1,128]{2,1,0:T(1,128)S(1)}, u32[]{:S(2)}, u32[]{:S(2)}) async-start(f32[2208,1,128]{2,1,0:T(1,128)} %bitcast.15), calls=%async_computation.3 | async-start | bytes 2260992 | tf_op jit(solution)/shard_map/all_to_all | solution.py:675
  77.7 11.0 %middle_1.1 = f32[2208,128]{1,0:T(8,128)} custom-call(s32[1]{0:T(128)} %bitcast.2.me, f32[12,12]{1,0:T(8,128)S(1)} %copy-done, f32[12,12]{1,0:T(8,128)S(1)} %copy-done.1, f32[12]{0:T(128)S(1)} %copy-done.2, f32[2208,128]{1,0:T(8,128)S(1)} %bitcast.23, bf16[1024,768]{1,0:T(8,128)(2,1)} %bitcast.26, bf16[1024,768]{1,0:T(8,128)(2,1)} %bitcast.28, ...), custom_call_target="tpu_custom_call" | custom-call | flops 1811939328 | bytes 6291456 | tf_op jit(solution)/shard_map/middle_1/pallas_call | solution.py:635
  88.7 16.8 %all-to-all-done.3 = f32[2208,1,128]{2,1,0:T(1,128)S(1)} async-done(((f32[2208,1,128]{2,1,0:T(1,128)}), f32[2208,1,128]{2,1,0:T(1,128)S(1)}, u32[]{:S(2)}, u32[]{:S(2)}) %all-to-all-start.3) | async-done | bytes 1130528 | tf_op jit(solution)/shard_map/all_to_all | solution.py:675
  105.5 3.6 %all-to-all-start.1 = ((f32[2208,1,128]{2,1,0:T(1,128)}), f32[2208,1,128]{2,1,0:T(1,128)S(1)}, u32[]{:S(2)}, u32[]{:S(2)}) async-start(f32[2208,1,128]{2,1,0:T(1,128)} %bitcast.9), calls=%async_computation.1 | async-start | bytes 2260992 | tf_op jit(solution)/shard_map/all_to_all | solution.py:675
  109.2 4.8 %inverse_x_0.1.refs_4_ = f32[3,184,1472]{2,1,0:T(8,128)} custom-call(s32[2]{0:T(128)S(1)} %pad_add_fusion.place, f32[2208,128]{1,0:T(8,128)S(1)} %bitcast.21, bf16[512,768]{1,0:T(8,128)(2,1)} %get-tuple-element.13.refs_0_, bf16[512,768]{1,0:T(8,128)(2,1)} %get-tuple-element.14.refs_1_, bf16[512,768]{1,0:T(8,128)(2,1)} %get-tuple-element.15.refs_2_, ...), custom_call_target="tpu_custom_call" | custom-call | flops 1358954496 | bytes 8388608 | tf_op jit(solution)/shard_map/inverse_x_0/pallas_call | solution.py:654
  114.0 23.2 %all-to-all-done.1 = f32[2208,1,128]{2,1,0:T(1,128)S(1)} async-done(((f32[2208,1,128]{2,1,0:T(1,128)}), f32[2208,1,128]{2,1,0:T(1,128)S(1)}, u32[]{:S(2)}, u32[]{:S(2)}) %all-to-all-start.1) | async-done | bytes 1130528 | tf_op jit(solution)/shard_map/all_to_all | solution.py:675
  137.1 5.6 %inverse_x_1.1 = f32[3,184,1472]{2,1,0:T(8,128)} custom-call(s32[2]{0:T(128)S(1)} %pad_add_fusion.place, f32[2208,128]{1,0:T(8,128)S(1)} %bitcast.22, bf16[512,768]{1,0:T(8,128)(2,1)} %get-tuple-element.13.refs_0_, bf16[512,768]{1,0:T(8,128)(2,1)} %get-tuple-element.14.refs_1_, bf16[512,768]{1,0:T(8,128)(2,1)} %get-tuple-element.15.refs_2_, ...), custom_call_target="tpu_custom_call" | custom-call | flops 1358954496 | bytes 8388608 | tf_op jit(solution)/shard_map/inverse_x_1/pallas_call | solution.py:654
Async XLA Ops:
  7.0 35.3 %all-to-all-start.2 = ((f32[2208,1,128]{2,1,0:T(1,128)}), f32[2208,1,128]{2,1,0:T(1,128)S(1)}, u32[]{:S(2)}, u32[]{:S(2)}) async-start(f32[2208,1,128]{2,1,0:T(1,128)} %bitcast.12), calls=%async_computation.2 | async-start | bytes 2260992 | tf_op jit(solution)/shard_map/all_to_all | solution.py:675
  42.4 31.6 %all-to-all-start = ((f32[2208,1,128]{2,1,0:T(1,128)}), f32[2208,1,128]{2,1,0:T(1,128)S(1)}, u32[]{:S(2)}, u32[]{:S(2)}) async-start(f32[2208,1,128]{2,1,0:T(1,128)} %bitcast.4), calls=%async_computation | async-start | bytes 2260992 | tf_op jit(solution)/shard_map/all_to_all | solution.py:675
  46.0 4.4 %copy-start = (f32[12,12]{1,0:T(8,128)S(1)}, f32[12,12]{1,0:T(8,128)}, u32[]{:S(2)}) copy-start(f32[12,12]{1,0:T(8,128)} %to_modes.3) | copy-start | bytes 1732
  46.0 4.4 %copy-start.1 = (f32[12,12]{1,0:T(8,128)S(1)}, f32[12,12]{1,0:T(8,128)}, u32[]{:S(2)}) copy-start(f32[12,12]{1,0:T(8,128)} %from_modes.3) | copy-start | bytes 1732
  46.0 4.4 %copy-start.2 = (f32[12]{0:T(128)S(1)}, f32[12]{0:T(128)}, u32[]{:S(2)}) copy-start(f32[12]{0:T(128)} %depth.3) | copy-start | bytes 148
  46.0 4.4 %copy-start.3 = (f32[3,16,128]{2,1,0:T(8,128)S(1)}, f32[3,16,128]{2,1,0:T(8,128)}, u32[]{:S(2)}) copy-start(f32[3,16,128]{2,1,0:T(8,128)} %constant.50.clone.refs_3_) | copy-start | bytes 73732
  46.0 4.4 %copy-start.4 = (f32[3,1024]{1,0:T(4,128)S(1)}, f32[3,1024]{1,0:T(4,128)}, u32[]{:S(2)}) copy-start(f32[3,1024]{1,0:T(4,128)} %constant.51.clone.refs_4_) | copy-start | bytes 36868
  46.0 4.4 %copy-start.5 = (f32[2,4,256]{2,1,0:T(4,128)S(1)}, f32[2,4,256]{2,1,0:T(4,128)}, u32[]{:S(2)}) copy-start(f32[2,4,256]{2,1,0:T(4,128)} %constant.49.clone.refs_2_) | copy-start | bytes 24580
  73.9 31.6 %all-to-all-start.3 = ((f32[2208,1,128]{2,1,0:T(1,128)}), f32[2208,1,128]{2,1,0:T(1,128)S(1)}, u32[]{:S(2)}, u32[]{:S(2)}) async-start(f32[2208,1,128]{2,1,0:T(1,128)} %bitcast.15), calls=%async_computation.3 | async-start | bytes 2260992 | tf_op jit(solution)/shard_map/all_to_all | solution.py:675
  105.5 31.6 %all-to-all-start.1 = ((f32[2208,1,128]{2,1,0:T(1,128)}), f32[2208,1,128]{2,1,0:T(1,128)S(1)}, u32[]{:S(2)}, u32[]{:S(2)}) async-start(f32[2208,1,128]{2,1,0:T(1,128)} %bitcast.9), calls=%async_computation.1 | async-start | bytes 2260992 | tf_op jit(solution)/shard_map/all_to_all | solution.py:675

commit v6 on v5

--- a/solution.py
+++ b/solution.py
@@ -110,6 +110,29 @@
     return jnp.take_along_axis(value, order, axis=1)
 
 
+def put_rows(ref, start, value):
+    height = ref.shape[0] * 8 // value.shape[0]
+    for d in range(value.shape[0] // 8):
+        ref[d * height + start : d * height + start + 8] = value[d * 8 : d * 8 + 8]
+
+
+def get_rows(ref, start, count):
+    height = ref.shape[0] // count
+    return jnp.concatenate([ref[pl.ds(start + d * height, 8)] for d in range(count)], axis=0)
+
+
+def strided(ref, start, count):
+    height = ref.shape[0] // count
+
+    def read(j):
+        return ref[pl.ds(start + j, count, stride=height)]
+
+    def write(j, value):
+        ref[pl.ds(start + j, count, stride=height)] = value
+
+    return read, write
+
+
 def empty_lanes(upper, rest):
     lane = lax.broadcasted_iota(jnp.int32, (1, LANES), 1) + rest * upper
     return lax.rem(lane, HALF) >= rest
@@ -164,8 +187,9 @@
     fill_tables(seeds_y, first, high.at[0], low.at[0], high.at[1], low.at[1])
 
 
-def forward_x(chunk, place, x, edge, *refs):
-    seeds, (out, *tables, even, uneven, buffer, packed, in_sems) = refs[:4], refs[4:]
+def forward_x(chunk, place, x, edge_in, *refs):
+    sources, (out, *tables, even, uneven, buffer, packed), rest_refs = refs[:4], refs[4:13], refs[13:]
+    edge, *seeds, in_sems, seed_sems = rest_refs
     levels, rows, cols = x.shape
     waves = tables[0].shape[0]
     groups = waves // 8
@@ -178,13 +202,19 @@
     def fetch(level):
         return pltpu.make_async_copy(x.at[level], buffer.at[level], in_sems.at[level])
 
-    height = out.shape[0] // groups
-
+    smalls = [
+        pltpu.make_async_copy(source, target, seed_sems.at[i])
+        for i, (source, target) in enumerate(zip((*sources, edge_in), (*seeds, edge)))
+    ]
+    for small in smalls:
+        small.start()
     for level in range(levels):
         fetch(level).start()
+    for small in smalls:
+        small.wait()
     fill_tables(seeds, chunk * (waves // STEP), *tables)
 
-    for level in range(levels):
+    def reflect(level):
         fetch(level).wait()
         for r in range(0, size, block):
 
@@ -217,41 +247,39 @@
                     for i, end in enumerate(ends):
                         other = other + end * edge[i : i + 1]
                 other = mirror(other)
-                even[where, lanes], even[above, lanes] = split(value + other)
-                uneven[where, lanes], uneven[above, lanes] = split(value - other)
-
+                even[level, where, lanes], even[level, above, lanes] = split(value + other)
+                uneven[level, where, lanes], uneven[level, above, lanes] = split(value - other)
+
+    def transform(level):
         across = ((1,), (1,))
         blank = jnp.zeros((HALF, waves), jnp.float32)
         for part, (source, high, low) in enumerate(((even, *tables[:2]), (uneven, *tables[2:]))):
-            both = dot(source[...], high[...], across)
-            spec = both[:size] + (both[size:] + dot(source[:size], low[...], across))
+            both = dot(source[level], high[...], across)
+            spec = both[:size] + (both[size:] + dot(source[level, :size], low[...], across))
             full = spec[:LANES].T
             first = level * STEP + part * 8
-            for d in range(groups):
-                out[d * height + first : d * height + first + 8] = full[d * 8 : d * 8 + 8]
+            put_rows(out, first, full)
             if level < 2:
                 first = part * 8
                 if level == 0:
-                    turned = jnp.concatenate([spec[LANES:], blank], axis=0).T
-                    packed[:, first : first + 8] = turned.reshape(groups, 8, LANES)
+                    put_rows(packed, first, jnp.concatenate([spec[LANES:], blank], axis=0).T)
                 else:
                     turned = jnp.concatenate([blank, spec[LANES:]], axis=0).T
-                    value = packed[:, first : first + 8].reshape(waves, LANES) + turned
-                    value = jnp.where(odd == 1, swap(value), value)
-                    packed[:, first : first + 8] = value.reshape(groups, 8, LANES)
+                    value = get_rows(packed, first, groups) + turned
+                    put_rows(packed, first, jnp.where(odd == 1, swap(value), value))
+            elif part == 0:
+                cosines = spec[LANES:]
             else:
-                pieces = [spec[LANES:], blank] if part == 0 else [blank, spec[LANES:]]
-                turned = jnp.concatenate(pieces, axis=0).T.reshape(groups, 8, LANES)
-                first = STEP
-                if part == 0:
-                    packed[:, first : first + 8] = turned
-                else:
-                    packed[:, first : first + 8] = packed[:, first : first + 8] + turned
-
-    def write(j, value):
-        out[pl.ds(levels * STEP + j, groups, stride=height)] = value
-
-    fold_rows(lambda j: packed[:, j], write, empty_lanes(upper, rest), rest)
+                put_rows(packed, STEP, jnp.concatenate([cosines, spec[LANES:]], axis=0).T)
+
+    reflect(0)
+    for level in range(levels):
+        if level + 1 < levels:
+            reflect(level + 1)
+        transform(level)
+    fold_rows(
+        strided(packed, 0, groups)[0], strided(out, levels * STEP, groups)[1], empty_lanes(upper, rest), rest
+    )
 
 
 def middle(
@@ -426,7 +454,6 @@
     odd, upper = place[0], place[1]
     rest = rows - LANES
     groups = waves // 8
-    height = got.shape[0] // groups
 
     copies = [(arrived, got)]
     copies += [(source.at[pl.ds(chunk * waves, waves)], target) for source, target in zip(sources, tables)]
@@ -435,20 +462,13 @@
     for fetch in fetches:
         fetch.start()
 
-    def turn(start, part):
-        first = start + part * 8
-        return jnp.concatenate([got[pl.ds(first + d * height, 8)] for d in range(groups)], axis=0).T
-
-    def keep_row(j, value):
-        unpacked[:, j] = value
-
     fetches[0].wait()
     unfold_rows(
-        lambda j: got[pl.ds(levels * STEP + j, groups, stride=height)], keep_row, empty_lanes(upper, rest), rest
+        strided(got, levels * STEP, groups)[0], strided(unpacked, 0, groups)[1], empty_lanes(upper, rest), rest
     )
-    last = unpacked[:, STEP:].reshape(waves, LANES).T
+    last = get_rows(unpacked, STEP, groups).T
     for part in range(2):
-        value = unpacked[:, part * 8 : part * 8 + 8].reshape(waves, LANES).T
+        value = get_rows(unpacked, part * 8, groups).T
         for i in range(2):
             rems[part, i] = value[i * HALF : (i + 1) * HALF]
         rems[part, 2] = last[part * HALF : (part + 1) * HALF]
@@ -465,7 +485,7 @@
     for level in range(levels):
         which = (odd, 1 - odd, 2)[level]
         for part in range(2):
-            value = turn(level * STEP, part)
+            value = get_rows(got, level * STEP + part * 8, groups).T
             for base, piece in zip((0, size), split(value)):
                 zs[level, part, base : base + LANES] = piece
             for base, piece in zip((0, size), split(rems[part, which])):
@@ -598,16 +618,17 @@
         size = LANES + HALF
         return pl.pallas_call(
             functools.partial(forward_x, chunk),
-            grid=(1,),
-            in_specs=[smem, anywhere] + [whole(a) for a in operands],
-            out_specs=pl.BlockSpec((devices * block, LANES), lambda i: (0, 0)),
+            in_specs=[smem] + [anywhere] * (1 + len(operands)),
+            out_specs=vmem,
             out_shape=jax.ShapeDtypeStruct((devices * block, LANES), f32),
             scratch_shapes=[
                 *[pltpu.VMEM((width, half), bf16)] * 4,
-                *[pltpu.VMEM((2 * size, half), bf16)] * 2,
+                *[pltpu.VMEM((levels, 2 * size, half), bf16)] * 2,
                 pltpu.VMEM(state.shape, f32),
-                pltpu.VMEM((devices, STEP + STEP // 2, LANES), f32),
+                pltpu.VMEM((devices * (STEP + STEP // 2), LANES), f32),
+                *[pltpu.VMEM(a.shape, f32) for a in operands],
                 pltpu.SemaphoreType.DMA((levels,)),
+                pltpu.SemaphoreType.DMA((len(operands),)),
             ],
             compiler_params=params(LIMITS[0]),
             cost_estimate=cost(12 * width * levels * size * half, 8 << 20),
@@ -662,7 +683,7 @@
                 pltpu.VMEM((levels, 2, 2 * size, width), bf16),
                 pltpu.VMEM((2, levels, HALF, width), f32),
                 *[pltpu.VMEM((width, half), bf16)] * 4,
-                pltpu.VMEM((devices, STEP + STEP // 2, LANES), f32),
+                pltpu.VMEM((devices * (STEP + STEP // 2), LANES), f32),
                 pltpu.SemaphoreType.DMA((5 + levels,)),
                 pltpu.SemaphoreType.DMA((levels - 1 + 2 * (half // TILE),)),
             ],

time: 143 us -> 143 us (level)
  no operation moved by 1% of the time
where the time goes in v6:
time: 143 us
  waiting for transfers between devices  73.7 us (52%)
  Pallas kernels  50 us (35%)
  starting transfers between devices  18.4 us (13%)
    all_to_all x4, waiting for transfers between devices, exchange(): lax.all_to_all(sent.reshape(-1, 1, LANES), AXES, 0, 0, tiled=True)  73.7 us
    pallas_call x2, Pallas kernels, through(): pl.pallas_call(functools.partial(middle, chunk, devices, wide=wide, tail=...  22 us
    all_to_all x4, starting transfers between devices, exchange(): lax.all_to_all(sent.reshape(-1, 1, LANES), AXES, 0, 0, tiled=True)  18.4 us
    pallas_call x2, Pallas kernels, to_columns(): pl.pallas_call(functools.partial(forward_x, chunk), in_specs=[smem] + [an...  13.3 us
    pallas_call x2, Pallas kernels, to_rows(): pl.pallas_call(functools.partial(inverse_x, chunk, more=more), in_specs=[...  10.4 us
    pallas_call x1, Pallas kernels, all_tables(): pl.pallas_call(make_tables, grid=(steps,), in_specs=[anywhere] + [whole(a...  4.33 us
  transfers between devices with their start and end apart: 4, of which 4 were waited for; matrix products, arithmetic and copies ran while one was open for 0% of the time, Pallas kernels for 27%

profile of v6, /device:TPU:0, one launch (start us, length us, event | category | flops | bytes accessed | tf_op | source)
XLA Modules:
  0.0 142.5 jit_solution(803668289954236480)
XLA Ops:
  0.0 0.1 pad_add_fusion.place
  0.1 6.7 %forward_x_0.1 = f32[2208,128]{1,0:T(8,128)} custom-call(s32[2]{0:T(128)S(1)} %pad_add_fusion.place, f32[3,184,1472]{2,1,0:T(8,128)} %x.3, f32[4,128]{1,0:T(4,128)} %constant.40.clone.edge_in, f32[32,768]{1,0:T(8,128)} %constant.41.clone.refs_0_, f32[32,768]{1,0:T(8,128)} %constant.42.clone.refs_1_, f32[16,768]{1,0:T(8,128)} %constant.43.clone.refs_2_, ...), custom_call_target="tpu_custom_call" | custom-call | flops 1358954496 | bytes 8388608 | tf_op jit(solution)/shard_map/forward_x_0/pallas_call | solution.py:619
  6.7 7.3 %all-to-all-start.2 = ((f32[2208,1,128]{2,1,0:T(1,128)}), f32[2208,1,128]{2,1,0:T(1,128)S(1)}, u32[]{:S(2)}, u32[]{:S(2)}) async-start(f32[2208,1,128]{2,1,0:T(1,128)} %bitcast.12), calls=%async_computation.2 | async-start | bytes 2260992 | tf_op jit(solution)/shard_map/all_to_all | solution.py:696
  14.1 6.7 %forward_x_1.1.order = f32[2208,128]{1,0:T(8,128)} custom-call(s32[2]{0:T(128)S(1)} %pad_add_fusion.place, f32[3,184,1472]{2,1,0:T(8,128)} %x.3, f32[4,128]{1,0:T(4,128)} %constant.40.clone.edge_in, f32[32,768]{1,0:T(8,128)} %constant.41.clone.refs_0_, f32[32,768]{1,0:T(8,128)} %constant.42.clone.refs_1_, f32[16,768]{1,0:T(8,128)} %constant.43.clone.refs_2_, ...), custom_call_target="tpu_custom_call" | custom-call | flops 1358954496 | bytes 8388608 | tf_op jit(solution)/shard_map/forward_x_1/pallas_call | solution.py:619
  20.7 21.3 %all-to-all-done.2 = f32[2208,1,128]{2,1,0:T(1,128)S(1)} async-done(((f32[2208,1,128]{2,1,0:T(1,128)}), f32[2208,1,128]{2,1,0:T(1,128)S(1)}, u32[]{:S(2)}, u32[]{:S(2)}) %all-to-all-start.2) | async-done | bytes 1130528 | tf_op jit(solution)/shard_map/all_to_all | solution.py:696
  42.0 3.6 %all-to-all-start = ((f32[2208,1,128]{2,1,0:T(1,128)}), f32[2208,1,128]{2,1,0:T(1,128)S(1)}, u32[]{:S(2)}, u32[]{:S(2)}) async-start(f32[2208,1,128]{2,1,0:T(1,128)} %bitcast.4), calls=%async_computation | async-start | bytes 2260992 | tf_op jit(solution)/shard_map/all_to_all | solution.py:696
  45.7 0.0 copy-start
  45.7 0.0 copy-start.1
  45.7 0.0 copy-start.2
  45.7 0.0 copy-start.3
  45.7 0.0 copy-start.4
  45.7 0.0 copy-start.5
  45.7 4.3 %make_tables.1 = (bf16[512,768]{1,0:T(8,128)(2,1)}, bf16[512,768]{1,0:T(8,128)(2,1)}, bf16[512,768]{1,0:T(8,128)(2,1)}, bf16[512,768]{1,0:T(8,128)(2,1)}, bf16[2...) custom-call(f32[2208,128]{1,0:T(8,128)} %forward_x_1.1.order, f32[32,768]{1,0:T(8,128)} %constant.41.clone.refs_0_, ...), custom_call_target="tpu_custom_call" | custom-call | flops 12582912 | bytes 8388608 | tf_op jit(solution)/shard_map/make_tables/pallas_call | solution.py:641
  50.1 0.0 copy-done
  50.1 0.0 copy-done.1
  50.1 0.0 copy-done.2
  50.1 0.0 copy-done.3
  50.1 0.0 copy-done.4
  50.1 0.0 copy-done.5
  50.1 11.0 %middle_0.1 = f32[2208,128]{1,0:T(8,128)} custom-call(s32[1]{0:T(128)} %bitcast.2.me, f32[12,12]{1,0:T(8,128)S(1)} %copy-done, f32[12,12]{1,0:T(8,128)S(1)} %copy-done.1, f32[12]{0:T(128)S(1)} %copy-done.2, f32[2208,128]{1,0:T(8,128)S(1)} %bitcast.24, bf16[1024,768]{1,0:T(8,128)(2,1)} %bitcast.25, bf16[1024,768]{1,0:T(8,128)(2,1)} %bitcast.27, ...), custom_call_target="tpu_custom_call" | custom-call | flops 1811939328 | bytes 6291456 | tf_op jit(solution)/shard_map/middle_0/pallas_call | solution.py:656
  61.1 12.5 %all-to-all-done = f32[2208,1,128]{2,1,0:T(1,128)S(1)} async-done(((f32[2208,1,128]{2,1,0:T(1,128)}), f32[2208,1,128]{2,1,0:T(1,128)S(1)}, u32[]{:S(2)}, u32[]{:S(2)}) %all-to-all-start) | async-done | bytes 1130528 | tf_op jit(solution)/shard_map/all_to_all | solution.py:696
  73.6 3.8 %all-to-all-start.3 = ((f32[2208,1,128]{2,1,0:T(1,128)}), f32[2208,1,128]{2,1,0:T(1,128)S(1)}, u32[]{:S(2)}, u32[]{:S(2)}) async-start(f32[2208,1,128]{2,1,0:T(1,128)} %bitcast.15), calls=%async_computation.3 | async-start | bytes 2260992 | tf_op jit(solution)/shard_map/all_to_all | solution.py:696
  77.4 11.0 %middle_1.1 = f32[2208,128]{1,0:T(8,128)} custom-call(s32[1]{0:T(128)} %bitcast.2.me, f32[12,12]{1,0:T(8,128)S(1)} %copy-done, f32[12,12]{1,0:T(8,128)S(1)} %copy-done.1, f32[12]{0:T(128)S(1)} %copy-done.2, f32[2208,128]{1,0:T(8,128)S(1)} %bitcast.23, bf16[1024,768]{1,0:T(8,128)(2,1)} %bitcast.26, bf16[1024,768]{1,0:T(8,128)(2,1)} %bitcast.28, ...), custom_call_target="tpu_custom_call" | custom-call | flops 1811939328 | bytes 6291456 | tf_op jit(solution)/shard_map/middle_1/pallas_call | solution.py:656
  88.4 16.8 %all-to-all-done.3 = f32[2208,1,128]{2,1,0:T(1,128)S(1)} async-done(((f32[2208,1,128]{2,1,0:T(1,128)}), f32[2208,1,128]{2,1,0:T(1,128)S(1)}, u32[]{:S(2)}, u32[]{:S(2)}) %all-to-all-start.3) | async-done | bytes 1130528 | tf_op jit(solution)/shard_map/all_to_all | solution.py:696
  105.2 3.6 %all-to-all-start.1 = ((f32[2208,1,128]{2,1,0:T(1,128)}), f32[2208,1,128]{2,1,0:T(1,128)S(1)}, u32[]{:S(2)}, u32[]{:S(2)}) async-start(f32[2208,1,128]{2,1,0:T(1,128)} %bitcast.9), calls=%async_computation.1 | async-start | bytes 2260992 | tf_op jit(solution)/shard_map/all_to_all | solution.py:696
  108.8 4.8 %inverse_x_0.1.refs_4_ = f32[3,184,1472]{2,1,0:T(8,128)} custom-call(s32[2]{0:T(128)S(1)} %pad_add_fusion.place, f32[2208,128]{1,0:T(8,128)S(1)} %bitcast.21, bf16[512,768]{1,0:T(8,128)(2,1)} %get-tuple-element.13.refs_0_, bf16[512,768]{1,0:T(8,128)(2,1)} %get-tuple-element.14.refs_1_, bf16[512,768]{1,0:T(8,128)(2,1)} %get-tuple-element.15.refs_2_, ...), custom_call_target="tpu_custom_call" | custom-call | flops 1358954496 | bytes 8388608 | tf_op jit(solution)/shard_map/inverse_x_0/pallas_call | solution.py:675
  113.6 23.2 %all-to-all-done.1 = f32[2208,1,128]{2,1,0:T(1,128)S(1)} async-done(((f32[2208,1,128]{2,1,0:T(1,128)}), f32[2208,1,128]{2,1,0:T(1,128)S(1)}, u32[]{:S(2)}, u32[]{:S(2)}) %all-to-all-start.1) | async-done | bytes 1130528 | tf_op jit(solution)/shard_map/all_to_all | solution.py:696
  136.8 5.6 %inverse_x_1.1 = f32[3,184,1472]{2,1,0:T(8,128)} custom-call(s32[2]{0:T(128)S(1)} %pad_add_fusion.place, f32[2208,128]{1,0:T(8,128)S(1)} %bitcast.22, bf16[512,768]{1,0:T(8,128)(2,1)} %get-tuple-element.13.refs_0_, bf16[512,768]{1,0:T(8,128)(2,1)} %get-tuple-element.14.refs_1_, bf16[512,768]{1,0:T(8,128)(2,1)} %get-tuple-element.15.refs_2_, ...), custom_call_target="tpu_custom_call" | custom-call | flops 1358954496 | bytes 8388608 | tf_op jit(solution)/shard_map/inverse_x_1/pallas_call | solution.py:675
Async XLA Ops:
  6.7 35.3 %all-to-all-start.2 = ((f32[2208,1,128]{2,1,0:T(1,128)}), f32[2208,1,128]{2,1,0:T(1,128)S(1)}, u32[]{:S(2)}, u32[]{:S(2)}) async-start(f32[2208,1,128]{2,1,0:T(1,128)} %bitcast.12), calls=%async_computation.2 | async-start | bytes 2260992 | tf_op jit(solution)/shard_map/all_to_all | solution.py:696
  42.0 31.6 %all-to-all-start = ((f32[2208,1,128]{2,1,0:T(1,128)}), f32[2208,1,128]{2,1,0:T(1,128)S(1)}, u32[]{:S(2)}, u32[]{:S(2)}) async-start(f32[2208,1,128]{2,1,0:T(1,128)} %bitcast.4), calls=%async_computation | async-start | bytes 2260992 | tf_op jit(solution)/shard_map/all_to_all | solution.py:696
  45.7 4.4 %copy-start = (f32[12,12]{1,0:T(8,128)S(1)}, f32[12,12]{1,0:T(8,128)}, u32[]{:S(2)}) copy-start(f32[12,12]{1,0:T(8,128)} %to_modes.3) | copy-start | bytes 1732
  45.7 4.4 %copy-start.1 = (f32[12,12]{1,0:T(8,128)S(1)}, f32[12,12]{1,0:T(8,128)}, u32[]{:S(2)}) copy-start(f32[12,12]{1,0:T(8,128)} %from_modes.3) | copy-start | bytes 1732
  45.7 4.4 %copy-start.2 = (f32[12]{0:T(128)S(1)}, f32[12]{0:T(128)}, u32[]{:S(2)}) copy-start(f32[12]{0:T(128)} %depth.3) | copy-start | bytes 148
  45.7 4.4 %copy-start.3 = (f32[3,16,128]{2,1,0:T(8,128)S(1)}, f32[3,16,128]{2,1,0:T(8,128)}, u32[]{:S(2)}) copy-start(f32[3,16,128]{2,1,0:T(8,128)} %constant.50.clone.refs_3_) | copy-start | bytes 73732
  45.7 4.4 %copy-start.4 = (f32[3,1024]{1,0:T(4,128)S(1)}, f32[3,1024]{1,0:T(4,128)}, u32[]{:S(2)}) copy-start(f32[3,1024]{1,0:T(4,128)} %constant.51.clone.refs_4_) | copy-start | bytes 36868
  45.7 4.4 %copy-start.5 = (f32[2,4,256]{2,1,0:T(4,128)S(1)}, f32[2,4,256]{2,1,0:T(4,128)}, u32[]{:S(2)}) copy-start(f32[2,4,256]{2,1,0:T(4,128)} %constant.49.clone.refs_2_) | copy-start | bytes 24580
  73.6 31.6 %all-to-all-start.3 = ((f32[2208,1,128]{2,1,0:T(1,128)}), f32[2208,1,128]{2,1,0:T(1,128)S(1)}, u32[]{:S(2)}, u32[]{:S(2)}) async-start(f32[2208,1,128]{2,1,0:T(1,128)} %bitcast.15), calls=%async_computation.3 | async-start | bytes 2260992 | tf_op jit(solution)/shard_map/all_to_all | solution.py:696
  105.2 31.6 %all-to-all-start.1 = ((f32[2208,1,128]{2,1,0:T(1,128)}), f32[2208,1,128]{2,1,0:T(1,128)S(1)}, u32[]{:S(2)}, u32[]{:S(2)}) async-start(f32[2208,1,128]{2,1,0:T(1,128)} %bitcast.9), calls=%async_computation.1 | async-start | bytes 2260992 | tf_op jit(solution)/shard_map/all_to_all | solution.py:696

commit v7 on v6

--- a/solution.py
+++ b/solution.py
@@ -444,10 +444,10 @@
     fold_rows(lambda j: out[:, fulls + j], send_row, empty, tail)
 
 
-def inverse_x(chunk, place, arrived, *refs, more):
+def inverse_x(chunk, place, got, *refs, more):
     sources, refs = refs[:4], refs[4:]
     prior, refs = (refs[0], refs[1:]) if more else (None, refs)
-    final, got, out, zs, rems, *tables, unpacked, sems, sent_sems = refs
+    final, out, zs, rems, *tables, unpacked, sems, sent_sems = refs
     levels, rows, cols = out.shape
     waves, half = tables[0].shape
     size = LANES + HALF
@@ -455,14 +455,12 @@
     rest = rows - LANES
     groups = waves // 8
 
-    copies = [(arrived, got)]
-    copies += [(source.at[pl.ds(chunk * waves, waves)], target) for source, target in zip(sources, tables)]
+    copies = [(source.at[pl.ds(chunk * waves, waves)], target) for source, target in zip(sources, tables)]
     copies += [(prior.at[level], out.at[level]) for level in range(levels)] if more else []
     fetches = [pltpu.make_async_copy(*pair, sems.at[i]) for i, pair in enumerate(copies)]
     for fetch in fetches:
         fetch.start()
 
-    fetches[0].wait()
     unfold_rows(
         strided(got, levels * STEP, groups)[0], strided(unpacked, 0, groups)[1], empty_lanes(upper, rest), rest
     )
@@ -491,10 +489,10 @@
             for base, piece in zip((0, size), split(rems[part, which])):
                 zs[level, part, base + LANES : base + size] = piece
         if level == 0:
-            for fetch in fetches[1:5]:
+            for fetch in fetches[:4]:
                 fetch.wait()
         if more:
-            fetches[5 + level].wait()
+            fetches[4 + level].wait()
 
         def store(lanes, value):
             full, tail = value[:LANES], value[LANES:]
@@ -674,17 +672,16 @@
         more = prior is not None
         return pl.pallas_call(
             functools.partial(inverse_x, chunk, more=more),
-            in_specs=[smem] + [anywhere] * (5 + more),
+            in_specs=[smem, vmem] + [anywhere] * (4 + more),
             out_specs=anywhere,
             out_shape=jax.ShapeDtypeStruct(state.shape, f32) if more else pltpu.HBM(state.shape, f32),
             scratch_shapes=[
-                pltpu.VMEM(got.shape, f32),
                 pltpu.VMEM(state.shape, f32),
                 pltpu.VMEM((levels, 2, 2 * size, width), bf16),
                 pltpu.VMEM((2, levels, HALF, width), f32),
                 *[pltpu.VMEM((width, half), bf16)] * 4,
                 pltpu.VMEM((devices * (STEP + STEP // 2), LANES), f32),
-                pltpu.SemaphoreType.DMA((5 + levels,)),
+                pltpu.SemaphoreType.DMA((4 + levels,)),
                 pltpu.SemaphoreType.DMA((levels - 1 + 2 * (half // TILE),)),
             ],
             compiler_params=params(LIMITS[3]),

time: 143 us -> 143 us (level)
  transfers between devices with their start and end apart: 4 -> 4, of which waited for: 4 -> 4; matrix products, arithmetic and copies ran while one was open for 0% -> 0% of each run, Pallas kernels for 27% -> 26%
where the time goes in v7:
time: 143 us; the launch traced here: 142 us
  waiting for transfers between devices  73.9 us (52%)
  Pallas kernels  49.8 us (35%)
  starting transfers between devices  18.4 us (13%)
    all_to_all x4, waiting for transfers between devices, exchange(): lax.all_to_all(sent.reshape(-1, 1, LANES), AXES, 0, 0, tiled=True)  73.9 us
    pallas_call x2, Pallas kernels, through(): pl.pallas_call(functools.partial(middle, chunk, devices, wide=wide, tail=...  22 us
    all_to_all x4, starting transfers between devices, exchange(): lax.all_to_all(sent.reshape(-1, 1, LANES), AXES, 0, 0, tiled=True)  18.4 us
    pallas_call x2, Pallas kernels, to_columns(): pl.pallas_call(functools.partial(forward_x, chunk), in_specs=[smem] + [an...  13.3 us
    pallas_call x2, Pallas kernels, to_rows(): pl.pallas_call(functools.partial(inverse_x, chunk, more=more), in_specs=[...  10.2 us
    pallas_call x1, Pallas kernels, all_tables(): pl.pallas_call(make_tables, grid=(steps,), in_specs=[anywhere] + [whole(a...  4.33 us
  transfers between devices with their start and end apart: 4, of which 4 were waited for; matrix products, arithmetic and copies ran while one was open for 0% of the time, Pallas kernels for 26%

profile of v7, /device:TPU:0, one launch (start us, length us, event | category | flops | bytes accessed | tf_op | source)
XLA Modules:
  0.0 142.5 jit_solution(2323707234103658744)
XLA Ops:
  0.0 0.1 pad_add_fusion.place
  0.1 6.7 %forward_x_0.1 = f32[2208,128]{1,0:T(8,128)} custom-call(s32[2]{0:T(128)S(1)} %pad_add_fusion.place, f32[3,184,1472]{2,1,0:T(8,128)} %x.3, f32[4,128]{1,0:T(4,128)} %constant.40.clone.edge_in, f32[32,768]{1,0:T(8,128)} %constant.41.clone.refs_0_, f32[32,768]{1,0:T(8,128)} %constant.42.clone.refs_1_, f32[16,768]{1,0:T(8,128)} %constant.43.clone.refs_2_, ...), custom_call_target="tpu_custom_call" | custom-call | flops 1358954496 | bytes 8388608 | tf_op jit(solution)/shard_map/forward_x_0/pallas_call | solution.py:617
  6.7 7.3 %all-to-all-start.2 = ((f32[2208,1,128]{2,1,0:T(1,128)}), f32[2208,1,128]{2,1,0:T(1,128)S(1)}, u32[]{:S(2)}, u32[]{:S(2)}) async-start(f32[2208,1,128]{2,1,0:T(1,128)} %bitcast.12), calls=%async_computation.2 | async-start | bytes 2260992 | tf_op jit(solution)/shard_map/all_to_all | solution.py:693
  14.1 6.7 %forward_x_1.1.order = f32[2208,128]{1,0:T(8,128)} custom-call(s32[2]{0:T(128)S(1)} %pad_add_fusion.place, f32[3,184,1472]{2,1,0:T(8,128)} %x.3, f32[4,128]{1,0:T(4,128)} %constant.40.clone.edge_in, f32[32,768]{1,0:T(8,128)} %constant.41.clone.refs_0_, f32[32,768]{1,0:T(8,128)} %constant.42.clone.refs_1_, f32[16,768]{1,0:T(8,128)} %constant.43.clone.refs_2_, ...), custom_call_target="tpu_custom_call" | custom-call | flops 1358954496 | bytes 8388608 | tf_op jit(solution)/shard_map/forward_x_1/pallas_call | solution.py:617
  20.7 21.3 %all-to-all-done.2 = f32[2208,1,128]{2,1,0:T(1,128)S(1)} async-done(((f32[2208,1,128]{2,1,0:T(1,128)}), f32[2208,1,128]{2,1,0:T(1,128)S(1)}, u32[]{:S(2)}, u32[]{:S(2)}) %all-to-all-start.2) | async-done | bytes 1130528 | tf_op jit(solution)/shard_map/all_to_all | solution.py:693
  42.0 3.6 %all-to-all-start = ((f32[2208,1,128]{2,1,0:T(1,128)}), f32[2208,1,128]{2,1,0:T(1,128)S(1)}, u32[]{:S(2)}, u32[]{:S(2)}) async-start(f32[2208,1,128]{2,1,0:T(1,128)} %bitcast.4), calls=%async_computation | async-start | bytes 2260992 | tf_op jit(solution)/shard_map/all_to_all | solution.py:693
  45.7 0.0 copy-start
  45.7 0.0 copy-start.1
  45.7 0.0 copy-start.2
  45.7 0.0 copy-start.3
  45.7 0.0 copy-start.4
  45.7 0.0 copy-start.5
  45.7 4.3 %make_tables.1 = (bf16[512,768]{1,0:T(8,128)(2,1)}, bf16[512,768]{1,0:T(8,128)(2,1)}, bf16[512,768]{1,0:T(8,128)(2,1)}, bf16[512,768]{1,0:T(8,128)(2,1)}, bf16[2...) custom-call(f32[2208,128]{1,0:T(8,128)} %forward_x_1.1.order, f32[32,768]{1,0:T(8,128)} %constant.41.clone.refs_0_, ...), custom_call_target="tpu_custom_call" | custom-call | flops 12582912 | bytes 8388608 | tf_op jit(solution)/shard_map/make_tables/pallas_call | solution.py:639
  50.1 0.0 copy-done
  50.1 0.0 copy-done.1
  50.1 0.0 copy-done.2
  50.1 0.0 copy-done.3
  50.1 0.0 copy-done.4
  50.1 0.0 copy-done.5
  50.1 11.0 %middle_0.1 = f32[2208,128]{1,0:T(8,128)} custom-call(s32[1]{0:T(128)} %bitcast.2.me, f32[12,12]{1,0:T(8,128)S(1)} %copy-done, f32[12,12]{1,0:T(8,128)S(1)} %copy-done.1, f32[12]{0:T(128)S(1)} %copy-done.2, f32[2208,128]{1,0:T(8,128)S(1)} %bitcast.24, bf16[1024,768]{1,0:T(8,128)(2,1)} %bitcast.25, bf16[1024,768]{1,0:T(8,128)(2,1)} %bitcast.27, ...), custom_call_target="tpu_custom_call" | custom-call | flops 1811939328 | bytes 6291456 | tf_op jit(solution)/shard_map/middle_0/pallas_call | solution.py:654
  61.1 12.5 %all-to-all-done = f32[2208,1,128]{2,1,0:T(1,128)S(1)} async-done(((f32[2208,1,128]{2,1,0:T(1,128)}), f32[2208,1,128]{2,1,0:T(1,128)S(1)}, u32[]{:S(2)}, u32[]{:S(2)}) %all-to-all-start) | async-done | bytes 1130528 | tf_op jit(solution)/shard_map/all_to_all | solution.py:693
  73.6 3.8 %all-to-all-start.3 = ((f32[2208,1,128]{2,1,0:T(1,128)}), f32[2208,1,128]{2,1,0:T(1,128)S(1)}, u32[]{:S(2)}, u32[]{:S(2)}) async-start(f32[2208,1,128]{2,1,0:T(1,128)} %bitcast.15), calls=%async_computation.3 | async-start | bytes 2260992 | tf_op jit(solution)/shard_map/all_to_all | solution.py:693
  77.4 11.0 %middle_1.1 = f32[2208,128]{1,0:T(8,128)} custom-call(s32[1]{0:T(128)} %bitcast.2.me, f32[12,12]{1,0:T(8,128)S(1)} %copy-done, f32[12,12]{1,0:T(8,128)S(1)} %copy-done.1, f32[12]{0:T(128)S(1)} %copy-done.2, f32[2208,128]{1,0:T(8,128)S(1)} %bitcast.23, bf16[1024,768]{1,0:T(8,128)(2,1)} %bitcast.26, bf16[1024,768]{1,0:T(8,128)(2,1)} %bitcast.28, ...), custom_call_target="tpu_custom_call" | custom-call | flops 1811939328 | bytes 6291456 | tf_op jit(solution)/shard_map/middle_1/pallas_call | solution.py:654
  88.4 16.8 %all-to-all-done.3 = f32[2208,1,128]{2,1,0:T(1,128)S(1)} async-done(((f32[2208,1,128]{2,1,0:T(1,128)}), f32[2208,1,128]{2,1,0:T(1,128)S(1)}, u32[]{:S(2)}, u32[]{:S(2)}) %all-to-all-start.3) | async-done | bytes 1130528 | tf_op jit(solution)/shard_map/all_to_all | solution.py:693
  105.2 3.6 %all-to-all-start.1 = ((f32[2208,1,128]{2,1,0:T(1,128)}), f32[2208,1,128]{2,1,0:T(1,128)S(1)}, u32[]{:S(2)}, u32[]{:S(2)}) async-start(f32[2208,1,128]{2,1,0:T(1,128)} %bitcast.9), calls=%async_computation.1 | async-start | bytes 2260992 | tf_op jit(solution)/shard_map/all_to_all | solution.py:693
  108.8 4.6 %inverse_x_0.1.refs_4_ = f32[3,184,1472]{2,1,0:T(8,128)} custom-call(s32[2]{0:T(128)S(1)} %pad_add_fusion.place, f32[2208,128]{1,0:T(8,128)S(1)} %bitcast.21, bf16[512,768]{1,0:T(8,128)(2,1)} %get-tuple-element.13.refs_0_, bf16[512,768]{1,0:T(8,128)(2,1)} %get-tuple-element.14.refs_1_, bf16[512,768]{1,0:T(8,128)(2,1)} %get-tuple-element.15.refs_2_, ...), custom_call_target="tpu_custom_call" | custom-call | flops 1358954496 | bytes 8388608 | tf_op jit(solution)/shard_map/inverse_x_0/pallas_call | solution.py:673
  113.5 23.3 %all-to-all-done.1 = f32[2208,1,128]{2,1,0:T(1,128)S(1)} async-done(((f32[2208,1,128]{2,1,0:T(1,128)}), f32[2208,1,128]{2,1,0:T(1,128)S(1)}, u32[]{:S(2)}, u32[]{:S(2)}) %all-to-all-start.1) | async-done | bytes 1130528 | tf_op jit(solution)/shard_map/all_to_all | solution.py:693
  136.8 5.5 %inverse_x_1.1 = f32[3,184,1472]{2,1,0:T(8,128)} custom-call(s32[2]{0:T(128)S(1)} %pad_add_fusion.place, f32[2208,128]{1,0:T(8,128)S(1)} %bitcast.22, bf16[512,768]{1,0:T(8,128)(2,1)} %get-tuple-element.13.refs_0_, bf16[512,768]{1,0:T(8,128)(2,1)} %get-tuple-element.14.refs_1_, bf16[512,768]{1,0:T(8,128)(2,1)} %get-tuple-element.15.refs_2_, ...), custom_call_target="tpu_custom_call" | custom-call | flops 1358954496 | bytes 8388608 | tf_op jit(solution)/shard_map/inverse_x_1/pallas_call | solution.py:673
Async XLA Ops:
  6.7 35.3 %all-to-all-start.2 = ((f32[2208,1,128]{2,1,0:T(1,128)}), f32[2208,1,128]{2,1,0:T(1,128)S(1)}, u32[]{:S(2)}, u32[]{:S(2)}) async-start(f32[2208,1,128]{2,1,0:T(1,128)} %bitcast.12), calls=%async_computation.2 | async-start | bytes 2260992 | tf_op jit(solution)/shard_map/all_to_all | solution.py:693
  42.0 31.6 %all-to-all-start = ((f32[2208,1,128]{2,1,0:T(1,128)}), f32[2208,1,128]{2,1,0:T(1,128)S(1)}, u32[]{:S(2)}, u32[]{:S(2)}) async-start(f32[2208,1,128]{2,1,0:T(1,128)} %bitcast.4), calls=%async_computation | async-start | bytes 2260992 | tf_op jit(solution)/shard_map/all_to_all | solution.py:693
  45.7 4.4 %copy-start = (f32[12,12]{1,0:T(8,128)S(1)}, f32[12,12]{1,0:T(8,128)}, u32[]{:S(2)}) copy-start(f32[12,12]{1,0:T(8,128)} %to_modes.3) | copy-start | bytes 1732
  45.7 4.4 %copy-start.1 = (f32[12,12]{1,0:T(8,128)S(1)}, f32[12,12]{1,0:T(8,128)}, u32[]{:S(2)}) copy-start(f32[12,12]{1,0:T(8,128)} %from_modes.3) | copy-start | bytes 1732
  45.7 4.4 %copy-start.2 = (f32[12]{0:T(128)S(1)}, f32[12]{0:T(128)}, u32[]{:S(2)}) copy-start(f32[12]{0:T(128)} %depth.3) | copy-start | bytes 148
  45.7 4.4 %copy-start.3 = (f32[3,16,128]{2,1,0:T(8,128)S(1)}, f32[3,16,128]{2,1,0:T(8,128)}, u32[]{:S(2)}) copy-start(f32[3,16,128]{2,1,0:T(8,128)} %constant.50.clone.refs_3_) | copy-start | bytes 73732
  45.7 4.4 %copy-start.4 = (f32[3,1024]{1,0:T(4,128)S(1)}, f32[3,1024]{1,0:T(4,128)}, u32[]{:S(2)}) copy-start(f32[3,1024]{1,0:T(4,128)} %constant.51.clone.refs_4_) | copy-start | bytes 36868
  45.7 4.4 %copy-start.5 = (f32[2,4,256]{2,1,0:T(4,128)S(1)}, f32[2,4,256]{2,1,0:T(4,128)}, u32[]{:S(2)}) copy-start(f32[2,4,256]{2,1,0:T(4,128)} %constant.49.clone.refs_2_) | copy-start | bytes 24580
  73.6 31.6 %all-to-all-start.3 = ((f32[2208,1,128]{2,1,0:T(1,128)}), f32[2208,1,128]{2,1,0:T(1,128)S(1)}, u32[]{:S(2)}, u32[]{:S(2)}) async-start(f32[2208,1,128]{2,1,0:T(1,128)} %bitcast.15), calls=%async_computation.3 | async-start | bytes 2260992 | tf_op jit(solution)/shard_map/all_to_all | solution.py:693
  105.2 31.6 %all-to-all-start.1 = ((f32[2208,1,128]{2,1,0:T(1,128)}), f32[2208,1,128]{2,1,0:T(1,128)S(1)}, u32[]{:S(2)}, u32[]{:S(2)}) async-start(f32[2208,1,128]{2,1,0:T(1,128)} %bitcast.9), calls=%async_computation.1 | async-start | bytes 2260992 | tf_op jit(solution)/shard_map/all_to_all | solution.py:693
